TPU v7x, 32 devices: a whole 2x2x4 slice. The times are simulated.
32 devices in a mesh: wide: 4 (over x, core), narrow: 8 (over z, y).
Axes of the slice: x: 2, y: 2, z: 4, core: 2. Of those that a mesh axis runs over, the one named last changes fastest.
Arguments:
- tokens: bfloat16 [32768, 768], P(('wide', 'narrow')), may hold values from -60 to 60
- cotangent: bfloat16 [32768, 768], P(('wide', 'narrow')), may hold values from -8 to 8
- segment_ids: int32 [32768], P(('wide', 'narrow')), may hold values from 0 to 14, as said below
- pad_mask: int32 [32768], P(('wide', 'narrow')), may hold values from 0 to 1, as said below
- lengths: int32 [32], P(('wide', 'narrow')), may hold values from 706 to 966, as said below
- params: float32 [55424, 128], P(('wide', 'narrow')), may hold values from -10 to 10
Outputs:
- output: bfloat16 [32768, 768], P(('wide', 'narrow'))
- grad_input: float32 [32768, 768], P(('wide', 'narrow'))
- grad_params: float32 [55424, 128], P(('wide', 'narrow'))
Inputs may be any that keep to these rules, and one draw needn't show every extreme that they name: `segment_ids`: within each sequence of 1024 slots the numbers start at 0 and never fall. An image is one class token, 4 registers and h * w patches with h and w from 8 to 16; images are packed in order while they fit in 1024 - 1024 % (69) slots, and slots past the length carry the number after the last image. The first sequence holds only images of 8 x 8 patches. `pad_mask`: 1 exactly at the positions below its sequence's length. `lengths`: A sequence's length is the number of tokens of its images.
All inputs are finite; a program needn't handle non-finite values.
Results may differ from a plain program's by a relative error of at most 0.0097.
Values may be sent and summed in bfloat16 or wider, within the bound.
No kernel may reach another device: no remote copies, remote signals or barrier semaphores. Data moves between devices by JAX's collectives and lax.ppermute only.
A program may use at most 256 MiB of HBM per device.

v0:
```python
from functools import partial
import math

import jax
import jax.numpy as jnp
from jax import lax
from jax.sharding import PartitionSpec as P

FF = 3072
HEADS = 12
BLOCK = 512
HGROUP = 4


EPSILON = 1e-06
NEGATIVE = -1e30


def layer_norm(values, norm_gain, norm_shift):
    center = values - jnp.mean(values, axis=-1, keepdims=True)
    spread = jnp.mean(center * center, axis=-1, keepdims=True)
    return center * lax.rsqrt(spread + EPSILON) * norm_gain + norm_shift


def split_vector(vector, amounts):
    pieces = []
    offset = 0
    for amount in amounts:
        pieces.append(vector[offset : offset + amount])
        offset = offset + amount
    return pieces


def attention_amounts(model_width):
    return [
        model_width,
        model_width,
        3 * model_width * model_width,
        model_width,
        model_width,
        model_width * model_width,
        model_width,
        model_width,
    ]


def feedforward_amounts(model_width, hidden_units):
    return [
        model_width,
        model_width,
        model_width * hidden_units,
        hidden_units,
        hidden_units * model_width,
        model_width,
        model_width,
    ]


def unpack(gathered, amounts):
    return split_vector(gathered.reshape(-1)[: sum(amounts)], amounts)


def column_sums(values):
    return jnp.sum(values.astype(jnp.float32), axis=0)


def lay_out(pieces, devices, rows_each):
    flat_vector = jnp.concatenate([piece.reshape(-1) for piece in pieces])
    flat_vector = jnp.pad(flat_vector, (0, devices * rows_each * 128 - flat_vector.shape[0]))
    return flat_vector.reshape(devices, rows_each, 128)


def block_allowed(segment_row, valid_row, first_row):
    positions = jnp.arange(segment_row.shape[0], dtype=jnp.int32)
    query_segment = lax.dynamic_slice_in_dim(segment_row, first_row, BLOCK, 0)
    query_position = first_row + jnp.arange(BLOCK, dtype=jnp.int32)
    same_image = (query_segment[:, None] == segment_row[None, :]) & valid_row[None, :]
    return same_image | (query_position[:, None] == positions[None, :])


def block_scores(query_block, key_group, allowed, score_scale):
    scores = (
        jnp.einsum("qhe,khe->hqk", query_block, key_group, preferred_element_type=jnp.float32)
        * score_scale
    )
    return jnp.where(allowed[None], scores, NEGATIVE)


def attend_forward(pieces, score_scale):
    query_seq, key_seq, value_seq, segment_row, valid_row = pieces
    sequence_length = query_seq.shape[0]
    head_groups = query_seq.shape[1]

    def one_group(group_number):
        query_group = lax.dynamic_index_in_dim(query_seq, group_number, 1, keepdims=False)
        key_group = lax.dynamic_index_in_dim(key_seq, group_number, 1, keepdims=False)
        value_group = lax.dynamic_index_in_dim(value_seq, group_number, 1, keepdims=False)

        def one_block(block_number):
            first_row = block_number * BLOCK
            query_block = lax.dynamic_slice_in_dim(query_group, first_row, BLOCK, 0)
            scores = block_scores(
                query_block,
                key_group,
                block_allowed(segment_row, valid_row, first_row),
                score_scale,
            )
            highest = jnp.max(scores, axis=-1, keepdims=True)
            raised = jnp.exp(scores - highest)
            summed = jnp.sum(raised, axis=-1, keepdims=True)
            weights = (raised / summed).astype(jnp.bfloat16)
            mixed_heads = jnp.einsum(
                "hqk,khe->qhe", weights, value_group, preferred_element_type=jnp.float32
            )
            return (mixed_heads.astype(jnp.bfloat16), highest, summed)

        return lax.map(one_block, jnp.arange(sequence_length // BLOCK, dtype=jnp.int32))

    mixed_heads, highest, summed = lax.map(one_group, jnp.arange(head_groups, dtype=jnp.int32))
    mixed_heads = jnp.transpose(mixed_heads, (1, 2, 0, 3, 4)).reshape(sequence_length, -1)
    return (mixed_heads, highest, summed)


def attend_backward(pieces, score_scale):
    query_seq, key_seq, value_seq, segment_row, valid_row, grad_seq, highest, summed = pieces
    sequence_length = query_seq.shape[0]
    head_groups = query_seq.shape[1]

    def one_group(group_number):
        query_group = lax.dynamic_index_in_dim(query_seq, group_number, 1, keepdims=False)
        key_group = lax.dynamic_index_in_dim(key_seq, group_number, 1, keepdims=False)
        value_group = lax.dynamic_index_in_dim(value_seq, group_number, 1, keepdims=False)
        grad_group = lax.dynamic_index_in_dim(grad_seq, group_number, 1, keepdims=False)
        high_group = lax.dynamic_index_in_dim(highest, group_number, 0, keepdims=False)
        sum_group = lax.dynamic_index_in_dim(summed, group_number, 0, keepdims=False)

        def one_block(carry, block_number):
            grad_keys, grad_values = carry
            first_row = block_number * BLOCK
            query_block = lax.dynamic_slice_in_dim(query_group, first_row, BLOCK, 0)
            grad_block = lax.dynamic_slice_in_dim(grad_group, first_row, BLOCK, 0)
            scores = block_scores(
                query_block,
                key_group,
                block_allowed(segment_row, valid_row, first_row),
                score_scale,
            )
            softmax_probs = jnp.exp(scores - high_group[block_number]) / sum_group[block_number]
            weights = softmax_probs.astype(jnp.bfloat16)
            grad_values = grad_values + jnp.einsum(
                "hqk,qhe->khe", weights, grad_block, preferred_element_type=jnp.float32
            )
            grad_probs = jnp.einsum(
                "qhe,khe->hqk", grad_block, value_group, preferred_element_type=jnp.float32
            )
            inner_sum = jnp.sum(softmax_probs * grad_probs, axis=-1, keepdims=True)
            grad_scores = (softmax_probs * (grad_probs - inner_sum)).astype(jnp.bfloat16)
            grad_query = (
                jnp.einsum(
                    "hqk,khe->qhe", grad_scores, key_group, preferred_element_type=jnp.float32
                )
                * score_scale
            )
            grad_keys = (
                grad_keys
                + jnp.einsum(
                    "hqk,qhe->khe", grad_scores, query_block, preferred_element_type=jnp.float32
                )
                * score_scale
            )
            return ((grad_keys, grad_values), grad_query)

        zero_rows = jnp.zeros(key_group.shape, jnp.float32)
        carried, grad_queries = lax.scan(
            one_block, (zero_rows, zero_rows), jnp.arange(sequence_length // BLOCK, dtype=jnp.int32)
        )
        return (grad_queries, carried[0], carried[1])

    grad_queries, grad_keys, grad_values = lax.map(
        one_group, jnp.arange(head_groups, dtype=jnp.int32)
    )
    grad_queries = jnp.transpose(grad_queries, (1, 2, 0, 3, 4)).reshape(sequence_length, -1)
    grad_keys = jnp.transpose(grad_keys, (1, 0, 2, 3)).reshape(sequence_length, -1)
    grad_values = jnp.transpose(grad_values, (1, 0, 2, 3)).reshape(sequence_length, -1)
    return jnp.concatenate([grad_queries, grad_keys, grad_values], axis=1)


def local(tokens, cotangent, segment_ids, pad_mask, lengths, params):
    row_count, model_width = tokens.shape
    sequence_count = lengths.shape[0]
    sequence_length = row_count // sequence_count
    hidden_units = FF
    head_dim = model_width // HEADS
    head_groups = HEADS // HGROUP
    score_scale = head_dim ** (-0.5)
    devices = lax.axis_size("wide") * lax.axis_size("narrow")
    att_count = 4 * model_width * model_width + 6 * model_width
    att_rows = (att_count // 128 + devices - 1) // devices
    mlp_rows = params.shape[0] - att_rows
    attention_list = attention_amounts(model_width)
    feedforward_list = feedforward_amounts(model_width, hidden_units)
    attention_gathered = lax.all_gather(
        params[:att_rows].astype(jnp.bfloat16), ("wide", "narrow"), axis=0, tiled=True
    )
    (
        first_gain,
        first_shift,
        triple_weight,
        query_bias,
        value_bias,
        output_weight,
        output_bias,
        first_scale,
    ) = unpack(attention_gathered, attention_list)
    inputs = tokens.astype(jnp.float32)
    gain_one = first_gain.astype(jnp.float32)
    shift_one = first_shift.astype(jnp.float32)
    normed_one = layer_norm(inputs, gain_one, shift_one).astype(jnp.bfloat16)
    bias_row = jnp.concatenate([query_bias, jnp.zeros_like(query_bias), value_bias]).astype(
        jnp.float32
    )
    triple = jnp.dot(
        normed_one,
        triple_weight.reshape(model_width, 3 * model_width),
        preferred_element_type=jnp.float32,
    )
    triple = (triple + bias_row).astype(jnp.bfloat16)
    shaped = triple.reshape(sequence_count, sequence_length, 3, head_groups, HGROUP, head_dim)
    query_rows = shaped[:, :, 0]
    key_rows = shaped[:, :, 1]
    value_rows = shaped[:, :, 2]
    positions = jnp.arange(sequence_length, dtype=jnp.int32)
    segment_rows = segment_ids.reshape(sequence_count, sequence_length)
    valid_rows = (pad_mask.reshape(sequence_count, sequence_length) > 0) & (
        positions[None, :] < lengths[:, None]
    )
    mixed_heads, highest, summed = lax.map(
        partial(attend_forward, score_scale=score_scale),
        (query_rows, key_rows, value_rows, segment_rows, valid_rows),
    )
    mixed_rows = mixed_heads.reshape(row_count, model_width)
    branch_one = jnp.dot(
        mixed_rows,
        output_weight.reshape(model_width, model_width),
        preferred_element_type=jnp.float32,
    )
    branch_one = branch_one + output_bias.astype(jnp.float32)
    scale_one = first_scale.astype(jnp.float32)
    middle = inputs + scale_one * branch_one
    feedforward_gathered = lax.all_gather(
        params[att_rows:].astype(jnp.bfloat16), ("wide", "narrow"), axis=0, tiled=True
    )
    (
        second_gain,
        second_shift,
        expand_weight,
        expand_bias,
        contract_weight,
        contract_bias,
        second_scale,
    ) = unpack(feedforward_gathered, feedforward_list)
    gain_two = second_gain.astype(jnp.float32)
    shift_two = second_shift.astype(jnp.float32)
    normed_two = layer_norm(middle, gain_two, shift_two).astype(jnp.bfloat16)
    expanded = jnp.dot(
        normed_two,
        expand_weight.reshape(model_width, hidden_units),
        preferred_element_type=jnp.float32,
    )
    expanded = expanded + expand_bias.astype(jnp.float32)
    activated = jax.nn.gelu(expanded, approximate=False).astype(jnp.bfloat16)
    contracted = jnp.dot(
        activated,
        contract_weight.reshape(hidden_units, model_width),
        preferred_element_type=jnp.float32,
    )
    contracted = contracted + contract_bias.astype(jnp.float32)
    scale_two = second_scale.astype(jnp.float32)
    output = (middle + scale_two * contracted).astype(jnp.bfloat16)
    feedforward_gathered = lax.all_gather(
        params[att_rows:].astype(jnp.bfloat16), ("wide", "narrow"), axis=0, tiled=True
    )
    (
        second_gain,
        second_shift,
        expand_weight,
        expand_bias,
        contract_weight,
        contract_bias,
        second_scale,
    ) = unpack(feedforward_gathered, feedforward_list)
    gain_two = second_gain.astype(jnp.float32)
    shift_two = second_shift.astype(jnp.float32)
    scale_two = second_scale.astype(jnp.float32)
    expand_matrix = expand_weight.reshape(model_width, hidden_units)
    contract_matrix = contract_weight.reshape(hidden_units, model_width)
    upstream = cotangent.astype(jnp.float32)
    grad_second_scale = jnp.sum(upstream * contracted, axis=0)
    grad_contracted = (upstream * scale_two).astype(jnp.bfloat16)
    grad_contract_bias = column_sums(grad_contracted)
    grad_contract_weight = jnp.einsum(
        "rf,rd->fd", activated, grad_contracted, preferred_element_type=jnp.float32
    )
    grad_activated = jnp.einsum(
        "rd,fd->rf", grad_contracted, contract_matrix, preferred_element_type=jnp.float32
    )
    gelu_values, gelu_pull = jax.vjp(partial(jax.nn.gelu, approximate=False), expanded)
    grad_expanded = gelu_pull(grad_activated)[0].astype(jnp.bfloat16)
    grad_expand_bias = column_sums(grad_expanded)
    grad_expand_weight = jnp.einsum(
        "rd,rf->df", normed_two, grad_expanded, preferred_element_type=jnp.float32
    )
    grad_normed_two = jnp.einsum(
        "rf,df->rd", grad_expanded, expand_matrix, preferred_element_type=jnp.float32
    )
    normed_again, norm_pull = jax.vjp(layer_norm, middle, gain_two, shift_two)
    grad_middle_norm, grad_second_gain, grad_second_shift = norm_pull(grad_normed_two)
    grad_middle = upstream + grad_middle_norm
    feedforward_term = lay_out(
        [
            grad_second_gain,
            grad_second_shift,
            grad_expand_weight,
            grad_expand_bias,
            grad_contract_weight,
            grad_contract_bias,
            grad_second_scale,
        ],
        devices,
        mlp_rows,
    )
    attention_gathered = lax.all_gather(
        params[:att_rows].astype(jnp.bfloat16), ("wide", "narrow"), axis=0, tiled=True
    )
    (
        first_gain,
        first_shift,
        triple_weight,
        query_bias,
        value_bias,
        output_weight,
        output_bias,
        first_scale,
    ) = unpack(attention_gathered, attention_list)
    gain_one = first_gain.astype(jnp.float32)
    shift_one = first_shift.astype(jnp.float32)
    scale_one = first_scale.astype(jnp.float32)
    triple_matrix = triple_weight.reshape(model_width, 3 * model_width)
    output_matrix = output_weight.reshape(model_width, model_width)
    grad_first_scale = jnp.sum(grad_middle * branch_one, axis=0)
    grad_branch = (grad_middle * scale_one).astype(jnp.bfloat16)
    grad_output_bias = column_sums(grad_branch)
    grad_output_weight = jnp.einsum(
        "rd,re->de", mixed_rows, grad_branch, preferred_element_type=jnp.float32
    )
    grad_mixed = jnp.einsum(
        "re,de->rd", grad_branch, output_matrix, preferred_element_type=jnp.float32
    ).astype(jnp.bfloat16)
    grad_mixed = grad_mixed.reshape(sequence_count, sequence_length, head_groups, HGROUP, head_dim)
    grad_triple = lax.map(
        partial(attend_backward, score_scale=score_scale),
        (query_rows, key_rows, value_rows, segment_rows, valid_rows, grad_mixed, highest, summed),
    )
    grad_triple = grad_triple.reshape(row_count, 3 * model_width).astype(jnp.bfloat16)
    grad_query_bias = column_sums(grad_triple[:, :model_width])
    grad_value_bias = column_sums(grad_triple[:, 2 * model_width :])
    grad_triple_weight = jnp.einsum(
        "rd,re->de", normed_one, grad_triple, preferred_element_type=jnp.float32
    )
    grad_normed_one = jnp.einsum(
        "re,de->rd", grad_triple, triple_matrix, preferred_element_type=jnp.float32
    )
    first_again, first_pull = jax.vjp(layer_norm, inputs, gain_one, shift_one)
    grad_input_norm, grad_first_gain, grad_first_shift = first_pull(grad_normed_one)
    grad_input = grad_middle + grad_input_norm
    attention_term = lay_out(
        [
            grad_first_gain,
            grad_first_shift,
            grad_triple_weight,
            grad_query_bias,
            grad_value_bias,
            grad_output_weight,
            grad_output_bias,
            grad_first_scale,
        ],
        devices,
        att_rows,
    )
    whole_term = jnp.concatenate([attention_term, feedforward_term], axis=1).reshape(-1, 128)
    owned = lax.psum_scatter(whole_term, ("wide", "narrow"), scatter_dimension=0, tiled=True)
    grad_params = owned * (1.0 / math.sqrt(row_count * devices))
    return (output, grad_input, grad_params)


def solution(mesh):
    return jax.shard_map(
        local,
        mesh=mesh,
        in_specs=(
            P(("wide", "narrow"), None),
            P(("wide", "narrow"), None),
            P(("wide", "narrow")),
            P(("wide", "narrow")),
            P(("wide", "narrow")),
            P(("wide", "narrow"), None),
        ),
        out_specs=(
            P(("wide", "narrow"), None),
            P(("wide", "narrow"), None),
            P(("wide", "narrow"), None),
        ),
        check_vma=False,
    )
```

profile of v0, /device:TPU:10, one launch (start us, length us, event | category | flops | bytes accessed | tf_op | source)
XLA Modules:
  0.0 1594.2 jit_solution(740318001230358281)
XLA Ops:
  15.1 61.6 %all-gather.5.cloned.1.call-done = bf16[32,578,128]{2,1,0:T(8,128)(2,1)} async-done(((bf16[1,578,128]{2,1,0:T(8,128)(2,1)}), bf16[32,578,128]{2,1,0:T(8,128)(2,1)}) %all-gather.5.cloned.1.call-update) | async-done | bytes 4734992 | tf_op jit(solution)/shard_map/all_gather | solution.py:202
  76.6 7.3 reshape.430
  85.3 3.9 slice.134
  89.2 7.6 reshape.404
  96.8 7.8 add_convert_fusion.1
  104.7 6.8 copy.34
  111.5 4.8 slice_bitcast_fusion
  116.3 81.5 %while.78 = (s32[]{:T(128)}, bf16[3,2,512,4,64]{2,4,3,1,0:T(8,128)(2,1)}, f32[3,2,4,512,1]{3,2,1,4,0:T(4,128)}, f32[3,2,4,512,1]{3,2,1,4,0:T(4,128)}, s32[3]{0:T...) while((s32[]{:T(128)}, ...), condition=%wide.region_7.8_spmd, body=%wide.region_2.7_spmd.sunk | while | flops 564261376 | bytes 37379716 | solution.py:119
  120.8 19.6 %while.81 = (s32[]{:T(128)}, bf16[2,512,4,64]{1,3,2,0:T(8,128)(2,1)}, f32[2,4,512,1]{2,1,3,0:T(4,128)S(1)}, f32[2,4,512,1]{2,1,3,0:T(4,128)S(1)}, s32[2]{0:T(128...) while((s32[]{:T(128)}, ...), condition=%wide.region_6.6_spmd, body=%wide.region_3.5_spmd.sunk | while | flops 564261376 | bytes 33119508 | solution.py:117
  147.9 19.6 %while.81 = (s32[]{:T(128)}, bf16[2,512,4,64]{1,3,2,0:T(8,128)(2,1)}, f32[2,4,512,1]{2,1,3,0:T(4,128)S(1)}, f32[2,4,512,1]{2,1,3,0:T(4,128)S(1)}, s32[2]{0:T(128...) while((s32[]{:T(128)}, ...), condition=%wide.region_6.6_spmd, body=%wide.region_3.5_spmd.sunk | while | flops 564261376 | bytes 33119508 | solution.py:117
  175.0 19.6 %while.81 = (s32[]{:T(128)}, bf16[2,512,4,64]{1,3,2,0:T(8,128)(2,1)}, f32[2,4,512,1]{2,1,3,0:T(4,128)S(1)}, f32[2,4,512,1]{2,1,3,0:T(4,128)S(1)}, s32[2]{0:T(128...) while((s32[]{:T(128)}, ...), condition=%wide.region_6.6_spmd, body=%wide.region_3.5_spmd.sunk | while | flops 564261376 | bytes 33119508 | solution.py:117
  205.6 5.2 fusion.79
  212.9 10.4 reshape.432
  224.0 9.4 fusion.80
  234.2 8.2 reshape.408
  242.5 9.4 reshape.409
  251.9 38.0 %multiply_convert_fusion.1 = (bf16[1024,3072]{1,0:T(8,128)(2,1)}, f32[1024,3072]{1,0:T(8,128)}, f32[1024,3072]{1,0:T(8,128)}) fusion(f32[3072]{0:T(1024)S(1)} %fusion.57, bf16[768,3072]{1,0:T(8,128)(2,1)} %reshape.408, f32[1024,768]{0,1:T(8,128)S(1)} %copy-done.10, f32[768]{0:T(1024)S(1)} %get-tuple-element.484, f32[768]{0:T(1024)S(1)} %get-tuple-element.485, ...), kind=kOutput, calls=%fused_computation.66 | convolution fusion | flops 5043388416 | bytes 39348224 | tf_op jit(solution)/shard_map/dot_general | solution.py:265
  289.9 18.1 %convert_reduce_fusion = (f32[3072]{0:T(1024)}, bf16[1024,3072]{1,0:T(8,128)(2,1)}) fusion(f32[1024,3072]{1,0:T(8,128)} %get-tuple-element.467, bf16[3072,768]{1,0:T(8,128)(2,1)} %reshape.409, bf16[1024,768]{0,1:T(8,128)(2,1)S(1)} %copy-done.21, f32[768]{0:T(1024)S(1)} %get-tuple-element.482, f32[1024,3072]{1,0:T(8,128)} %get-tuple-element.501, ...), kind=kOutput, calls=%fused_computation.64 | convolution fusion | flops 4887671808 | bytes 37776384 | tf_op jit(solution)/shard_map/rd,fd->rf/dot_general | solution.py:304
  308.0 10.3 fusion.81
  318.4 3.5 copy.38
  321.9 3.5 multiply_reduce_fusion.1
  326.8 13.2 multiply_reduce_fusion.2
  342.6 211.8 %while.80 = (s32[]{:T(128)}, bf16[3,2,512,4,64]{2,4,3,1,0:T(8,128)(2,1)}, bf16[3,1024,4,64]{1,3,2,0:T(8,128)(2,1)}, bf16[3,1024,4,64]{1,3,2,0:T(8,128)(2,1)}, s3...) while((s32[]{:T(128)}, ...), condition=%wide.region_16.17_spmd, body=%wide.region_12.16_spmd.sunk | while | flops 1366686208 | bytes 196231136 | solution.py:179
  352.6 57.5 %while.82 = (s32[]{:T(128)}, f32[1024,4,64]{0,2,1:T(8,128)S(1)}, f32[1024,4,64]{0,2,1:T(8,128)S(1)}, bf16[2,512,4,64]{1,3,2,0:T(8,128)(2,1)}, s32[2]{0:T(128)S(1...) while((s32[]{:T(128)}, f32[1024,4,64]{0,2,1:T(8,128)S(1)}, ...), condition=%wide.region_15.15_spmd.clone, body=%wide.region_13.14_spmd.clone.sunk | while | flops 1366686208 | bytes 186727968 | solution.py:174
  353.9 4.5 fusion.136
  361.1 6.4 multiply_reduce_fusion.6
  372.0 3.4 fusion.138
  382.6 4.5 fusion.136
  389.8 6.4 multiply_reduce_fusion.6
  400.7 3.4 fusion.138
  423.0 57.5 %while.82 = (s32[]{:T(128)}, f32[1024,4,64]{0,2,1:T(8,128)S(1)}, f32[1024,4,64]{0,2,1:T(8,128)S(1)}, bf16[2,512,4,64]{1,3,2,0:T(8,128)(2,1)}, s32[2]{0:T(128)S(1...) while((s32[]{:T(128)}, f32[1024,4,64]{0,2,1:T(8,128)S(1)}, ...), condition=%wide.region_15.15_spmd.clone, body=%wide.region_13.14_spmd.clone.sunk | while | flops 1366686208 | bytes 186727968 | solution.py:174
  424.3 4.5 fusion.136
  431.5 6.4 multiply_reduce_fusion.6
  442.4 3.4 fusion.138
  453.1 4.5 fusion.136
  460.3 6.4 multiply_reduce_fusion.6
  471.2 3.4 fusion.138
  493.5 57.5 %while.82 = (s32[]{:T(128)}, f32[1024,4,64]{0,2,1:T(8,128)S(1)}, f32[1024,4,64]{0,2,1:T(8,128)S(1)}, bf16[2,512,4,64]{1,3,2,0:T(8,128)(2,1)}, s32[2]{0:T(128)S(1...) while((s32[]{:T(128)}, f32[1024,4,64]{0,2,1:T(8,128)S(1)}, ...), condition=%wide.region_15.15_spmd.clone, body=%wide.region_13.14_spmd.clone.sunk | while | flops 1366686208 | bytes 186727968 | solution.py:174
  494.8 4.5 fusion.136
  502.0 6.4 multiply_reduce_fusion.6
  512.9 3.4 fusion.138
  523.5 4.5 fusion.136
  530.7 6.4 multiply_reduce_fusion.6
  541.6 3.4 fusion.138
  558.2 7.1 fusion.82
  565.3 7.0 fusion.54
  575.9 7.9 convolution_bitcast_fusion
  583.8 7.8 fusion.71
  591.6 3.5 copy.40
  599.3 7.9 reshape.413
  610.5 9.5 copy.48
  620.0 10.8 reshape.417
  633.3 60.8 %dynamic-update-slice.9 = f32[2363904]{0:T(1024)} dynamic-update-slice(f32[2363904]{0:T(1024)} %constant_dynamic-update-slice_fusion, f32[1769472]{0:T(1024)} %reshape.413, s32[]{} %constant.240) | dynamic-update-slice | bytes 14155780
  703.8 80.6 %dynamic-update-slice.2 = f32[4724736]{0:T(1024)} dynamic-update-slice(f32[4724736]{0:T(1024)} %constant_dynamic-update-slice_fusion.1, f32[2359296]{0:T(1024)} %bitcast.234, s32[]{} %constant.240) | dynamic-update-slice | bytes 18874372
  785.7 80.0 %dynamic-update-slice.4 = f32[4724736]{0:T(1024)} dynamic-update-slice(f32[4724736]{0:T(1024)} %constant_dynamic-update-slice_fusion.11, f32[2359296]{0:T(1024)} %reshape.417, s32[]{} %constant.242) | dynamic-update-slice | bytes 18874372
  868.4 14.5 pad.9
  882.9 15.0 reshape.418
  898.0 8.7 pad.8
  906.7 9.6 reshape.415
  916.2 20.0 %pad_maximum_fusion = f32[32,1732,128]{2,1,0:T(8,128)} fusion(f32[32,1154,128]{2,1,0:T(8,128)} %reshape.418, f32[32,578,128]{2,1,0:T(8,128)} %reshape.415), kind=kLoop, calls=%fused_computation.61 | loop fusion | flops 7094272 | bytes 56754176 | tf_op jit(solution)/shard_map/concatenate | solution.py:390
  936.2 24.1 %reshape.419 = f32[55424,128]{1,0:T(8,128)} reshape(f32[32,1732,128]{2,1,0:T(8,128)} %pad_maximum_fusion) | data formatting | bytes 56754176 | tf_op jit(solution)/shard_map/reshape | solution.py:390
  960.3 607.0 %fusion = f32[1744,128]{1,0:T(8,128)} fusion(f32[55424,128]{1,0:T(8,128)} %reshape.419), kind=kCustom, calls=%all-reduce-scatter | all-reduce-scatter fusion | flops 7143425 | bytes 29270016
  1568.2 4.4 collective-permute-start
  1572.7 5.9 add_add_fusion.2
  (490 shorter events, 240.4 us)
Async XLA Ops:
  7.2 6.2 copy-start.27
  7.2 69.5 %all-gather.5.cloned.1.call-start = ((), (), s32[]{:S(2)}) async-start(), calls=%async_computation | async-start | bytes 4933632 | tf_op jit(solution)/shard_map/all_gather | solution.py:202
  9.2 203.6 %all-gather.7.cloned.1.call-start = ((), (), s32[]{:S(2)}) async-start(), calls=%async_computation.1 | async-start | bytes 9799680 | tf_op jit(solution)/shard_map/all_gather | solution.py:250
  10.2 4.8 copy-start.49
  11.9 84.8 %copy-start.4 = (bf16[1024,768]{0,1:T(8,128)(2,1)}, bf16[1024,768]{0,1:T(8,128)(2,1)S(1)}, u32[]{:S(2)}) copy-start(bf16[1024,768]{0,1:T(8,128)(2,1)S(1)} %copy.33) | copy-start | bytes 4718596
  12.2 84.6 %copy-start.31 = (f32[1024]{0:T(1024)}, f32[1024]{0:T(1024)S(1)}, u32[]{:S(2)}) copy-start(f32[1024]{0:T(1024)S(1)} %broadcast_multiply_fusion.1) | copy-start | bytes 12292
  12.7 63.9 %copy-start.39 = (f32[1024]{0:T(1024)}, f32[1024]{0:T(1024)S(1)}, u32[]{:S(2)}) copy-start(f32[1024]{0:T(1024)S(1)} %fusion.50) | copy-start | bytes 12292
  12.7 84.1 %copy-start.37 = (f32[1024]{0:T(1024)}, f32[1024]{0:T(1024)S(1)}, u32[]{:S(2)}) copy-start(f32[1024]{0:T(1024)S(1)} %fusion.59) | copy-start | bytes 12292
  85.3 11.5 copy-start.35
  85.3 11.5 copy-start.59
  111.5 4.8 copy-start.13
  197.9 7.7 copy-start.25
  199.0 4.8 slice-start.2
  199.0 6.6 copy-start.5
  199.0 6.6 copy-start.61
  199.0 6.6 copy-start.63
  210.8 114.6 %copy-start.33 = (f32[1024]{0:T(1024)}, f32[1024]{0:T(1024)S(1)}, u32[]{:S(2)}) copy-start(f32[1024]{0:T(1024)S(1)} %broadcast_multiply_fusion) | copy-start | bytes 12292
  212.9 112.5 %copy-start.41 = (f32[1024]{0:T(1024)}, f32[1024]{0:T(1024)S(1)}, u32[]{:S(2)}) copy-start(f32[1024]{0:T(1024)S(1)} %fusion.60) | copy-start | bytes 12292
  234.2 17.7 %copy-start.57 = (f32[768]{0:T(1024)}, f32[768]{0:T(1024)S(1)}, u32[]{:S(2)}) copy-start(f32[768]{0:T(1024)S(1)} %get-tuple-element.484) | copy-start | bytes 9220
  234.2 91.2 %copy-start.43 = (f32[768]{0:T(1024)}, f32[768]{0:T(1024)S(1)}, u32[]{:S(2)}) copy-start(f32[768]{0:T(1024)S(1)} %get-tuple-element.485) | copy-start | bytes 9220
  234.2 92.1 %copy-start.55 = (f32[768]{0:T(1024)}, f32[768]{0:T(1024)S(1)}, u32[]{:S(2)}) copy-start(f32[768]{0:T(1024)S(1)} %get-tuple-element.482) | copy-start | bytes 9220
  242.5 9.4 copy-start.10
  251.9 38.0 %copy-start.21 = (bf16[1024,768]{0,1:T(8,128)(2,1)S(1)}, bf16[1024,768]{0,1:T(8,128)(2,1)}, u32[]{:S(2)}) copy-start(bf16[1024,768]{0,1:T(8,128)(2,1)} %copy.37) | copy-start | bytes 4718596
  326.3 13.7 copy-start.20
  326.4 13.7 copy-start.45
  326.8 13.2 copy-start.30
  360.4 7.1 slice-start
  361.0 6.4 slice-start.1
  372.0 4.7 copy-start.2
  389.2 7.1 slice-start
  389.8 6.4 slice-start.1
  400.7 4.7 copy-start.2
  430.9 7.1 slice-start
  431.5 6.4 slice-start.1
  459.6 7.1 slice-start
  460.3 6.4 slice-start.1
  501.3 7.1 slice-start
  502.0 6.4 slice-start.1
  530.1 7.1 slice-start
  530.7 6.4 slice-start.1
  558.1 7.2 copy-start.6
  558.1 7.2 copy-start.32
  558.1 7.2 copy-start.36
  558.1 7.2 copy-start.38
  558.1 7.2 copy-start.60
  558.1 7.2 copy-start.65
  558.2 17.7 %slice-start.3 = ((s8[6291456]{0:T(1024)(128)(4,1)}), s8[4194304]{0:T(1024)(128)(4,1)S(1)}, s32[]{:S(2)}) async-start(s8[6291456]{0:T(1024)(128)(4,1)} %bitcast.250), calls=%async_computation.5 | async-start | bytes 8388608
  565.3 7.6 copy-start.29
  565.3 7.6 copy-start.67
  565.3 10.5 slice-start.4
  572.9 10.9 slice-start.5
  575.9 7.9 copy-start.23
  575.9 7.9 copy-start.56
  575.9 7.9 slice-start.6
  591.6 6.1 copy-start.40
  694.1 5.8 copy-start.52
  694.1 7.1 copy-start.47
  694.1 8.4 copy-start.50
  703.8 80.6 %copy-start.48 = (f32[3072]{0:T(1024)S(1)}, f32[3072]{0:T(1024)}, u32[]{:S(2)}) copy-start(f32[3072]{0:T(1024)} %get-tuple-element.504) | copy-start | bytes 36868
  785.7 80.1 %copy-start.51 = (f32[768]{0:T(1024)S(1)}, f32[768]{0:T(1024)}, u32[]{:S(2)}) copy-start(f32[768]{0:T(1024)} %get-tuple-element.368) | copy-start | bytes 9220
  785.7 81.4 %copy-start.53 = (f32[768]{0:T(1024)S(1)}, f32[768]{0:T(1024)}, u32[]{:S(2)}) copy-start(f32[768]{0:T(1024)} %get-tuple-element.367) | copy-start | bytes 9220
  785.7 81.4 %copy-start.54 = (f32[768]{0:T(1024)S(1)}, f32[768]{0:T(1024)}, u32[]{:S(2)}) copy-start(f32[768]{0:T(1024)} %get-tuple-element.369) | copy-start | bytes 9220
  960.3 612.3 %copy-start.46 = (f32[1024]{0:T(1024)S(1)}, f32[1024]{0:T(1024)}, u32[]{:S(2)}) copy-start(f32[1024]{0:T(1024)} %copy-done.45) | copy-start | bytes 12292
  1568.2 15.4 collective-permute-start
  (64 other events, 157.1 us)
Sparse Core Ops, SparseCore 0:
  11.4 65.1 all-gather.4
  79.5 80.7 all-gather.6
where the time goes:
time: 1620 us; the launch traced here: 1590 us
  blocking collectives  607 us (37%)
  local copies, waits for them, and re-layouts  539 us (33%)
  matrix products  257 us (16%)
  other arithmetic  79.2 us (5%)
  waiting for transfers between devices  61.6 us (4%)
  loops' own time  31 us (2%)
    unnamed x1, blocking collectives  607 us
    unnamed x154, local copies, waits for them, and re-layouts  283 us
    all_gather x1, waiting for transfers between devices, local(): lax.all_gather(params[:att_rows].astype(jnp.bfloat16), ('wide', 'narrow')...  61.6 us
    dot_general x12, matrix products, block_scores(): jnp.einsum('qhe,khe->hqk', query_block, key_group, preferred_element_type...  48.5 us
    dot_general x1, matrix products, local(): jnp.dot(normed_two, expand_weight.reshape(model_width, hidden_units), pre...  38 us
    while x120, local copies, waits for them, and re-layouts  36.8 us
  transfers between devices with their start and end apart: 3, of which 1 were waited for; matrix products, arithmetic and copies ran while one was open for 9% of the time, Pallas kernels for 0%

commit v1 on v0

v1 whole, which is shorter than its diff:
```python
import math
from functools import partial

import jax
import jax.numpy as jnp
from jax import lax
from jax.experimental import pallas as pl
from jax.experimental.pallas import tpu as pltpu
from jax.sharding import PartitionSpec as P

FF = 3072
HEADS = 12
EPSILON = 1e-06
NEGATIVE = -1e30
AXES = ("wide", "narrow")
LANES = 128
SUB = 16
QB = 128
MEGA = 1 << 20
F32 = jnp.float32
BF16 = jnp.bfloat16

BLOCKS = 32
QKV_BLOCKS, QKV_RT, QKV_CT = 24, 2, 18
WO_BLOCKS, WO_RT, WO_CT = 8, 6, 6
W1_BLOCKS, W1_RT, W1_CT = 16, 3, 24
W2_BLOCKS, W2_RT, W2_CT = 16, 12, 6
ATT_HALF, MLP_HALF = 18, 36
CHUNK = 768
CHUNKS = FF // CHUNK

G1, C1, BQ, BV, BO, S1 = 0, 6, 12, 18, 24, 30
G2, C2, B1, B2, S2 = 36, 42, 48, 72, 78
SMALL = 88

NT = (((1,), (1,)), ((), ()))
NN = (((1,), (0,)), ((), ()))
TN = (((0,), (0,)), ((), ()))


def mm(lhs, rhs, dims):
    return lax.dot_general(lhs, rhs, dims, preferred_element_type=F32)


def row_of(ref, first, count):
    return jnp.concatenate([ref[first + k : first + k + 1, :] for k in range(count)], axis=1)


def put_row(ref, first, values):
    for k in range(values.shape[1] // LANES):
        ref[first + k : first + k + 1, :] = values[:, k * LANES : (k + 1) * LANES]


def fold8(values):
    rows, columns = values.shape
    return jnp.sum(values.reshape(rows // 8, 8, columns), axis=0)


def total(values):
    return jnp.sum(values, axis=0, keepdims=True)


def vmem():
    return pl.BlockSpec(memory_space=pltpu.VMEM)


def smem():
    return pl.BlockSpec(memory_space=pltpu.SMEM)


def anywhere():
    return pl.BlockSpec(memory_space=pl.ANY)


def shape(dims, kind):
    return jax.ShapeDtypeStruct(dims, kind)


def cost(flops, moved, exps=0):
    return pl.CostEstimate(flops=int(flops), transcendentals=int(exps), bytes_accessed=int(moved))


def normalized(values):
    center = values - jnp.mean(values, axis=-1, keepdims=True)
    inverse = lax.rsqrt(jnp.mean(center * center, axis=-1, keepdims=True) + EPSILON)
    return center * inverse, inverse


def norm_pullback(unit, inverse, grad, gain):
    scaled = grad * gain
    first = jnp.mean(scaled, axis=-1, keepdims=True)
    second = jnp.mean(scaled * unit, axis=-1, keepdims=True)
    return inverse * (scaled - first - unit * second)


def gelu_pair(z):
    magnitude = jnp.abs(z)
    t = 1.0 / (1.0 + (0.3275911 * math.sqrt(0.5)) * magnitude)
    density = jnp.exp(z * z * -0.5)
    tail = 0.5 * 1.061405429
    tail = tail * t + 0.5 * -1.453152027
    tail = tail * t + 0.5 * 1.421413741
    tail = tail * t + 0.5 * -0.284496736
    tail = tail * t + 0.5 * 0.254829592
    tail = tail * t * density
    cumulative = jnp.where(z < 0, tail, 1.0 - tail)
    return z * cumulative, cumulative + z * density * (1.0 / math.sqrt(2.0 * math.pi))


def fetch(copies):
    for copy in copies:
        copy.start()


def settle(copies):
    for copy in copies:
        copy.wait()


ATT_BEFORE, ATT_AFTER = 64, 32
MLP_BEFORE, MLP_AFTER = 64, 40


def window_offsets(me, att_rows, mlp_rows):
    att = ATT_BEFORE + 12 + me * (576 - att_rows) + jnp.where(me < QKV_BLOCKS, 0, 12)
    mlp = MLP_BEFORE + 12 + me * (1152 - mlp_rows) + jnp.where(me < W1_BLOCKS, 0, 24)
    return att, mlp


def each_tile(me, act):
    @pl.when(me < QKV_BLOCKS)
    def _():
        for ct in range(QKV_CT):
            for rt in range(QKV_RT):
                act("att", ct // 9, (ct % 9) * QKV_RT + rt, rt * SUB * QKV_CT + ct, QKV_CT)

    @pl.when(me >= QKV_BLOCKS)
    def _():
        for rt in range(WO_RT):
            for ct in range(WO_CT):
                act("att", rt // 3, (rt % 3) * WO_CT + ct, rt * SUB * WO_CT + ct, WO_CT)

    @pl.when(me < W1_BLOCKS)
    def _():
        for ct in range(W1_CT):
            for rt in range(W1_RT):
                act("mlp", ct // 12, (ct % 12) * W1_RT + rt, rt * SUB * W1_CT + ct, W1_CT)

    @pl.when(me >= W1_BLOCKS)
    def _():
        for rt in range(W2_RT):
            for ct in range(W2_CT):
                act("mlp", rt // 6, (rt % 6) * W2_CT + ct, rt * SUB * W2_CT + ct, W2_CT)


def small_rows(me, act):
    @pl.when(me == 0)
    def _():
        act("att", True, 12, G1)
        act("mlp", True, 12, G2)

    @pl.when(me == QKV_BLOCKS - 1)
    def _():
        act("att", False, 12, BQ)

    @pl.when(me == W1_BLOCKS - 1)
    def _():
        act("mlp", False, 24, B1)

    @pl.when(me == BLOCKS - 1)
    def _():
        act("att", False, 12, BO)
        act("mlp", False, 12, B2)


def pack_kernel(att_rows, me_ref, own, tails, heads, att, mlp, small, win_a, win_m):
    me = me_ref[0]
    mlp_rows = own.shape[0] - att_rows
    win_a[0:ATT_BEFORE, :] = tails[0:ATT_BEFORE, :]
    win_a[ATT_BEFORE : ATT_BEFORE + att_rows, :] = own[0:att_rows, :]
    win_a[ATT_BEFORE + att_rows :, :] = heads[0:ATT_AFTER, :]
    win_m[0:MLP_BEFORE, :] = tails[ATT_BEFORE:, :]
    win_m[MLP_BEFORE : MLP_BEFORE + mlp_rows, :] = own[att_rows:, :]
    win_m[MLP_BEFORE + mlp_rows :, :] = heads[ATT_AFTER:, :]
    att_off, mlp_off = window_offsets(me, att_rows, mlp_rows)

    def tile(kind, half, index, first, stride):
        window, out, off = (win_a, att, att_off) if kind == "att" else (win_m, mlp, mlp_off)
        out[half, index] = window[pl.ds(off + first, SUB, stride=stride), :].astype(BF16)

    each_tile(me, tile)
    small[...] = jnp.zeros_like(small)

    def vector(kind, before, rows, first):
        window, off, size = (win_a, att_off, 576) if kind == "att" else (win_m, mlp_off, 1152)
        start = off - 12 if before else off + size
        rounded = window[pl.ds(start, rows), :].astype(BF16).astype(F32)
        small[first : first + rows, :] = rounded

    small_rows(me, vector)


def pack(me, own, tails, heads, att_rows):
    mlp_rows = own.shape[0] - att_rows
    return pl.pallas_call(
        partial(pack_kernel, att_rows),
        out_shape=(
            shape((2, ATT_HALF, SUB, LANES), BF16),
            shape((2, MLP_HALF, SUB, LANES), BF16),
            shape((SMALL, LANES), F32),
        ),
        in_specs=[smem(), vmem(), vmem(), vmem()],
        out_specs=(vmem(), vmem(), vmem()),
        scratch_shapes=[
            pltpu.VMEM((ATT_BEFORE + att_rows + ATT_AFTER, LANES), F32),
            pltpu.VMEM((MLP_BEFORE + mlp_rows + MLP_AFTER, LANES), F32),
        ],
        name="pack",
    )(me, own, tails, heads)


def spread_kernel(att_rows, mlp_rows, scale, me_ref, att_a, att_b, mlp_a, mlp_b, small, win_a, win_m):
    me = me_ref[0]
    att_off, mlp_off = window_offsets(me, att_rows, mlp_rows)
    win_a[...] = jnp.zeros_like(win_a)
    win_m[...] = jnp.zeros_like(win_m)

    def tile(kind, half, index, first, stride):
        window, off = (win_a, att_off) if kind == "att" else (win_m, mlp_off)
        source = {"att": (att_a, att_b), "mlp": (mlp_a, mlp_b)}[kind][half]
        window[pl.ds(off + first, SUB, stride=stride), :] = source[index] * scale

    each_tile(me, tile)

    def vector(kind, before, rows, first):
        window, off, size = (win_a, att_off, 576) if kind == "att" else (win_m, mlp_off, 1152)
        start = off - 12 if before else off + size
        window[pl.ds(start, rows), :] = small[first : first + rows, :] * scale

    small_rows(me, vector)


def spread(me, att_a, att_b, mlp_a, mlp_b, small, att_rows, mlp_rows, scale):
    return pl.pallas_call(
        partial(spread_kernel, att_rows, mlp_rows, scale),
        out_shape=(
            shape((ATT_BEFORE + att_rows + ATT_AFTER, LANES), F32),
            shape((MLP_BEFORE + mlp_rows + MLP_AFTER, LANES), F32),
        ),
        in_specs=[smem()] + [vmem()] * 5,
        out_specs=(vmem(), vmem()),
        name="spread",
    )(me, att_a, att_b, mlp_a, mlp_b, small)


def half_copies(me, first, count, halves, scratch, sems, base=0):
    copies = []
    for i in range(count):
        slot = jnp.bitwise_xor(me, first + i)
        for h, half in enumerate(halves):
            size = half.shape[1]
            copies.append(
                pltpu.make_async_copy(
                    half.at[slot], scratch.at[i, pl.ds(h * size, size)], sems.at[base + 2 * i + h]
                )
            )
    return copies


def qkv_column(w, ct):
    tiles = [w[d, ct * QKV_RT + rt] for d in range(QKV_BLOCKS) for rt in range(QKV_RT)]
    return jnp.concatenate(tiles, axis=0)


def wo_column(w, ct):
    tiles = [w[i, rt * WO_CT + ct] for i in range(WO_BLOCKS) for rt in range(WO_RT)]
    return jnp.concatenate(tiles, axis=0)


def norm_rows(rows, gain, shift, source, target, step=32):
    def one(i, carry):
        at = pl.ds(pl.multiple_of(i * step, step), step)
        unit, _ = normalized(source[at, :].astype(F32))
        target[at, :] = (unit * gain + shift).astype(BF16)
        return carry

    lax.fori_loop(0, rows // step, one, 0)


def qkv_kernel(me_ref, tokens, small, wa, wb, n1, qkv, w, sems):
    copies = half_copies(me_ref[0], 0, QKV_BLOCKS, (wa, wb), w, sems)
    fetch(copies)
    rows = tokens.shape[0]
    norm_rows(rows, row_of(small, G1, 6), row_of(small, C1, 6), tokens, n1)
    settle(copies)
    bias = jnp.concatenate(
        [row_of(small, BQ, 6), jnp.zeros((1, 768), F32), row_of(small, BV, 6)], axis=1
    )
    for c in range(QKV_CT // 2):
        weight = jnp.concatenate([qkv_column(w, 2 * c), qkv_column(w, 2 * c + 1)], axis=1)
        lanes = slice(256 * c, 256 * c + 256)
        qkv[:, lanes] = (mm(n1[...], weight, NN) + bias[:, lanes]).astype(BF16)


def project_qkv(me, tokens, small, att):
    rows, width = tokens.shape
    return pl.pallas_call(
        qkv_kernel,
        out_shape=(shape((rows, width), BF16), shape((rows, 3 * width), BF16)),
        in_specs=[smem(), vmem(), vmem(), anywhere(), anywhere()],
        out_specs=(vmem(), vmem()),
        scratch_shapes=[
            pltpu.VMEM((QKV_BLOCKS, 2 * ATT_HALF, SUB, LANES), BF16),
            pltpu.SemaphoreType.DMA((2 * QKV_BLOCKS,)),
        ],
        compiler_params=pltpu.CompilerParams(vmem_limit_bytes=40 * MEGA),
        cost_estimate=cost(6 * rows * width * width, 12 * rows * width),
        name="qkv_forward",
    )(me, tokens, small, att[0], att[1])


CLASSES = (128, 256, 384, 512, 768)


def head_masked(block):
    lane = lax.broadcasted_iota(jnp.int32, block.shape, 1)
    zero = jnp.zeros_like(block)
    return jnp.concatenate(
        [jnp.where(lane < 64, block, zero), jnp.where(lane >= 64, block, zero)], axis=0
    )


def pick_heads(both):
    return jnp.concatenate([both[0:64, 0:QB], both[64:128, QB : 2 * QB]], axis=0)


def lane_block(p, group):
    return pl.ds(pl.multiple_of((group * 6 + p) * LANES, LANES), LANES)


def mask_bias(start, width, b, key_ids, query_ids, bias):
    for j in range(width // QB):
        at = pl.ds(pl.multiple_of(start + j * QB, SUB), QB)
        same = key_ids[at, :] == query_ids[pl.ds(b, 1), :]
        bias[j * QB : (j + 1) * QB, :] = jnp.where(same, 0.0, NEGATIVE)


def attend_kernel(windows, qkv, key_ids, query_ids, mixed, stats, bias, scores):
    blocks = qkv.shape[0] // QB

    def one_block(b, carry):
        start = pl.multiple_of(windows[0, b], SUB)
        rows = pl.ds(pl.multiple_of(b * QB, QB), QB)
        for index, width in enumerate(CLASSES):

            @pl.when(windows[1, b] == index)
            def _(width=width):
                mask_bias(start, width, b, key_ids, query_ids, bias)
                pieces = [slice(j * QB, (j + 1) * QB) for j in range(width // QB)]

                def one_pair(p, inner):
                    queries = head_masked(qkv[rows, lane_block(p, 0)] * 0.125)
                    highest = jnp.full((8, 2 * QB), NEGATIVE, F32)
                    for piece in pieces:
                        at = pl.ds(pl.multiple_of(start + piece.start, SUB), QB)
                        part = mm(qkv[at, lane_block(p, 1)], queries, NT)
                        part = part + jnp.concatenate([bias[piece, :]] * 2, axis=1)
                        scores[piece, :] = part
                        highest = jnp.maximum(
                            highest, jnp.max(part.reshape(QB // 8, 8, 2 * QB), axis=0)
                        )
                    highest = jnp.max(highest, axis=0, keepdims=True)
                    summed = jnp.zeros((8, 2 * QB), F32)
                    both = jnp.zeros((LANES, 2 * QB), F32)
                    for piece in pieces:
                        at = pl.ds(pl.multiple_of(start + piece.start, SUB), QB)
                        raised = jnp.exp(scores[piece, :] - highest)
                        summed = summed + fold8(raised)
                        both = both + mm(qkv[at, lane_block(p, 2)], raised.astype(BF16), TN)
                    inverse = 1.0 / total(summed)
                    out = pick_heads(both * inverse)
                    mixed[rows, lane_block(p, 0)] = out.T.astype(BF16)
                    stats[b * 6 + p, 0:1, :] = highest
                    stats[b * 6 + p, 1:2, :] = inverse
                    return inner

                lax.fori_loop(0, 6, one_pair, 0, unroll=2)

        return carry

    lax.fori_loop(0, blocks, one_block, 0)


def attend(windows, qkv, key_ids, query_ids):
    rows = qkv.shape[0]
    width = qkv.shape[1] // 3
    return pl.pallas_call(
        attend_kernel,
        out_shape=(shape((rows, width), BF16), shape((rows // QB * 6, 2, 2 * QB), F32)),
        in_specs=[smem(), vmem(), vmem(), vmem()],
        out_specs=(vmem(), vmem()),
        scratch_shapes=[
            pltpu.VMEM((CLASSES[-1], QB), F32),
            pltpu.VMEM((CLASSES[-1], 2 * QB), F32),
        ],
        compiler_params=pltpu.CompilerParams(vmem_limit_bytes=40 * MEGA),
        cost_estimate=cost(2 * rows * rows * width, 8 * rows * width, 4 * rows * rows),
        name="attend_forward",
    )(windows, qkv, key_ids, query_ids)


def join_kernel(me_ref, tokens, mixed, small, wa, wb, x1, branch, n2, w, sems):
    copies = half_copies(me_ref[0], QKV_BLOCKS, WO_BLOCKS, (wa, wb), w, sems)
    fetch(copies)
    rows = tokens.shape[0]
    bias, scale = row_of(small, BO, 6), row_of(small, S1, 6)
    gain, shift = row_of(small, G2, 6), row_of(small, C2, 6)
    settle(copies)
    for c in range(3):
        weight = jnp.concatenate([wo_column(w, 2 * c), wo_column(w, 2 * c + 1)], axis=1)
        lanes = slice(256 * c, 256 * c + 256)
        branch[:, lanes] = mm(mixed[...], weight, NN) + bias[:, lanes]
    step = 32

    def one(i, carry):
        at = pl.ds(pl.multiple_of(i * step, step), step)
        values = tokens[at, :].astype(F32) + scale * branch[at, :]
        x1[at, :] = values
        unit, _ = normalized(values)
        n2[at, :] = (unit * gain + shift).astype(BF16)
        return carry

    lax.fori_loop(0, rows // step, one, 0)


def join(me, tokens, mixed, small, att):
    rows, width = tokens.shape
    return pl.pallas_call(
        join_kernel,
        out_shape=(
            shape((rows, width), F32),
            shape((rows, width), F32),
            shape((rows, width), BF16),
        ),
        in_specs=[smem(), vmem(), vmem(), vmem(), anywhere(), anywhere()],
        out_specs=(vmem(), vmem(), vmem()),
        scratch_shapes=[
            pltpu.VMEM((WO_BLOCKS, 2 * ATT_HALF, SUB, LANES), BF16),
            pltpu.SemaphoreType.DMA((2 * WO_BLOCKS,)),
        ],
        compiler_params=pltpu.CompilerParams(vmem_limit_bytes=40 * MEGA),
        cost_estimate=cost(2 * rows * width * width, 14 * rows * width),
        name="project_and_norm",
    )(me, tokens, mixed, small, att[0], att[1])


def w1_matrix(w1, f):
    columns = []
    for ct in range(6):
        tiles = [w1[f, d, ct * W1_RT + rt] for d in range(W1_BLOCKS) for rt in range(W1_RT)]
        columns.append(jnp.concatenate(tiles, axis=0))
    return jnp.concatenate(columns, axis=1)


def w2_matrix(w2, f):
    columns = []
    for ct in range(W2_CT):
        tiles = [w2[4 * f + k, rt * W2_CT + ct] for k in range(4) for rt in range(W2_RT)]
        columns.append(jnp.concatenate(tiles, axis=0))
    return jnp.concatenate(columns, axis=1)


def mlp_kernel(
    me_ref, n2, cot, x1, small, wa, wb,
    out, dx1, vectors, grads,
    w1, w2, macc, dnacc, dm, u, dz, gb1, sems1, sems2,
):
    me = me_ref[0]
    rows = n2.shape[0]
    slots1 = [jnp.bitwise_xor(me, d) for d in range(W1_BLOCKS)]

    def into_w1(f):
        half = (wa, wb)[f // 2]
        part = pl.ds(MLP_HALF // 2 * (f % 2), MLP_HALF // 2)
        return [
            pltpu.make_async_copy(half.at[slots1[d], part], w1.at[f, d], sems1.at[f, d])
            for d in range(W1_BLOCKS)
        ]

    def into_w2(f):
        return [
            pltpu.make_async_copy(
                (wa, wb)[h].at[jnp.bitwise_xor(me, W1_BLOCKS + 4 * f + k)],
                w2.at[4 * f + k, pl.ds(h * MLP_HALF, MLP_HALF)],
                sems2.at[f, 2 * k + h],
            )
            for k in range(4)
            for h in range(2)
        ]

    arriving = [into_w1(f) + into_w2(f) for f in range(CHUNKS)]
    for f in range(CHUNKS):
        fetch(arriving[f])

    def out_copies(f):
        copies = []
        for d in range(W1_BLOCKS):
            part = pl.ds(MLP_HALF // 2 * (f % 2), MLP_HALF // 2)
            target = grads.at[f // 2, slots1[d], part]
            copies.append(pltpu.make_async_copy(w1.at[f, d], target, sems1.at[f, d]))
        for k in range(4):
            slot = jnp.bitwise_xor(me, W1_BLOCKS + 4 * f + k)
            for h in range(2):
                source = w2.at[4 * f + k, pl.ds(h * MLP_HALF, MLP_HALF)]
                copies.append(
                    pltpu.make_async_copy(source, grads.at[h, slot], sems2.at[f, 2 * k + h])
                )
        return copies

    scale = row_of(small, S2, 6)
    step = 32

    def prepare(i, carry):
        at = pl.ds(pl.multiple_of(i * step, step), step)
        rounded = (cot[at, :].astype(F32) * scale).astype(BF16)
        dm[at, :] = rounded
        macc[at, :] = jnp.zeros((step, macc.shape[1]), F32)
        dnacc[at, :] = jnp.zeros((step, macc.shape[1]), F32)
        return carry + fold8(rounded.astype(F32))

    zero = jnp.zeros((8, 768), F32)
    gb2 = lax.fori_loop(0, rows // step, prepare, zero)
    gb1[...] = jnp.zeros_like(gb1)
    tall = 256

    for f in range(CHUNKS):
        settle(arriving[f])

        def one_tile(i, carry, f=f):
            at = pl.ds(pl.multiple_of(i * tall, tall), tall)
            first = w1_matrix(w1, f)
            second = w2_matrix(w2, f)
            for c in range(CHUNK // 256):
                lanes = slice(256 * c, 256 * c + 256)
                bias = row_of(small, B1 + 6 * f + 2 * c, 2)
                z = mm(n2[at, :], first[:, lanes], NN) + bias
                du = mm(dm[at, :], second[lanes, :], NT)
                for r in range(tall // 32):
                    part = slice(32 * r, 32 * r + 32)
                    place = pl.ds(pl.multiple_of(i * tall + 32 * r, 32), 32)
                    value, slope = gelu_pair(z[part, :])
                    u[place, lanes] = value.astype(BF16)
                    rounded = (du[part, :] * slope).astype(BF16)
                    dz[place, lanes] = rounded
                    gb1[f, :, lanes] += fold8(rounded.astype(F32))
            macc[at, :] += mm(u[at, :], second, NN)
            dnacc[at, :] += mm(dz[at, :], first, NT)
            return carry

        lax.fori_loop(0, rows // tall, one_tile, 0)
        for c in range(CHUNK // 256):
            lanes = slice(256 * c, 256 * c + 256)
            grad = mm(u[:, lanes], dm[...], TN)
            for r in range(SUB):
                tile_row = SUB * c + r
                k, rt = tile_row // W2_RT, tile_row % W2_RT
                for ct in range(W2_CT):
                    tile = grad[SUB * r : SUB * r + SUB, LANES * ct : LANES * ct + LANES]
                    w2[4 * f + k, rt * W2_CT + ct] = tile.astype(BF16)
        for c in range(CHUNK // 256):
            lanes = slice(256 * c, 256 * c + 256)
            grad = mm(n2[:, lanes], dz[...], TN)
            for r in range(SUB):
                tile_row = SUB * c + r
                d, rt = tile_row // W1_RT, tile_row % W1_RT
                for ct in range(6):
                    tile = grad[SUB * r : SUB * r + SUB, LANES * ct : LANES * ct + LANES]
                    w1[f, d, ct * W1_RT + rt] = tile.astype(BF16)
        leaving = out_copies(f)
        fetch(leaving)
        arriving[f] = leaving

    bias, gain = row_of(small, B2, 6), row_of(small, G2, 6)

    def finish(i, carry):
        gs2, gg2, gc2 = carry
        at = pl.ds(pl.multiple_of(i * SUB, SUB), SUB)
        upstream = cot[at, :].astype(F32)
        values = x1[at, :]
        contracted = macc[at, :] + bias
        out[at, :] = (values + scale * contracted).astype(BF16)
        unit, inverse = normalized(values)
        grad = dnacc[at, :]
        dx1[at, :] = upstream + norm_pullback(unit, inverse, grad, gain)
        return (
            gs2 + fold8(upstream * contracted),
            gg2 + fold8(grad * unit),
            gc2 + fold8(grad),
        )

    gs2, gg2, gc2 = lax.fori_loop(0, rows // SUB, finish, (zero, zero, zero))
    put_row(vectors, G2 - G2, total(gg2))
    put_row(vectors, C2 - G2, total(gc2))
    for f in range(CHUNKS):
        put_row(vectors, B1 - G2 + 6 * f, total(gb1[f]))
    put_row(vectors, B2 - G2, total(gb2))
    put_row(vectors, S2 - G2, total(gs2))
    for f in range(CHUNKS):
        settle(arriving[f])


def feed_forward(me, n2, cot, x1, small, mlp):
    rows, width = n2.shape
    return pl.pallas_call(
        mlp_kernel,
        out_shape=(
            shape((rows, width), BF16),
            shape((rows, width), F32),
            shape((48, LANES), F32),
            shape((2, BLOCKS, MLP_HALF, SUB, LANES), BF16),
        ),
        in_specs=[smem(), vmem(), vmem(), vmem(), vmem(), anywhere(), anywhere()],
        out_specs=(vmem(), vmem(), vmem(), anywhere()),
        scratch_shapes=[
            pltpu.VMEM((CHUNKS, W1_BLOCKS, MLP_HALF // 2, SUB, LANES), BF16),
            pltpu.VMEM((W2_BLOCKS, 2 * MLP_HALF, SUB, LANES), BF16),
            pltpu.VMEM((rows, width), F32),
            pltpu.VMEM((rows, width), F32),
            pltpu.VMEM((rows, width), BF16),
            pltpu.VMEM((rows, CHUNK), BF16),
            pltpu.VMEM((rows, CHUNK), BF16),
            pltpu.VMEM((CHUNKS, 8, CHUNK), F32),
            pltpu.SemaphoreType.DMA((CHUNKS, W1_BLOCKS)),
            pltpu.SemaphoreType.DMA((CHUNKS, 8)),
        ],
        compiler_params=pltpu.CompilerParams(vmem_limit_bytes=58 * MEGA),
        cost_estimate=cost(12 * rows * width * FF, 40 * MEGA),
        name="feed_forward",
    )(me, n2, cot, x1, small, mlp[0], mlp[1])


def split_kernel(me_ref, dx1, branch, mixed, small, wa, wb, da, vectors, grads, w, db, sems):
    me = me_ref[0]
    copies = half_copies(me, QKV_BLOCKS, WO_BLOCKS, (wa, wb), w, sems)
    fetch(copies)
    rows = dx1.shape[0]
    scale = row_of(small, S1, 6)
    step = 32

    def one(i, carry):
        gs1, gbo = carry
        at = pl.ds(pl.multiple_of(i * step, step), step)
        grad = dx1[at, :]
        rounded = (grad * scale).astype(BF16)
        db[at, :] = rounded
        return gs1 + fold8(grad * branch[at, :]), gbo + fold8(rounded.astype(F32))

    zero = jnp.zeros((8, 768), F32)
    gs1, gbo = lax.fori_loop(0, rows // step, one, (zero, zero))
    put_row(vectors, 0, total(gbo))
    put_row(vectors, 6, total(gs1))
    vectors[12:16, :] = jnp.zeros((4, LANES), F32)
    settle(copies)
    weight = jnp.concatenate([wo_column(w, ct) for ct in range(WO_CT)], axis=1)
    for c in range(3):
        lanes = slice(256 * c, 256 * c + 256)
        da[:, lanes] = mm(db[...], weight[lanes, :], NT).astype(BF16)
    for c in range(3):
        grad = mm(mixed[:, 256 * c : 256 * c + 256], db[...], TN)
        for r in range(SUB):
            tile_row = SUB * c + r
            i, rt = tile_row // WO_RT, tile_row % WO_RT
            for ct in range(WO_CT):
                tile = grad[SUB * r : SUB * r + SUB, LANES * ct : LANES * ct + LANES]
                w[i, rt * WO_CT + ct] = tile.astype(BF16)
    leaving = []
    for i in range(WO_BLOCKS):
        slot = jnp.bitwise_xor(me, QKV_BLOCKS + i)
        for h in range(2):
            source = w.at[i, pl.ds(h * ATT_HALF, ATT_HALF)]
            leaving.append(pltpu.make_async_copy(source, grads.at[h, slot], sems.at[2 * i + h]))
    fetch(leaving)
    settle(leaving)


def split(me, dx1, branch, mixed, small, att):
    rows, width = dx1.shape
    return pl.pallas_call(
        split_kernel,
        out_shape=(
            shape((rows, width), BF16),
            shape((16, LANES), F32),
            shape((2, BLOCKS, ATT_HALF, SUB, LANES), BF16),
        ),
        in_specs=[smem(), vmem(), vmem(), vmem(), vmem(), anywhere(), anywhere()],
        out_specs=(vmem(), vmem(), anywhere()),
        scratch_shapes=[
            pltpu.VMEM((WO_BLOCKS, 2 * ATT_HALF, SUB, LANES), BF16),
            pltpu.VMEM((rows, width), BF16),
            pltpu.SemaphoreType.DMA((2 * WO_BLOCKS,)),
        ],
        compiler_params=pltpu.CompilerParams(vmem_limit_bytes=40 * MEGA),
        cost_estimate=cost(4 * rows * width * width, 14 * rows * width),
        name="project_backward",
    )(me, dx1, branch, mixed, small, att[0], att[1])


def attend_back_kernel(
    windows, qkv, da, stats, key_ids, query_ids, dqkv, bias, probs, dprobs, dkeys, dvalues
):
    blocks = qkv.shape[0] // QB

    def clear(b, carry):
        rows = pl.ds(pl.multiple_of(b * QB, QB), QB)
        dkeys[rows, :] = jnp.zeros((QB, dkeys.shape[1]), F32)
        dvalues[rows, :] = jnp.zeros((QB, dkeys.shape[1]), F32)
        return carry

    lax.fori_loop(0, blocks, clear, 0)

    def one_block(b, carry):
        start = pl.multiple_of(windows[0, b], SUB)
        rows = pl.ds(pl.multiple_of(b * QB, QB), QB)
        for index, width in enumerate(CLASSES):

            @pl.when(windows[1, b] == index)
            def _(width=width):
                mask_bias(start, width, b, key_ids, query_ids, bias)
                pieces = [slice(j * QB, (j + 1) * QB) for j in range(width // QB)]

                def one_pair(p, inner):
                    queries = head_masked(qkv[rows, lane_block(p, 0)] * 0.125)
                    grads = head_masked(da[rows, lane_block(p, 0)])
                    highest = stats[b * 6 + p, 0:1, :]
                    inverse = stats[b * 6 + p, 1:2, :]
                    inner_sum = jnp.zeros((8, 2 * QB), F32)
                    for piece in pieces:
                        at = pl.ds(pl.multiple_of(start + piece.start, SUB), QB)
                        part = mm(qkv[at, lane_block(p, 1)], queries, NT)
                        part = part + jnp.concatenate([bias[piece, :]] * 2, axis=1)
                        weight = jnp.exp(part - highest) * inverse
                        dweight = mm(qkv[at, lane_block(p, 2)], grads, NT)
                        inner_sum = inner_sum + fold8(weight * dweight)
                        probs[piece, :] = weight
                        dprobs[piece, :] = dweight
                        dvalues[at, lane_block(p, 0)] += mm(weight.astype(BF16), grads, NN)
                    inner_sum = total(inner_sum)
                    both = jnp.zeros((LANES, 2 * QB), F32)
                    for piece in pieces:
                        at = pl.ds(pl.multiple_of(start + piece.start, SUB), QB)
                        dscore = probs[piece, :] * (dprobs[piece, :] - inner_sum)
                        dscore = dscore.astype(BF16)
                        dkeys[at, lane_block(p, 0)] += mm(dscore, queries, NN)
                        both = both + mm(qkv[at, lane_block(p, 1)], dscore, TN)
                    out = pick_heads(both) * 0.125
                    dqkv[rows, lane_block(p, 0)] = out.T.astype(BF16)
                    return inner

                lax.fori_loop(0, 6, one_pair, 0, unroll=2)

        return carry

    lax.fori_loop(0, blocks, one_block, 0)
    width = dkeys.shape[1]

    def store(b, carry):
        rows = pl.ds(pl.multiple_of(b * 32, 32), 32)
        dqkv[rows, width : 2 * width] = dkeys[rows, :].astype(BF16)
        dqkv[rows, 2 * width :] = dvalues[rows, :].astype(BF16)
        return carry

    lax.fori_loop(0, qkv.shape[0] // 32, store, 0)


def attend_back(windows, qkv, da, stats, key_ids, query_ids):
    rows, triple = qkv.shape
    width = triple // 3
    return pl.pallas_call(
        attend_back_kernel,
        out_shape=shape((rows, triple), BF16),
        in_specs=[smem()] + [vmem()] * 5,
        out_specs=vmem(),
        scratch_shapes=[
            pltpu.VMEM((CLASSES[-1], QB), F32),
            pltpu.VMEM((CLASSES[-1], 2 * QB), F32),
            pltpu.VMEM((CLASSES[-1], 2 * QB), F32),
            pltpu.VMEM((rows, width), F32),
            pltpu.VMEM((rows, width), F32),
        ],
        compiler_params=pltpu.CompilerParams(vmem_limit_bytes=48 * MEGA),
        cost_estimate=cost(6 * rows * rows * width, 14 * rows * width, 4 * rows * rows),
        name="attend_backward",
    )(windows, qkv, da, stats, key_ids, query_ids)


def weight_grad_kernel(me_ref, n1, dqkv, given, grads, w, sems):
    me = me_ref[0]
    for c in range(3):
        for half in range(2):
            columns = slice(1152 * half, 1152 * half + 1152)
            grad = mm(n1[:, 256 * c : 256 * c + 256], dqkv[:, columns], TN)
            for r in range(SUB):
                tile_row = SUB * c + r
                d, rt = tile_row // QKV_RT, tile_row % QKV_RT
                for ct in range(9):
                    tile = grad[SUB * r : SUB * r + SUB, LANES * ct : LANES * ct + LANES]
                    w[d, (9 * half + ct) * QKV_RT + rt] = tile.astype(BF16)
    leaving = []
    for d in range(QKV_BLOCKS):
        slot = jnp.bitwise_xor(me, d)
        for h in range(2):
            source = w.at[d, pl.ds(h * ATT_HALF, ATT_HALF)]
            leaving.append(pltpu.make_async_copy(source, grads.at[h, slot], sems.at[2 * d + h]))
    fetch(leaving)
    settle(leaving)


def weight_grad(me, n1, dqkv, given):
    rows, width = n1.shape
    return pl.pallas_call(
        weight_grad_kernel,
        out_shape=shape(given.shape, BF16),
        in_specs=[smem(), vmem(), vmem(), anywhere()],
        out_specs=anywhere(),
        scratch_shapes=[
            pltpu.VMEM((QKV_BLOCKS, 2 * ATT_HALF, SUB, LANES), BF16),
            pltpu.SemaphoreType.DMA((2 * QKV_BLOCKS,)),
        ],
        input_output_aliases={3: 0},
        compiler_params=pltpu.CompilerParams(vmem_limit_bytes=40 * MEGA),
        cost_estimate=cost(6 * rows * width * width, 10 * rows * width),
        name="qkv_weight_grad",
    )(me, n1, dqkv, given)


def input_grad_kernel(me_ref, tokens, dx1, dqkv, small, wa, wb, dx, vectors, w, dn, sems):
    copies = half_copies(me_ref[0], 0, QKV_BLOCKS, (wa, wb), w, sems)
    fetch(copies)
    rows = tokens.shape[0]
    zero = jnp.zeros((8, 768), F32)

    def sums(i, carry):
        at = pl.ds(pl.multiple_of(i * 32, 32), 32)
        return (
            carry[0] + fold8(dqkv[at, 0:768].astype(F32)),
            carry[1] + fold8(dqkv[at, 1536:2304].astype(F32)),
        )

    gbq, gbv = lax.fori_loop(0, rows // 32, sums, (zero, zero))
    settle(copies)
    weight = jnp.concatenate([qkv_column(w, ct) for ct in range(QKV_CT)], axis=1)
    for c in range(3):
        lanes = slice(256 * c, 256 * c + 256)
        dn[:, lanes] = mm(dqkv[...], weight[lanes, :], NT)
    gain = row_of(small, G1, 6)

    def finish(i, carry):
        at = pl.ds(pl.multiple_of(i * SUB, SUB), SUB)
        unit, inverse = normalized(tokens[at, :].astype(F32))
        grad = dn[at, :]
        dx[at, :] = dx1[at, :] + norm_pullback(unit, inverse, grad, gain)
        return carry[0] + fold8(grad * unit), carry[1] + fold8(grad)

    gg1, gc1 = lax.fori_loop(0, rows // SUB, finish, (zero, zero))
    put_row(vectors, 0, total(gg1))
    put_row(vectors, 6, total(gc1))
    put_row(vectors, 12, total(gbq))
    put_row(vectors, 18, total(gbv))


def input_grad(me, tokens, dx1, dqkv, small, att):
    rows, width = tokens.shape
    return pl.pallas_call(
        input_grad_kernel,
        out_shape=(shape((rows, width), F32), shape((24, LANES), F32)),
        in_specs=[smem(), vmem(), vmem(), vmem(), vmem(), anywhere(), anywhere()],
        out_specs=(vmem(), vmem()),
        scratch_shapes=[
            pltpu.VMEM((QKV_BLOCKS, 2 * ATT_HALF, SUB, LANES), BF16),
            pltpu.VMEM((rows, width), F32),
            pltpu.SemaphoreType.DMA((2 * QKV_BLOCKS,)),
        ],
        compiler_params=pltpu.CompilerParams(vmem_limit_bytes=44 * MEGA),
        cost_estimate=cost(6 * rows * width * width, 18 * rows * width),
        name="input_grad",
    )(me, tokens, dx1, dqkv, small, att[0], att[1])


X, C, Z1, Z0, Y = 16, 8, 4, 2, 1


def exchange(values, bit):
    return lax.ppermute(values, AXES, [(d, d ^ bit) for d in range(BLOCKS)])


def shifted(values, by):
    pairs = [(d, d + by) for d in range(BLOCKS) if 0 <= d + by < BLOCKS]
    return lax.ppermute(values, AXES, pairs)


def widen(values, bit, axis):
    return jnp.stack([values, exchange(values, bit)], axis=axis)


def spread_blocks(halves):
    values = widen(halves, Z1, 0)
    values = widen(values, Z0, 1)
    first, second = values[:, :, 0], values[:, :, 1]
    first = widen(first, X, 0)
    second = widen(second, Y, 2)
    first = widen(first, Y, 3)
    second = widen(second, X, 0)
    first = widen(first, C, 1)
    second = widen(second, C, 1)
    flat = (BLOCKS,) + halves.shape[1:]
    return first.reshape(flat), second.reshape(flat)


def narrow_step(values, bit, axis, last=False):
    keep = lax.index_in_dim(values, 0, axis, keepdims=False)
    send = lax.index_in_dim(values, 1, axis, keepdims=False)
    summed = keep.astype(F32) + exchange(send, bit).astype(F32)
    return summed if last else summed.astype(BF16)


def reduce_blocks(grads):
    parts = []
    for half in range(2):
        values = grads[half].reshape((2, 2, 2, 2, 2) + grads.shape[2:])
        parts.append(narrow_step(values, C, 1))
    first, second = parts
    first = narrow_step(first, X, 0)
    second = narrow_step(second, Y, 3)
    first = narrow_step(first, Y, 2)
    second = narrow_step(second, X, 0)
    out = []
    for values in (first, second):
        values = narrow_step(values, Z0, 1)
        out.append(narrow_step(values, Z1, 0, last=True))
    return out


def attention_amounts(width):
    return [width, width, 3 * width * width, width, width, width * width, width, width]


def feedforward_amounts(width):
    return [width, width, width * FF, FF, FF * width, width, width]


def pieces_of(vector, amounts):
    out, offset = [], 0
    for amount in amounts:
        out.append(vector[offset : offset + amount])
        offset += amount
    return out


def tiles_by_column(matrix, blocks, rt):
    ct = matrix.shape[1] // LANES
    return matrix.reshape(blocks, rt, SUB, ct, LANES).transpose(0, 3, 1, 2, 4)


def tiles_by_row(matrix, blocks, rt):
    ct = matrix.shape[1] // LANES
    return matrix.reshape(blocks, rt, SUB, ct, LANES).transpose(0, 1, 3, 2, 4)


def gather_plainly(params, att_rows, width):
    rounded = params.astype(BF16)
    att = lax.all_gather(rounded[:att_rows], AXES, axis=0, tiled=True).reshape(-1)
    mlp = lax.all_gather(rounded[att_rows:], AXES, axis=0, tiled=True).reshape(-1)
    g1, c1, wqkv, bq, bv, wo, bo, s1 = pieces_of(att, attention_amounts(width))
    g2, c2, w1, b1, w2, b2, s2 = pieces_of(mlp, feedforward_amounts(width))
    tile = (SUB, LANES)
    att = jnp.concatenate(
        [
            tiles_by_column(wqkv.reshape(width, -1), QKV_BLOCKS, QKV_RT).reshape((-1, 36) + tile),
            tiles_by_row(wo.reshape(width, -1), WO_BLOCKS, WO_RT).reshape((-1, 36) + tile),
        ]
    )
    mlp = jnp.concatenate(
        [
            tiles_by_column(w1.reshape(width, -1), W1_BLOCKS, W1_RT).reshape((-1, 72) + tile),
            tiles_by_row(w2.reshape(FF, -1), W2_BLOCKS, W2_RT).reshape((-1, 72) + tile),
        ]
    )
    vectors = jnp.concatenate([g1, c1, bq, bv, bo, s1, g2, c2, b1, b2, s2]).astype(F32)
    small = jnp.pad(vectors.reshape(-1, LANES), ((0, SMALL - 84), (0, 0)))
    return (att[:, :18], att[:, 18:]), (mlp[:, :36], mlp[:, 36:]), small


def reduce_plainly(gatt, gmlp, small, att_rows, mlp_rows, width, devices):
    att = jnp.concatenate([gatt[0], gatt[1]], axis=1).astype(F32)
    mlp = jnp.concatenate([gmlp[0], gmlp[1]], axis=1).astype(F32)
    five = lambda v, dims: v.reshape((v.shape[0],) + dims + (SUB, LANES))
    wqkv = five(att[:QKV_BLOCKS], (QKV_CT, QKV_RT)).transpose(0, 2, 3, 1, 4).reshape(-1)
    wo = five(att[QKV_BLOCKS:], (WO_RT, WO_CT)).transpose(0, 1, 3, 2, 4).reshape(-1)
    w1 = five(mlp[:W1_BLOCKS], (W1_CT, W1_RT)).transpose(0, 2, 3, 1, 4).reshape(-1)
    w2 = five(mlp[W1_BLOCKS:], (W2_RT, W2_CT)).transpose(0, 1, 3, 2, 4).reshape(-1)
    line = lambda first, count: small[first : first + count].reshape(-1)
    att = [line(G1, 12), wqkv, line(BQ, 12), wo, line(BO, 12)]
    mlp = [line(G2, 12), w1, line(B1, 24), w2, line(B2, 12)]

    def lay(parts, rows):
        vector = jnp.concatenate(parts)
        vector = jnp.pad(vector, (0, devices * rows * LANES - vector.shape[0]))
        return vector.reshape(devices, rows, LANES)

    whole = jnp.concatenate([lay(att, att_rows), lay(mlp, mlp_rows)], axis=1)
    return lax.psum_scatter(whole.reshape(-1, LANES), AXES, scatter_dimension=0, tiled=True)


def key_windows(segments, real):
    length = segments.shape[0]
    position = jnp.arange(length, dtype=jnp.int32)
    ids = jnp.where(real, segments, length + position)
    first = segments[0::QB]
    final = segments[QB - 1 :: QB]
    begin = jnp.sum((segments[None, :] < first[:, None]).astype(jnp.int32), axis=1)
    begin = jnp.where(real[0::QB], begin, position[0::QB])
    end = jnp.sum(((segments[None, :] <= final[:, None]) & real[None, :]).astype(jnp.int32), axis=1)
    end = jnp.where(real[QB - 1 :: QB], end, position[QB - 1 :: QB] + 1)
    begin = begin // SUB * SUB
    need = end - begin
    kind = sum((need > width).astype(jnp.int32) for width in CLASSES[:-1])
    widths = sum(
        jnp.where(kind == i, width, 0) for i, width in enumerate(CLASSES)
    )
    begin = jnp.minimum(begin, length - widths)
    return ids, jnp.stack([begin, kind]).astype(jnp.int32)


def local(tokens, cotangent, segment_ids, pad_mask, lengths, params):
    rows, width = tokens.shape
    wide, narrow = lax.axis_size("wide"), lax.axis_size("narrow")
    devices = wide * narrow
    att_count = 4 * width * width + 6 * width
    att_rows = (att_count // LANES + devices - 1) // devices
    mlp_rows = params.shape[0] - att_rows
    paired = (wide, narrow) == (4, 8)
    scale = 1.0 / math.sqrt(rows * devices)

    position = jnp.arange(rows, dtype=jnp.int32)
    real = (pad_mask > 0) & (position < lengths[0])
    ids, windows = key_windows(segment_ids, real)
    key_ids = ids.reshape(rows, 1)
    query_ids = ids.reshape(rows // QB, QB)

    if paired:
        me = lax.axis_index(AXES).astype(jnp.int32).reshape(1)
        tails = jnp.concatenate([params[att_rows - ATT_BEFORE : att_rows], params[-MLP_BEFORE:]])
        heads = jnp.concatenate([params[:ATT_AFTER], params[att_rows : att_rows + MLP_AFTER]])
        tails, heads = shifted(tails, 1), shifted(heads, -1)
        att_own, mlp_own, small_own = pack(me, params, tails, heads, att_rows)
        small = lax.psum(small_own, AXES)
        att = spread_blocks(att_own)
        mlp = spread_blocks(mlp_own)
    else:
        me = jnp.zeros((1,), jnp.int32)
        att, mlp, small = gather_plainly(params, att_rows, width)

    n1, qkv = project_qkv(me, tokens, small, att)
    mixed, stats = attend(windows, qkv, key_ids, query_ids)
    x1, branch, n2 = join(me, tokens, mixed, small, att)
    output, dx1, small_mlp, gmlp = feed_forward(me, n2, cotangent, x1, small, mlp)
    da, small_proj, gatt = split(me, dx1, branch, mixed, small, att)
    dqkv = attend_back(windows, qkv, da, stats, key_ids, query_ids)
    gatt = weight_grad(me, n1, dqkv, gatt)
    grad_input, small_norm = input_grad(me, tokens, dx1, dqkv, small, att)
    small_grads = jnp.concatenate(
        [small_norm, small_proj[:12], small_mlp, jnp.zeros((SMALL - 84, LANES), F32)]
    )

    if paired:
        mlp_sums = reduce_blocks(gmlp)
        att_sums = reduce_blocks(gatt)
        small_sums = lax.psum(small_grads, AXES)
        win_a, win_m = spread(
            me, *att_sums, *mlp_sums, small_sums, att_rows, mlp_rows, scale
        )
        before = shifted(jnp.concatenate([win_a[:ATT_BEFORE], win_m[:MLP_BEFORE]]), -1)
        after = shifted(jnp.concatenate([win_a[-ATT_AFTER:], win_m[-MLP_AFTER:]]), 1)
        out_a = win_a[ATT_BEFORE : ATT_BEFORE + att_rows]
        out_m = win_m[MLP_BEFORE : MLP_BEFORE + mlp_rows]
        out_a = out_a + jnp.pad(after[:ATT_AFTER], ((0, att_rows - ATT_AFTER), (0, 0)))
        out_a = out_a + jnp.pad(before[:ATT_BEFORE], ((att_rows - ATT_BEFORE, 0), (0, 0)))
        out_m = out_m + jnp.pad(after[ATT_AFTER:], ((0, mlp_rows - MLP_AFTER), (0, 0)))
        out_m = out_m + jnp.pad(before[ATT_BEFORE:], ((mlp_rows - MLP_BEFORE, 0), (0, 0)))
        grad_params = jnp.concatenate([out_a, out_m])
    else:
        owned = reduce_plainly(gatt, gmlp, small_grads, att_rows, mlp_rows, width, devices)
        grad_params = owned * scale
    return output, grad_input, grad_params


def solution(mesh):
    return jax.shard_map(
        local,
        mesh=mesh,
        in_specs=(
            P(AXES, None),
            P(AXES, None),
            P(AXES),
            P(AXES),
            P(AXES),
            P(AXES, None),
        ),
        out_specs=(P(AXES, None), P(AXES, None), P(AXES, None)),
        check_vma=False,
    )
```

time: 1620 us -> 567 us (0.35)
  the two profiles are of different devices: /device:TPU:10 before, /device:TPU:2 now
where the time goes in v1:
time: 567 us; the launch traced here: 559 us
  Pallas kernels  199 us (35%)
  waiting for transfers between devices  134 us (24%)
  blocking collectives  91.7 us (16%)
  local copies, waits for them, and re-layouts  49 us (9%)
  starting transfers between devices  45.9 us (8%)
  other arithmetic  36.1 us (6%)
    ppermute x36, waiting for transfers between devices, exchange(): return lax.ppermute(values, AXES, [(d, d ^ bit) for d in range(BLOCKS)])  128 us
    pallas_call x1, Pallas kernels, feed_forward(): pl.pallas_call(mlp_kernel, out_shape=(shape((rows, width), BF16), shape((...  68 us
    psum x1, blocking collectives, local(): small_sums = lax.psum(small_grads, AXES)  49 us
    psum x1, blocking collectives, local(): small = lax.psum(small_own, AXES)  42.6 us
    pallas_call x1, Pallas kernels, attend_back(): pl.pallas_call(attend_back_kernel, out_shape=shape((rows, triple), BF16),...  36.8 us
    ppermute x36, starting transfers between devices, exchange(): return lax.ppermute(values, AXES, [(d, d ^ bit) for d in range(BLOCKS)])  30.9 us
    pallas_call x1, Pallas kernels, input_grad(): pl.pallas_call(input_grad_kernel, out_shape=(shape((rows, width), F32), s...  30.5 us
    unnamed x72, local copies, waits for them, and re-layouts  18.8 us
  transfers between devices with their start and end apart: 40, of which 19 were waited for; matrix products, arithmetic and copies ran while one was open for 8% of the time, Pallas kernels for 13%

profile of v1, /device:TPU:2, one launch (start us, length us, event | category | flops | bytes accessed | tf_op | source)
XLA Modules:
  0.0 558.8 jit_solution(6186509826026307799)
XLA Ops:
  1.4 3.4 collective-permute-start
  6.3 5.7 %collective-permute-start.1 = (f32[72,128]{1,0:T(8,128)S(1)}, f32[72,128]{1,0:T(8,128)S(1)}, u32[]{:S(2)}, u32[]{:S(2)}) collective-permute-start(f32[72,128]{1,0:T(8,128)S(1)} %pad_maximum_fusion.19), channel_id=1, source_target_pairs={{1,0},{2,1},{3,2},{4,3},{5,4},{6,5},{7,6},{8,7},{9,8},{10,9},{11,1... | collective-permute-start | bytes 110600 | tf_op jit(solution)/shard_map/ppermute | solution.py:898
  12.1 1.6 collective-permute-done.1.heads
  14.3 2.1 pack.1
  17.5 13.2 %collective-permute-done.10 = bf16[2,36,16,128]{3,2,1,0:T(8,128)(2,1)S(1)} collective-permute-done((bf16[2,36,16,128]{3,2,1,0:T(8,128)(2,1)}, bf16[2,36,16,128]{3,2,1,0:T(8,128)(2,1)S(1)}, u32[]{:S(2)}, u32[]{:S(2)}) %collective-permute-start.10) | collective-permute-done | bytes 294944 | tf_op jit(solution)/shard_map/ppermute | solution.py:893
  31.9 15.2 %collective-permute-done.11 = bf16[2,2,36,16,128]{4,3,2,1,0:T(8,128)(2,1)S(1)} collective-permute-done((bf16[2,2,36,16,128]{4,3,2,1,0:T(8,128)(2,1)S(1)}, bf16[2,2,36,16,128]{4,3,2,1,0:T(8,128)(2,1)S(1)}, u32[]{:S(2)}, u32[]{:S(2)}) %collective-permute-start.11) | collective-permute-done | bytes 589856 | tf_op jit(solution)/shard_map/ppermute | solution.py:893
  48.4 3.2 collective-permute-start.2
  51.6 6.2 %collective-permute-done.2 = bf16[2,18,16,128]{3,2,1,0:T(8,128)(2,1)S(1)} collective-permute-done((bf16[2,18,16,128]{3,2,1,0:T(8,128)(2,1)S(1)}, bf16[2,18,16,128]{3,2,1,0:T(8,128)(2,1)S(1)}, u32[]{:S(2)}, u32[]{:S(2)}) %collective-permute-start.2) | collective-permute-done | bytes 147488 | tf_op jit(solution)/shard_map/ppermute | solution.py:893
  58.6 3.1 collective-permute-done.15
  64.0 1.9 collective-permute-done.3
  66.9 1.6 collective-permute-start.4
  68.5 26.5 %collective-permute-done.7 = bf16[2,2,18,16,128]{4,3,2,0,1:T(8,128)(2,1)S(1)} collective-permute-done((bf16[2,2,18,16,128]{4,3,2,0,1:T(8,128)(2,1)S(1)}, bf16[2,2,18,16,128]{4,3,2,0,1:T(8,128)(2,1)S(1)}, u32[]{:S(2)}, u32[]{:S(2)}) %collective-permute-start.7) | collective-permute-done | bytes 294944 | tf_op jit(solution)/shard_map/ppermute | solution.py:893
  96.9 2.4 fusion.42
  99.4 8.1 %collective-permute-done.8 = bf16[2,2,2,18,16,128]{5,4,3,2,0,1:T(8,128)(2,1)S(1)} collective-permute-done((bf16[2,2,2,18,16,128]{5,4,3,2,0,1:T(8,128)(2,1)S(1)}, bf16[2,2,2,18,16,128]{5,4,3,2,0,1:T(8,128)(2,1)S(1)}, u32[]{:S(2)}, u32[]{:S(2)}) %collective-permute-start.8) | collective-permute-done | bytes 589856 | tf_op jit(solution)/shard_map/ppermute | solution.py:893
  108.6 2.6 fusion.43
  111.7 1.6 fusion.41
  115.2 42.6 %psum.14.small = f32[88,128]{1,0:T(8,128)S(1)} all-reduce(f32[88,128]{1,0:T(8,128)S(1)} %copy-done.25), channel_id=1, replica_groups=mesh['wide'=4,'narrow'=8] {'wide','narrow'}, use_global_device_ids=true, to_apply=%region_2.3 | all-reduce | flops 11264 | bytes 90112 | tf_op jit(solution)/shard_map/psum | solution.py:1056
  157.8 1.9 pad_maximum_fusion.3
  160.9 1.5 pad_maximum_fusion.2
  163.8 14.9 %qkv_forward.1 = (bf16[1024,768]{1,0:T(8,128)(2,1)S(1)}, bf16[1024,2304]{1,0:T(8,128)(2,1)S(1)}) custom-call(s32[1]{0:T(128)} %bitcast.me_ref, bf16[1024,768]{1,0:T(8,128)(2,1)S(1)} %copy-done.4, f32[88,128]{1,0:T(8,128)S(1)} %psum.14.small, bf16[32,18,16,128]{3,2,1,0:T(8,128)(2,1)S(1)} %bitcast.213, bf16[32,18,16,128]{3,2,1,0:T(8,128)(2,1)S(1)} %bitcast.209), custom_call_target="tpu_custom_call" | custom-call | flops 3623878656 | bytes 9437184 | tf_op jit(solution)/shard_map/qkv_forward/pallas_call | solution.py:307
  179.9 18.3 %attend_forward.1 = (bf16[1024,768]{1,0:T(8,128)(2,1)S(1)}, f32[48,2,256]{2,1,0:T(2,128)S(1)}) custom-call(s32[2,8]{1,0:T(2,128)S(1)} %pad_add_fusion.2.windows, bf16[1024,2304]{1,0:T(8,128)(2,1)S(1)} %get-tuple-element.26.qkv, s32[1024,1]{1,0:T(8,128)S(1)} %copy.30.key_ids, s32[8,128]{1,0:T(8,128)S(1)} %bitcast.218), custom_call_target="tpu_custom_call" | custom-call | flops 1610612736 | bytes 6291456 | tf_op jit(solution)/shard_map/attend_forward/pallas_call | solution.py:397
  198.2 10.8 %project_and_norm.1 = (f32[1024,768]{1,0:T(8,128)S(1)}, f32[1024,768]{1,0:T(8,128)}, bf16[1024,768]{1,0:T(8,128)(2,1)S(1)}) custom-call(s32[1]{0:T(128)} %bitcast.me_ref, bf16[1024,768]{1,0:T(8,128)(2,1)S(1)} %copy-done.4, bf16[1024,768]{1,0:T(8,128)(2,1)S(1)} %get-tuple-element.27.mixed, f32[88,128]{1,0:T(8,128)S(1)} %psum.14.small, ...), custom_call_target="tpu_custom_call" | custom-call | flops 1207959552 | bytes 11010048 | tf_op jit(solution)/shard_map/project_and_norm/pallas_call | solution.py:438
  209.1 3.8 pad_maximum_fusion.1
  212.9 3.1 copy.32
  216.0 2.1 pad_maximum_fusion
  218.1 2.9 copy.31
  221.1 68.0 %feed_forward.1 = (bf16[1024,768]{1,0:T(8,128)(2,1)}, f32[1024,768]{1,0:T(8,128)}, f32[48,128]{1,0:T(8,128)}, bf16[2,32,36,16,128]{4,3,2,1,0:T(8,128)(2,1)}) custom-call(s32[1]{0:T(128)} %bitcast.me_ref, bf16[1024,768]{1,0:T(8,128)(2,1)} %copy-done.14, bf16[1024,768]{1,0:T(8,128)(2,1)} %cot.1, f32[1024,768]{1,0:T(8,128)} %copy-done.13, ...), custom_call_target="tpu_custom_call" | custom-call | flops 28991029248 | bytes 41943040 | tf_op jit(solution)/shard_map/feed_forward/pallas_call | solution.py:614
  289.1 9.0 %fusion.46 = (bf16[1,32,36,16,128]{4,3,2,1,0:T(8,128)(2,1)}, bf16[1,32,36,16,128]{4,3,2,1,0:T(8,128)(2,1)}) fusion(bf16[2,32,36,16,128]{4,3,2,1,0:T(8,128)(2,1)} %get-tuple-element.39), kind=kLoop, calls=%fused_computation.150 | loop fusion | bytes 18874368 | tf_op jit(solution)/shard_map/slice | solution.py:929
  299.6 1.9 copy-done.8
  301.5 6.2 %project_backward.1 = (bf16[1024,768]{1,0:T(8,128)(2,1)S(1)}, f32[16,128]{1,0:T(8,128)S(1)}, bf16[2,32,18,16,128]{4,3,2,1,0:T(8,128)(2,1)}) custom-call(s32[1]{0:T(128)} %bitcast.me_ref, f32[1024,768]{1,0:T(8,128)S(1)} %copy-done.2, f32[1024,768]{1,0:T(8,128)S(1)} %copy-done.8, bf16[1024,768]{1,0:T(8,128)(2,1)S(1)} %copy-done.7, f32[88,128]{1,0:T(8,128)S(1)} %copy-done.12, ...), custom_call_target="tpu_custom_call" | custom-call | flops 2415919104 | bytes 11010048 | tf_op jit(solution)/shard_map/project_backward/pallas_call | solution.py:688
  310.2 36.8 %attend_backward.1.dqkv = bf16[1024,2304]{1,0:T(8,128)(2,1)} custom-call(s32[2,8]{1,0:T(2,128)S(1)} %pad_add_fusion.2.windows, bf16[1024,2304]{1,0:T(8,128)(2,1)} %copy-done.17, bf16[1024,768]{1,0:T(8,128)(2,1)S(1)} %copy-done.16, f32[48,2,256]{2,1,0:T(2,128)S(1)} %get-tuple-element.35.stats, s32[1024,1]{1,0:T(8,128)S(1)} %copy.30.key_ids, ...), custom_call_target="tpu_custom_call" | custom-call | flops 4831838208 | bytes 11010048 | tf_op jit(solution)/shard_map/attend_backward/pallas_call | solution.py:778
  347.0 2.3 copy-done.1
  349.3 9.6 %qkv_weight_grad.1 = bf16[2,32,18,16,128]{4,3,2,1,0:T(8,128)(2,1)S(1)} custom-call(s32[1]{0:T(128)} %bitcast.me_ref, bf16[1024,768]{1,0:T(8,128)(2,1)S(1)} %copy-done.10, bf16[1024,2304]{1,0:T(8,128)(2,1)S(1)} %copy-done.1, bf16[2,32,18,16,128]{4,3,2,1,0:T(8,128)(2,1)S(1)} %copy-done), custom_call_target="tpu_custom_call", output_to_operand_aliasing={{}: (3, {})} | custom-call | flops 3623878656 | bytes 7864320 | tf_op jit(solution)/shard_map/qkv_weight_grad/pallas_call | solution.py:820
  361.5 2.2 fusion.47
  363.7 1.8 copy.66
  367.7 2.3 fusion.48
  370.0 1.8 copy.67
  373.2 30.5 %input_grad.1 = (f32[1024,768]{1,0:T(8,128)}, f32[24,128]{1,0:T(8,128)S(1)}) custom-call(s32[1]{0:T(128)} %bitcast.me_ref, bf16[1024,768]{1,0:T(8,128)(2,1)S(1)} %copy-done.5, f32[1024,768]{1,0:T(8,128)S(1)} %copy-done.3, bf16[1024,2304]{1,0:T(8,128)(2,1)} %attend_backward.1.dqkv, f32[88,128]{1,0:T(8,128)S(1)} %copy-done.12, ...), custom_call_target="tpu_custom_call" | custom-call | flops 3623878656 | bytes 14155776 | tf_op jit(solution)/shard_map/input_grad/pallas_call | solution.py:873
  403.7 1.6 fusion.4
  406.3 1.6 fusion.5
  409.2 49.0 %psum.15.small = f32[88,128]{1,0:T(8,128)} all-reduce(f32[88,128]{1,0:T(8,128)} %maximum_maximum_fusion), channel_id=1, replica_groups=mesh['wide'=4,'narrow'=8] {'wide','narrow'}, use_global_device_ids=true, to_apply=%region_3.4 | all-reduce | flops 11264 | bytes 90112 | tf_op jit(solution)/shard_map/psum | solution.py:1078
  459.8 2.1 collective-permute-start.20
  461.9 4.5 collective-permute-done.25
  466.5 1.4 collective-permute-start.26
  468.8 3.7 collective-permute-done.26
  473.3 2.3 fusion
  475.8 3.2 collective-permute-start.34
  479.0 2.3 fusion.1
  481.7 1.5 collective-permute-start.22
  483.9 16.8 %collective-permute-done.34 = bf16[2,2,2,36,16,128]{5,4,3,1,2,0:T(8,128)(2,1)S(1)} collective-permute-done((bf16[2,2,2,36,16,128]{5,4,3,1,2,0:T(8,128)(2,1)S(1)}, bf16[2,2,2,36,16,128]{5,4,3,1,2,0:T(8,128)(2,1)S(1)}, u32[]{:S(2)}, u32[]{:S(2)}) %collective-permute-start.34) | collective-permute-done | bytes 1179680 | tf_op jit(solution)/shard_map/ppermute | solution.py:893
  501.6 8.9 %collective-permute-done.29 = bf16[2,2,2,36,16,128]{5,4,3,0,1,2:T(8,128)(2,1)S(1)} collective-permute-done((bf16[2,2,2,36,16,128]{5,4,3,0,1,2:T(8,128)(2,1)S(1)}, bf16[2,2,2,36,16,128]{5,4,3,0,1,2:T(8,128)(2,1)S(1)}, u32[]{:S(2)}, u32[]{:S(2)}) %collective-permute-start.29) | collective-permute-done | bytes 1179680 | tf_op jit(solution)/shard_map/ppermute | solution.py:893
  510.9 1.4 collective-permute-start.30
  513.0 4.4 collective-permute-done.35
  518.4 2.5 collective-permute-done.30
  521.2 6.1 %collective-permute-done.36 = bf16[2,36,16,128]{3,2,1,0:T(8,128)(2,1)S(1)} collective-permute-done((bf16[2,36,16,128]{3,2,1,0:T(8,128)(2,1)S(1)}, bf16[2,36,16,128]{3,2,1,0:T(8,128)(2,1)S(1)}, u32[]{:S(2)}, u32[]{:S(2)}) %collective-permute-start.36) | collective-permute-done | bytes 294944 | tf_op jit(solution)/shard_map/ppermute | solution.py:893
  527.4 1.8 collective-permute-start.37
  529.2 1.6 collective-permute-done.31
  530.8 1.9 collective-permute-start.32
  532.8 2.3 collective-permute-done.37
  535.8 2.7 collective-permute-done.32
  539.3 2.3 spread.1
  544.6 1.9 collective-permute-start.39
  546.5 3.9 collective-permute-start.38
  550.5 4.9 collective-permute-done.38
  (197 shorter events, 46.8 us)
Async XLA Ops:
  1.4 12.3 %collective-permute-start = (f32[128,128]{1,0:T(8,128)S(1)}, f32[128,128]{1,0:T(8,128)S(1)}, u32[]{:S(2)}, u32[]{:S(2)}) collective-permute-start(f32[128,128]{1,0:T(8,128)S(1)} %pad_maximum_fusion.17), channel_id=1, source_target_pairs={{0,1},{1,2},{2,3},{3,4},{4,5},{5,6},{6,7},{7,8},{8,9},{9,10},{10,1... | collective-permute-start | bytes 196616 | tf_op jit(solution)/shard_map/ppermute | solution.py:898
  6.3 7.3 %collective-permute-start.1 = (f32[72,128]{1,0:T(8,128)S(1)}, f32[72,128]{1,0:T(8,128)S(1)}, u32[]{:S(2)}, u32[]{:S(2)}) collective-permute-start(f32[72,128]{1,0:T(8,128)S(1)} %pad_maximum_fusion.19), channel_id=1, source_target_pairs={{1,0},{2,1},{3,2},{4,3},{5,4},{6,5},{7,6},{8,7},{9,8},{10,9},{11,1... | collective-permute-start | bytes 110600 | tf_op jit(solution)/shard_map/ppermute | solution.py:898
  16.4 14.3 %collective-permute-start.10 = (bf16[2,36,16,128]{3,2,1,0:T(8,128)(2,1)}, bf16[2,36,16,128]{3,2,1,0:T(8,128)(2,1)S(1)}, u32[]{:S(2)}, u32[]{:S(2)}) collective-permute-start(bf16[2,36,16,128]{3,2,1,0:T(8,128)(2,1)} %get-tuple-element.30), channel_id=1, source_target_pairs={{0,4},{1,5},{2,6},{3,7},{4,0},{5,1},{6,2},{7,3},{8,12},{9,13},{10,... | collective-permute-start | bytes 884744 | tf_op jit(solution)/shard_map/ppermute | solution.py:893
  30.7 17.7 %copy-start.23 = (bf16[2,18,16,128]{3,2,1,0:T(8,128)(2,1)S(1)}, bf16[2,18,16,128]{3,2,1,0:T(8,128)(2,1)}, u32[]{:S(2)}) copy-start(bf16[2,18,16,128]{3,2,1,0:T(8,128)(2,1)} %get-tuple-element.25) | copy-start | bytes 442372
  31.8 15.3 %collective-permute-start.11 = (bf16[2,2,36,16,128]{4,3,2,1,0:T(8,128)(2,1)S(1)}, bf16[2,2,36,16,128]{4,3,2,1,0:T(8,128)(2,1)S(1)}, u32[]{:S(2)}, u32[]{:S(2)}) collective-permute-start(bf16[2,2,36,16,128]{4,3,2,1,0:T(8,128)(2,1)S(1)} %get-tuple-element.81), channel_id=1, source_target_pairs={{0,2},{1,3},{2,0},{3,1},{4,6},{5,7},{6,4},{7,5},{8,10},{9,11},{10,... | collective-permute-start | bytes 1769480 | tf_op jit(solution)/shard_map/ppermute | solution.py:893
  47.2 14.5 %collective-permute-start.15 = (bf16[2,2,36,16,128]{4,3,2,0,1:T(8,128)(2,1)S(1)}, bf16[2,2,36,16,128]{4,3,2,0,1:T(8,128)(2,1)S(1)}, u32[]{:S(2)}, u32[]{:S(2)}) collective-permute-start(bf16[2,2,36,16,128]{4,3,2,0,1:T(8,128)(2,1)S(1)} %bitcast.231), channel_id=1, source_target_pairs={{0,1},{1,0},{2,3},{3,2},{4,5},{5,4},{6,7},{7,6},{8,9},{9,8},{10,11... | collective-permute-start | bytes 1769480 | tf_op jit(solution)/shard_map/ppermute | solution.py:893
  47.6 15.0 %collective-permute-start.12 = (bf16[2,2,36,16,128]{4,3,2,0,1:T(8,128)(2,1)S(1)}, bf16[2,2,36,16,128]{4,3,2,0,1:T(8,128)(2,1)S(1)}, u32[]{:S(2)}, u32[]{:S(2)}) collective-permute-start(bf16[2,2,36,16,128]{4,3,2,0,1:T(8,128)(2,1)S(1)} %get-tuple-element.70), channel_id=1, source_target_pairs={{0,16},{1,17},{2,18},{3,19},{4,20},{5,21},{6,22},{7,23},{8,24},{9,... | collective-permute-start | bytes 1769480 | tf_op jit(solution)/shard_map/ppermute | solution.py:893
  48.4 9.4 %collective-permute-start.2 = (bf16[2,18,16,128]{3,2,1,0:T(8,128)(2,1)S(1)}, bf16[2,18,16,128]{3,2,1,0:T(8,128)(2,1)S(1)}, u32[]{:S(2)}, u32[]{:S(2)}) collective-permute-start(bf16[2,18,16,128]{3,2,1,0:T(8,128)(2,1)S(1)} %copy-done.23), channel_id=1, source_target_pairs={{0,4},{1,5},{2,6},{3,7},{4,0},{5,1},{6,2},{7,3},{8,12},{9,13},{10,... | collective-permute-start | bytes 442376 | tf_op jit(solution)/shard_map/ppermute | solution.py:893
  57.9 8.1 %collective-permute-start.3 = (bf16[2,2,18,16,128]{4,3,2,1,0:T(8,128)(2,1)S(1)}, bf16[2,2,18,16,128]{4,3,2,1,0:T(8,128)(2,1)S(1)}, u32[]{:S(2)}, u32[]{:S(2)}) collective-permute-start(bf16[2,2,18,16,128]{4,3,2,1,0:T(8,128)(2,1)S(1)} %get-tuple-element.90), channel_id=1, source_target_pairs={{0,2},{1,3},{2,0},{3,1},{4,6},{5,7},{6,4},{7,5},{8,10},{9,11},{10,... | collective-permute-start | bytes 884744 | tf_op jit(solution)/shard_map/ppermute | solution.py:893
  61.8 35.1 %collective-permute-start.16 = (bf16[2,2,2,36,16,128]{5,4,3,2,0,1:T(8,128)(2,1)S(1)}, bf16[2,2,2,36,16,128]{5,4,3,2,0,1:T(8,128)(2,1)S(1)}, u32[]{:S(2)}, u32[]{:S(2)}) collective-permute-start(bf16[2,2,2,36,16,128]{5,4,3,2,0,1:T(8,128)(2,1)S(1)} %get-tuple-element.68), channel_id=1, source_target_pairs={{0,16},{1,17},{2,18},{3,19},{4,20},{5,21},{6,22},{7,23},{8,24},{9,... | collective-permute-start | bytes 3538952 | tf_op jit(solution)/shard_map/ppermute | solution.py:893
  62.7 45.9 %collective-permute-start.13 = (bf16[2,2,2,36,16,128]{5,4,3,1,2,0:T(8,128)(2,1)S(1)}, bf16[2,2,2,36,16,128]{5,4,3,1,2,0:T(8,128)(2,1)S(1)}, u32[]{:S(2)}, u32[]{:S(2)}) collective-permute-start(bf16[2,2,2,36,16,128]{5,4,3,1,2,0:T(8,128)(2,1)S(1)} %get-tuple-element.73), channel_id=1, source_target_pairs={{0,1},{1,0},{2,3},{3,2},{4,5},{5,4},{6,7},{7,6},{8,9},{9,8},{10,11... | collective-permute-start | bytes 3538952 | tf_op jit(solution)/shard_map/ppermute | solution.py:893
  66.0 29.0 %collective-permute-start.7 = (bf16[2,2,18,16,128]{4,3,2,0,1:T(8,128)(2,1)S(1)}, bf16[2,2,18,16,128]{4,3,2,0,1:T(8,128)(2,1)S(1)}, u32[]{:S(2)}, u32[]{:S(2)}) collective-permute-start(bf16[2,2,18,16,128]{4,3,2,0,1:T(8,128)(2,1)S(1)} %bitcast.234), channel_id=1, source_target_pairs={{0,1},{1,0},{2,3},{3,2},{4,5},{5,4},{6,7},{7,6},{8,9},{9,8},{10,11... | collective-permute-start | bytes 884744 | tf_op jit(solution)/shard_map/ppermute | solution.py:893
  66.9 29.6 %collective-permute-start.4 = (bf16[2,2,18,16,128]{4,3,2,0,1:T(8,128)(2,1)S(1)}, bf16[2,2,18,16,128]{4,3,2,0,1:T(8,128)(2,1)S(1)}, u32[]{:S(2)}, u32[]{:S(2)}) collective-permute-start(bf16[2,2,18,16,128]{4,3,2,0,1:T(8,128)(2,1)S(1)} %get-tuple-element.85), channel_id=1, source_target_pairs={{0,16},{1,17},{2,18},{3,19},{4,20},{5,21},{6,22},{7,23},{8,24},{9,... | collective-permute-start | bytes 884744 | tf_op jit(solution)/shard_map/ppermute | solution.py:893
  95.1 12.4 %collective-permute-start.8 = (bf16[2,2,2,18,16,128]{5,4,3,2,0,1:T(8,128)(2,1)S(1)}, bf16[2,2,2,18,16,128]{5,4,3,2,0,1:T(8,128)(2,1)S(1)}, u32[]{:S(2)}, u32[]{:S(2)}) collective-permute-start(bf16[2,2,2,18,16,128]{5,4,3,2,0,1:T(8,128)(2,1)S(1)} %get-tuple-element.83), channel_id=1, source_target_pairs={{0,16},{1,17},{2,18},{3,19},{4,20},{5,21},{6,22},{7,23},{8,24},{9,... | collective-permute-start | bytes 1769480 | tf_op jit(solution)/shard_map/ppermute | solution.py:893
  96.6 15.2 %collective-permute-start.5 = (bf16[2,2,2,18,16,128]{5,4,3,1,2,0:T(8,128)(2,1)S(1)}, bf16[2,2,2,18,16,128]{5,4,3,1,2,0:T(8,128)(2,1)S(1)}, u32[]{:S(2)}, u32[]{:S(2)}) collective-permute-start(bf16[2,2,2,18,16,128]{5,4,3,1,2,0:T(8,128)(2,1)S(1)} %get-tuple-element.88), channel_id=1, source_target_pairs={{0,1},{1,0},{2,3},{3,2},{4,5},{5,4},{6,7},{7,6},{8,9},{9,8},{10,11... | collective-permute-start | bytes 1769480 | tf_op jit(solution)/shard_map/ppermute | solution.py:893
  99.4 109.7 %collective-permute-start.17 = (bf16[2,2,2,2,36,16,128]{6,5,4,3,1,2,0:T(8,128)(2,1)}, bf16[2,2,2,2,36,16,128]{6,5,4,3,1,2,0:T(8,128)(2,1)}, u32[]{:S(2)}, u32[]{:S(2)}) collective-permute-start(bf16[2,2,2,2,36,16,128]{6,5,4,3,1,2,0:T(8,128)(2,1)} %get-tuple-element.64), channel_id=1, source_target_pairs={{0,8},{1,9},{2,10},{3,11},{4,12},{5,13},{6,14},{7,15},{8,0},{9,1},... | collective-permute-start | bytes 7077896 | tf_op jit(solution)/shard_map/ppermute | solution.py:893
  108.6 49.2 %collective-permute-start.9 = (bf16[2,2,2,2,18,16,128]{6,5,4,3,1,2,0:T(8,128)(2,1)S(1)}, bf16[2,2,2,2,18,16,128]{6,5,4,3,1,2,0:T(8,128)(2,1)}, u32[]{:S(2)}, u32[]{:S(2)}) collective-permute-start(bf16[2,2,2,2,18,16,128]{6,5,4,3,1,2,0:T(8,128)(2,1)S(1)} %get-tuple-element.75), channel_id=1, source_target_pairs={{0,8},{1,9},{2,10},{3,11},{4,12},{5,13},{6,14},{7,15},{8,0},{9,1},... | collective-permute-start | bytes 3538952 | tf_op jit(solution)/shard_map/ppermute | solution.py:893
  111.2 2.9 copy-start.29
  111.2 3.9 copy-start.25
  111.2 104.8 %collective-permute-start.14 = (bf16[2,2,2,2,36,16,128]{6,5,4,1,2,0,3:T(8,128)(2,1)}, bf16[2,2,2,2,36,16,128]{6,5,4,1,2,0,3:T(8,128)(2,1)}, u32[]{:S(2)}, u32[]{:S(2)}) collective-permute-start(bf16[2,2,2,2,36,16,128]{6,5,4,1,2,0,3:T(8,128)(2,1)} %get-tuple-element.66), channel_id=1, source_target_pairs={{0,8},{1,9},{2,10},{3,11},{4,12},{5,13},{6,14},{7,15},{8,0},{9,1},... | collective-permute-start | bytes 7077896 | tf_op jit(solution)/shard_map/ppermute | solution.py:893
  113.3 46.8 %collective-permute-start.6 = (bf16[2,2,2,2,18,16,128]{6,5,4,1,2,0,3:T(8,128)(2,1)}, bf16[2,2,2,2,18,16,128]{6,5,4,1,2,0,3:T(8,128)(2,1)}, u32[]{:S(2)}, u32[]{:S(2)}) collective-permute-start(bf16[2,2,2,2,18,16,128]{6,5,4,1,2,0,3:T(8,128)(2,1)} %get-tuple-element.77), channel_id=1, source_target_pairs={{0,8},{1,9},{2,10},{3,11},{4,12},{5,13},{6,14},{7,15},{8,0},{9,1},... | collective-permute-start | bytes 3538952 | tf_op jit(solution)/shard_map/ppermute | solution.py:893
  157.8 40.4 %copy-start.11 = (f32[88,128]{1,0:T(8,128)}, f32[88,128]{1,0:T(8,128)S(1)}, u32[]{:S(2)}) copy-start(f32[88,128]{1,0:T(8,128)S(1)} %psum.14.small) | copy-start | bytes 135172
  179.9 18.3 %copy-start.17 = (bf16[1024,2304]{1,0:T(8,128)(2,1)}, bf16[1024,2304]{1,0:T(8,128)(2,1)S(1)}, u32[]{:S(2)}) copy-start(bf16[1024,2304]{1,0:T(8,128)(2,1)S(1)} %get-tuple-element.26.qkv) | copy-start | bytes 14155780
  198.2 10.9 %copy-start.6 = (bf16[1024,768]{1,0:T(8,128)(2,1)}, bf16[1024,768]{1,0:T(8,128)(2,1)S(1)}, u32[]{:S(2)}) copy-start(bf16[1024,768]{1,0:T(8,128)(2,1)S(1)} %get-tuple-element.27.mixed) | copy-start | bytes 4718596
  198.2 10.9 %copy-start.19 = (bf16[2,1,2,2,2,36,16,128]{7,6,5,4,2,3,0,1:T(8,128)(2,1)S(1)}, bf16[2,1,2,2,2,36,16,128]{7,6,5,4,2,3,0,1:T(8,128)(2,1)}, u32[]{:S(2)}) copy-start(bf16[2,1,2,2,2,36,16,128]{7,6,5,4,2,3,0,1:T(8,128)(2,1)} %get-tuple-element.63) | copy-start | bytes 7077892
  209.0 3.8 copy-start.13
  209.1 3.8 copy-start.14
  212.9 3.2 copy-start.21
  289.1 9.1 %copy-start.2 = (f32[1024,768]{1,0:T(8,128)S(1)}, f32[1024,768]{1,0:T(8,128)}, u32[]{:S(2)}) copy-start(f32[1024,768]{1,0:T(8,128)} %get-tuple-element.32.dx1) | copy-start | bytes 9437188
  289.1 9.1 %copy-start.12 = (f32[88,128]{1,0:T(8,128)S(1)}, f32[88,128]{1,0:T(8,128)}, u32[]{:S(2)}) copy-start(f32[88,128]{1,0:T(8,128)} %copy-done.11) | copy-start | bytes 135172
  310.2 36.8 %copy-start = (bf16[2,32,18,16,128]{4,3,2,1,0:T(8,128)(2,1)S(1)}, bf16[2,32,18,16,128]{4,3,2,1,0:T(8,128)(2,1)}, u32[]{:S(2)}) copy-start(bf16[2,32,18,16,128]{4,3,2,1,0:T(8,128)(2,1)} %get-tuple-element.38.given) | copy-start | bytes 14155780
  310.2 36.8 %copy-start.10 = (bf16[1024,768]{1,0:T(8,128)(2,1)S(1)}, bf16[1024,768]{1,0:T(8,128)(2,1)}, u32[]{:S(2)}) copy-start(bf16[1024,768]{1,0:T(8,128)(2,1)} %copy-done.9) | copy-start | bytes 4718596
  347.0 2.3 copy-start.1
  349.3 12.1 %slice-start.2 = ((s8[4718592]{0:T(1024)(128)(4,1)}), s8[524288]{0:T(1024)(128)(4,1)S(1)}, s32[]{:S(2)}) async-start(s8[4718592]{0:T(1024)(128)(4,1)} %bitcast.224), calls=%async_computation.2 | async-start | bytes 1048576
  358.9 2.5 slice-start.3
  361.5 42.3 %collective-permute-start.23 = (bf16[2,2,2,2,18,16,128]{6,5,4,1,2,0,3:T(8,128)(2,1)}, bf16[2,2,2,2,18,16,128]{6,5,4,1,2,0,3:T(8,128)(2,1)}, u32[]{:S(2)}, u32[]{:S(2)}) collective-permute-start(bf16[2,2,2,2,18,16,128]{6,5,4,1,2,0,3:T(8,128)(2,1)} %bitcast.205), channel_id=1, source_target_pairs={{0,8},{1,9},{2,10},{3,11},{4,12},{5,13},{6,14},{7,15},{8,0},{9,1},... | collective-permute-start | bytes 3538952 | tf_op jit(solution)/shard_map/ppermute | solution.py:893
  361.5 6.3 %slice-start = ((s8[4718592]{0:T(1024)(128)(4,1)}), s8[4194304]{0:T(1024)(128)(4,1)S(1)}, s32[]{:S(2)}) async-start(s8[4718592]{0:T(1024)(128)(4,1)} %bitcast.221), calls=%async_computation | async-start | bytes 8388608
  363.7 4.0 slice-start.1
  365.6 107.7 %collective-permute-start.33 = (bf16[2,2,2,2,36,16,128]{6,5,4,1,2,0,3:T(8,128)(2,1)}, bf16[2,2,2,2,36,16,128]{6,5,4,1,2,0,3:T(8,128)(2,1)}, u32[]{:S(2)}, u32[]{:S(2)}) collective-permute-start(bf16[2,2,2,2,36,16,128]{6,5,4,1,2,0,3:T(8,128)(2,1)} %bitcast.203), channel_id=1, source_target_pairs={{0,8},{1,9},{2,10},{3,11},{4,12},{5,13},{6,14},{7,15},{8,0},{9,1},... | collective-permute-start | bytes 7077896 | tf_op jit(solution)/shard_map/ppermute | solution.py:893
  367.7 38.5 %collective-permute-start.18 = (bf16[2,2,2,2,18,16,128]{6,5,4,1,2,3,0:T(8,128)(2,1)}, bf16[2,2,2,2,18,16,128]{6,5,4,1,2,3,0:T(8,128)(2,1)}, u32[]{:S(2)}, u32[]{:S(2)}) collective-permute-start(bf16[2,2,2,2,18,16,128]{6,5,4,1,2,3,0:T(8,128)(2,1)} %bitcast.206), channel_id=1, source_target_pairs={{0,8},{1,9},{2,10},{3,11},{4,12},{5,13},{6,14},{7,15},{8,0},{9,1},... | collective-permute-start | bytes 3538952 | tf_op jit(solution)/shard_map/ppermute | solution.py:893
  370.0 2.7 copy-start.3
  370.0 3.2 copy-start.5
  371.8 107.2 %collective-permute-start.28 = (bf16[2,2,2,2,36,16,128]{6,5,4,1,2,3,0:T(8,128)(2,1)}, bf16[2,2,2,2,36,16,128]{6,5,4,1,2,3,0:T(8,128)(2,1)}, u32[]{:S(2)}, u32[]{:S(2)}) collective-permute-start(bf16[2,2,2,2,36,16,128]{6,5,4,1,2,3,0:T(8,128)(2,1)} %bitcast.204), channel_id=1, source_target_pairs={{0,8},{1,9},{2,10},{3,11},{4,12},{5,13},{6,14},{7,15},{8,0},{9,1},... | collective-permute-start | bytes 7077896 | tf_op jit(solution)/shard_map/ppermute | solution.py:893
  406.2 52.0 %collective-permute-start.24 = (bf16[2,2,2,18,16,128]{5,4,3,1,2,0:T(8,128)(2,1)}, bf16[2,2,2,18,16,128]{5,4,3,1,2,0:T(8,128)(2,1)}, u32[]{:S(2)}, u32[]{:S(2)}) collective-permute-start(bf16[2,2,2,18,16,128]{5,4,3,1,2,0:T(8,128)(2,1)} %slice_bitcast_fusion.8), channel_id=1, source_target_pairs={{0,1},{1,0},{2,3},{3,2},{4,5},{5,4},{6,7},{7,6},{8,9},{9,8},{10,11... | collective-permute-start | bytes 1769480 | tf_op jit(solution)/shard_map/ppermute | solution.py:893
  406.3 2.3 copy-start.27
  408.0 51.6 %collective-permute-start.19 = (bf16[2,2,2,18,16,128]{5,4,3,0,1,2:T(8,128)(2,1)S(1)}, bf16[2,2,2,18,16,128]{5,4,3,0,1,2:T(8,128)(2,1)S(1)}, u32[]{:S(2)}, u32[]{:S(2)}) collective-permute-start(bf16[2,2,2,18,16,128]{5,4,3,0,1,2:T(8,128)(2,1)S(1)} %slice_bitcast_fusion.10), channel_id=1, source_target_pairs={{0,16},{1,17},{2,18},{3,19},{4,20},{5,21},{6,22},{7,23},{8,24},{9,... | collective-permute-start | bytes 1769480 | tf_op jit(solution)/shard_map/ppermute | solution.py:893
  459.5 13.8 %copy-start.18 = (bf16[2,1,2,2,2,36,16,128]{7,6,5,4,3,2,1,0:T(8,128)(2,1)S(1)}, bf16[2,1,2,2,2,36,16,128]{7,6,5,4,3,2,1,0:T(8,128)(2,1)}, u32[]{:S(2)}) copy-start(bf16[2,1,2,2,2,36,16,128]{7,6,5,4,3,2,1,0:T(8,128)(2,1)} %get-tuple-element.53) | copy-start | bytes 7077892
  459.5 6.9 %collective-permute-start.25 = (bf16[2,2,18,16,128]{4,3,2,0,1:T(8,128)(2,1)S(1)}, bf16[2,2,18,16,128]{4,3,2,0,1:T(8,128)(2,1)S(1)}, u32[]{:S(2)}, u32[]{:S(2)}) collective-permute-start(bf16[2,2,18,16,128]{4,3,2,0,1:T(8,128)(2,1)S(1)} %slice_bitcast_fusion.16), channel_id=1, source_target_pairs={{0,16},{1,17},{2,18},{3,19},{4,20},{5,21},{6,22},{7,23},{8,24},{9,... | collective-permute-start | bytes 884744 | tf_op jit(solution)/shard_map/ppermute | solution.py:893
  459.8 8.1 %collective-permute-start.20 = (bf16[2,2,18,16,128]{4,3,2,0,1:T(8,128)(2,1)S(1)}, bf16[2,2,18,16,128]{4,3,2,0,1:T(8,128)(2,1)S(1)}, u32[]{:S(2)}, u32[]{:S(2)}) collective-permute-start(bf16[2,2,18,16,128]{4,3,2,0,1:T(8,128)(2,1)S(1)} %slice_bitcast_fusion.18), channel_id=1, source_target_pairs={{0,1},{1,0},{2,3},{3,2},{4,5},{5,4},{6,7},{7,6},{8,9},{9,8},{10,11... | collective-permute-start | bytes 884744 | tf_op jit(solution)/shard_map/ppermute | solution.py:893
  466.5 6.0 %collective-permute-start.26 = (bf16[2,18,16,128]{3,2,1,0:T(8,128)(2,1)S(1)}, bf16[2,18,16,128]{3,2,1,0:T(8,128)(2,1)S(1)}, u32[]{:S(2)}, u32[]{:S(2)}) collective-permute-start(bf16[2,18,16,128]{3,2,1,0:T(8,128)(2,1)S(1)} %slice_bitcast_fusion.24), channel_id=1, source_target_pairs={{0,2},{1,3},{2,0},{3,1},{4,6},{5,7},{6,4},{7,5},{8,10},{9,11},{10,... | collective-permute-start | bytes 442376 | tf_op jit(solution)/shard_map/ppermute | solution.py:893
  468.0 13.6 %collective-permute-start.21 = (bf16[2,18,16,128]{3,2,1,0:T(8,128)(2,1)S(1)}, bf16[2,18,16,128]{3,2,1,0:T(8,128)(2,1)S(1)}, u32[]{:S(2)}, u32[]{:S(2)}) collective-permute-start(bf16[2,18,16,128]{3,2,1,0:T(8,128)(2,1)S(1)} %slice_bitcast_fusion.26), channel_id=1, source_target_pairs={{0,2},{1,3},{2,0},{3,1},{4,6},{5,7},{6,4},{7,5},{8,10},{9,11},{10,... | collective-permute-start | bytes 442376 | tf_op jit(solution)/shard_map/ppermute | solution.py:893
  472.6 10.7 %collective-permute-start.27 = (bf16[18,16,128]{2,1,0:T(8,128)(2,1)S(1)}, bf16[18,16,128]{2,1,0:T(8,128)(2,1)S(1)}, u32[]{:S(2)}, u32[]{:S(2)}) collective-permute-start(bf16[18,16,128]{2,1,0:T(8,128)(2,1)S(1)} %slice_bitcast_fusion.28), channel_id=1, source_target_pairs={{0,4},{1,5},{2,6},{3,7},{4,0},{5,1},{6,2},{7,3},{8,12},{9,13},{10,... | collective-permute-start | bytes 221192 | tf_op jit(solution)/shard_map/ppermute | solution.py:893
  475.6 3.5 copy-start.20
  475.8 25.0 %collective-permute-start.34 = (bf16[2,2,2,36,16,128]{5,4,3,1,2,0:T(8,128)(2,1)S(1)}, bf16[2,2,2,36,16,128]{5,4,3,1,2,0:T(8,128)(2,1)S(1)}, u32[]{:S(2)}, u32[]{:S(2)}) collective-permute-start(bf16[2,2,2,36,16,128]{5,4,3,1,2,0:T(8,128)(2,1)S(1)} %slice_bitcast_fusion), channel_id=1, source_target_pairs={{0,1},{1,0},{2,3},{3,2},{4,5},{5,4},{6,7},{7,6},{8,9},{9,8},{10,11... | collective-permute-start | bytes 3538952 | tf_op jit(solution)/shard_map/ppermute | solution.py:893
  481.5 29.0 %collective-permute-start.29 = (bf16[2,2,2,36,16,128]{5,4,3,0,1,2:T(8,128)(2,1)S(1)}, bf16[2,2,2,36,16,128]{5,4,3,0,1,2:T(8,128)(2,1)S(1)}, u32[]{:S(2)}, u32[]{:S(2)}) collective-permute-start(bf16[2,2,2,36,16,128]{5,4,3,0,1,2:T(8,128)(2,1)S(1)} %slice_bitcast_fusion.2), channel_id=1, source_target_pairs={{0,16},{1,17},{2,18},{3,19},{4,20},{5,21},{6,22},{7,23},{8,24},{9,... | collective-permute-start | bytes 3538952 | tf_op jit(solution)/shard_map/ppermute | solution.py:893
  481.7 30.7 %collective-permute-start.22 = (bf16[18,16,128]{2,1,0:T(8,128)(2,1)S(1)}, bf16[18,16,128]{2,1,0:T(8,128)(2,1)S(1)}, u32[]{:S(2)}, u32[]{:S(2)}) collective-permute-start(bf16[18,16,128]{2,1,0:T(8,128)(2,1)S(1)} %slice_bitcast_fusion.30), channel_id=1, source_target_pairs={{0,4},{1,5},{2,6},{3,7},{4,0},{5,1},{6,2},{7,3},{8,12},{9,13},{10,... | collective-permute-start | bytes 221192 | tf_op jit(solution)/shard_map/ppermute | solution.py:893
  501.2 16.3 %collective-permute-start.35 = (bf16[2,2,36,16,128]{4,3,2,0,1:T(8,128)(2,1)S(1)}, bf16[2,2,36,16,128]{4,3,2,0,1:T(8,128)(2,1)S(1)}, u32[]{:S(2)}, u32[]{:S(2)}) collective-permute-start(bf16[2,2,36,16,128]{4,3,2,0,1:T(8,128)(2,1)S(1)} %slice_bitcast_fusion.4), channel_id=1, source_target_pairs={{0,16},{1,17},{2,18},{3,19},{4,20},{5,21},{6,22},{7,23},{8,24},{9,... | collective-permute-start | bytes 1769480 | tf_op jit(solution)/shard_map/ppermute | solution.py:893
  510.9 9.9 %collective-permute-start.30 = (bf16[2,2,36,16,128]{4,3,2,0,1:T(8,128)(2,1)S(1)}, bf16[2,2,36,16,128]{4,3,2,0,1:T(8,128)(2,1)S(1)}, u32[]{:S(2)}, u32[]{:S(2)}) collective-permute-start(bf16[2,2,36,16,128]{4,3,2,0,1:T(8,128)(2,1)S(1)} %slice_bitcast_fusion.6), channel_id=1, source_target_pairs={{0,1},{1,0},{2,3},{3,2},{4,5},{5,4},{6,7},{7,6},{8,9},{9,8},{10,11... | collective-permute-start | bytes 1769480 | tf_op jit(solution)/shard_map/ppermute | solution.py:893
  517.6 9.6 %collective-permute-start.36 = (bf16[2,36,16,128]{3,2,1,0:T(8,128)(2,1)S(1)}, bf16[2,36,16,128]{3,2,1,0:T(8,128)(2,1)S(1)}, u32[]{:S(2)}, u32[]{:S(2)}) collective-permute-start(bf16[2,36,16,128]{3,2,1,0:T(8,128)(2,1)S(1)} %slice_bitcast_fusion.12), channel_id=1, source_target_pairs={{0,2},{1,3},{2,0},{3,1},{4,6},{5,7},{6,4},{7,5},{8,10},{9,11},{10,... | collective-permute-start | bytes 884744 | tf_op jit(solution)/shard_map/ppermute | solution.py:893
  521.1 9.6 %collective-permute-start.31 = (bf16[2,36,16,128]{3,2,1,0:T(8,128)(2,1)S(1)}, bf16[2,36,16,128]{3,2,1,0:T(8,128)(2,1)S(1)}, u32[]{:S(2)}, u32[]{:S(2)}) collective-permute-start(bf16[2,36,16,128]{3,2,1,0:T(8,128)(2,1)S(1)} %slice_bitcast_fusion.14), channel_id=1, source_target_pairs={{0,2},{1,3},{2,0},{3,1},{4,6},{5,7},{6,4},{7,5},{8,10},{9,11},{10,... | collective-permute-start | bytes 884744 | tf_op jit(solution)/shard_map/ppermute | solution.py:893
  527.4 7.7 %collective-permute-start.37 = (bf16[36,16,128]{2,1,0:T(8,128)(2,1)S(1)}, bf16[36,16,128]{2,1,0:T(8,128)(2,1)S(1)}, u32[]{:S(2)}, u32[]{:S(2)}) collective-permute-start(bf16[36,16,128]{2,1,0:T(8,128)(2,1)S(1)} %slice_bitcast_fusion.20), channel_id=1, source_target_pairs={{0,4},{1,5},{2,6},{3,7},{4,0},{5,1},{6,2},{7,3},{8,12},{9,13},{10,... | collective-permute-start | bytes 442376 | tf_op jit(solution)/shard_map/ppermute | solution.py:893
  530.8 7.7 %collective-permute-start.32 = (bf16[36,16,128]{2,1,0:T(8,128)(2,1)S(1)}, bf16[36,16,128]{2,1,0:T(8,128)(2,1)S(1)}, u32[]{:S(2)}, u32[]{:S(2)}) collective-permute-start(bf16[36,16,128]{2,1,0:T(8,128)(2,1)S(1)} %slice_bitcast_fusion.22), channel_id=1, source_target_pairs={{0,4},{1,5},{2,6},{3,7},{4,0},{5,1},{6,2},{7,3},{8,12},{9,13},{10,... | collective-permute-start | bytes 442376 | tf_op jit(solution)/shard_map/ppermute | solution.py:893
  544.6 10.8 %collective-permute-start.39 = (f32[128,128]{1,0:T(8,128)S(1)}, f32[128,128]{1,0:T(8,128)S(1)}, u32[]{:S(2)}, u32[]{:S(2)}) collective-permute-start(f32[128,128]{1,0:T(8,128)S(1)} %pad_maximum_fusion.18), channel_id=1, source_target_pairs={{1,0},{2,1},{3,2},{4,3},{5,4},{6,5},{7,6},{8,7},{9,8},{10,9},{11,1... | collective-permute-start | bytes 196616 | tf_op jit(solution)/shard_map/ppermute | solution.py:898
  546.5 8.9 %collective-permute-start.38 = (f32[72,128]{1,0:T(8,128)S(1)}, f32[72,128]{1,0:T(8,128)S(1)}, u32[]{:S(2)}, u32[]{:S(2)}) collective-permute-start(f32[72,128]{1,0:T(8,128)S(1)} %pad_maximum_fusion.20), channel_id=1, source_target_pairs={{0,1},{1,2},{2,3},{3,4},{4,5},{5,6},{6,7},{7,8},{8,9},{9,10},{10,1... | collective-permute-start | bytes 110600 | tf_op jit(solution)/shard_map/ppermute | solution.py:898
  (10 other events, 13.0 us)

commit v2 on v1

v2 whole, which is shorter than its diff:
```python
import math
from functools import partial

import jax
import jax.numpy as jnp
from jax import lax
from jax.experimental import pallas as pl
from jax.experimental.pallas import tpu as pltpu
from jax.sharding import PartitionSpec as P

FF = 3072
HEADS = 12
EPSILON = 1e-06
NEGATIVE = -1e30
AXES = ("wide", "narrow")
LANES = 128
SUB = 16
QB = 128
MEGA = 1 << 20
F32 = jnp.float32
BF16 = jnp.bfloat16

BLOCKS = 32
QKV_BLOCKS, QKV_RT, QKV_CT = 24, 2, 18
WO_BLOCKS, WO_RT, WO_CT = 8, 6, 6
W1_BLOCKS, W1_RT, W1_CT = 16, 3, 24
W2_BLOCKS, W2_RT, W2_CT = 16, 12, 6
ATT_HALF, MLP_HALF = 18, 36
ATT_SENT = ATT_HALF + 1
HALF_BLOCKS = BLOCKS // 2
CHUNK = 768
CHUNKS = FF // CHUNK

G1, C1, BQ, BV, BO, S1 = 0, 6, 12, 18, 24, 30
G2, C2, B1, B2, S2 = 36, 42, 48, 72, 78
SMALL = 88

NT = (((1,), (1,)), ((), ()))
NN = (((1,), (0,)), ((), ()))
TN = (((0,), (0,)), ((), ()))


def mm(lhs, rhs, dims):
    return lax.dot_general(lhs, rhs, dims, preferred_element_type=F32)


def row_of(ref, first, count):
    return jnp.concatenate([ref[first + k : first + k + 1, :] for k in range(count)], axis=1)


def put_row(ref, first, values):
    for k in range(values.shape[1] // LANES):
        ref[first + k : first + k + 1, :] = values[:, k * LANES : (k + 1) * LANES]


def fold8(values):
    rows, columns = values.shape
    return jnp.sum(values.reshape(rows // 8, 8, columns), axis=0)


def total(values):
    return jnp.sum(values, axis=0, keepdims=True)


def vmem():
    return pl.BlockSpec(memory_space=pltpu.VMEM)


def smem():
    return pl.BlockSpec(memory_space=pltpu.SMEM)


def anywhere():
    return pl.BlockSpec(memory_space=pl.ANY)


def shape(dims, kind):
    return jax.ShapeDtypeStruct(dims, kind)


def cost(flops, moved, exps=0):
    return pl.CostEstimate(flops=int(flops), transcendentals=int(exps), bytes_accessed=int(moved))


def normalized(values):
    center = values - jnp.mean(values, axis=-1, keepdims=True)
    inverse = lax.rsqrt(jnp.mean(center * center, axis=-1, keepdims=True) + EPSILON)
    return center * inverse, inverse


def norm_pullback(unit, inverse, grad, gain):
    scaled = grad * gain
    first = jnp.mean(scaled, axis=-1, keepdims=True)
    second = jnp.mean(scaled * unit, axis=-1, keepdims=True)
    return inverse * (scaled - first - unit * second)


def gelu_pair(z):
    magnitude = jnp.abs(z)
    t = 1.0 / (1.0 + (0.3275911 * math.sqrt(0.5)) * magnitude)
    density = jnp.exp(z * z * -0.5)
    tail = 0.5 * 1.061405429
    tail = tail * t + 0.5 * -1.453152027
    tail = tail * t + 0.5 * 1.421413741
    tail = tail * t + 0.5 * -0.284496736
    tail = tail * t + 0.5 * 0.254829592
    tail = tail * t * density
    cumulative = jnp.where(z < 0, tail, 1.0 - tail)
    return z * cumulative, cumulative + z * density * (1.0 / math.sqrt(2.0 * math.pi))


def fetch(copies):
    for copy in copies:
        copy.start()


def settle(copies):
    for copy in copies:
        copy.wait()


ATT_BEFORE, ATT_AFTER = 64, 32
MLP_BEFORE, MLP_AFTER = 64, 40


def window_offsets(me, att_rows, mlp_rows):
    att = ATT_BEFORE + 12 + me * (576 - att_rows) + jnp.where(me < QKV_BLOCKS, 0, 12)
    mlp = MLP_BEFORE + 12 + me * (1152 - mlp_rows) + jnp.where(me < W1_BLOCKS, 0, 24)
    return att, mlp


def each_tile(me, act):
    @pl.when(me < QKV_BLOCKS)
    def _():
        for ct in range(QKV_CT):
            for rt in range(QKV_RT):
                act("att", ct // 9, (ct % 9) * QKV_RT + rt, rt * SUB * QKV_CT + ct, QKV_CT)

    @pl.when(me >= QKV_BLOCKS)
    def _():
        for rt in range(WO_RT):
            for ct in range(WO_CT):
                act("att", rt // 3, (rt % 3) * WO_CT + ct, rt * SUB * WO_CT + ct, WO_CT)

    @pl.when(me < W1_BLOCKS)
    def _():
        for ct in range(W1_CT):
            for rt in range(W1_RT):
                act("mlp", ct // 12, (ct % 12) * W1_RT + rt, rt * SUB * W1_CT + ct, W1_CT)

    @pl.when(me >= W1_BLOCKS)
    def _():
        for rt in range(W2_RT):
            for ct in range(W2_CT):
                act("mlp", rt // 6, (rt % 6) * W2_CT + ct, rt * SUB * W2_CT + ct, W2_CT)


def small_rows(me, act):
    @pl.when(me == 0)
    def _():
        act("att", True, 12, G1)
        act("mlp", True, 12, G2)

    @pl.when(me == QKV_BLOCKS - 1)
    def _():
        act("att", False, 12, BQ)

    @pl.when(me == W1_BLOCKS - 1)
    def _():
        act("mlp", False, 24, B1)

    @pl.when(me == BLOCKS - 1)
    def _():
        act("att", False, 12, BO)
        act("mlp", False, 12, B2)


OWNERS = (0, W1_BLOCKS - 1, QKV_BLOCKS - 1, BLOCKS - 1)


def sent_rows(kind, first):
    return 12 if kind == "mlp" and first in (G2, B2) else 0


def pack_kernel(att_rows, me_ref, own, tails, heads, att, mlp, win_a, win_m, table):
    me = me_ref[0]
    mlp_rows = own.shape[0] - att_rows
    win_a[0:ATT_BEFORE, :] = tails[0:ATT_BEFORE, :]
    win_a[ATT_BEFORE : ATT_BEFORE + att_rows, :] = own[0:att_rows, :]
    win_a[ATT_BEFORE + att_rows :, :] = heads[0:ATT_AFTER, :]
    win_m[0:MLP_BEFORE, :] = tails[ATT_BEFORE:, :]
    win_m[MLP_BEFORE : MLP_BEFORE + mlp_rows, :] = own[att_rows:, :]
    win_m[MLP_BEFORE + mlp_rows :, :] = heads[ATT_AFTER:, :]
    att_off, mlp_off = window_offsets(me, att_rows, mlp_rows)

    def tile(kind, half, index, first, stride):
        window, out, off = (win_a, att, att_off) if kind == "att" else (win_m, mlp, mlp_off)
        out[half, index] = window[pl.ds(off + first, SUB, stride=stride), :].astype(BF16)

    each_tile(me, tile)
    table[...] = jnp.zeros_like(table)

    def vector(kind, before, rows, first):
        window, off, size = (win_a, att_off, 576) if kind == "att" else (win_m, mlp_off, 1152)
        start = off - 12 if before else off + size
        place = sent_rows(kind, first)
        table[place : place + rows, :] = window[pl.ds(start, rows), :]

    small_rows(me, vector)
    att[0, ATT_HALF] = table[0:SUB, :].astype(BF16)
    att[1, ATT_HALF] = table[SUB : 2 * SUB, :].astype(BF16)


def pack(me, own, tails, heads, att_rows):
    mlp_rows = own.shape[0] - att_rows
    return pl.pallas_call(
        partial(pack_kernel, att_rows),
        out_shape=(
            shape((2, ATT_SENT, SUB, LANES), BF16),
            shape((2, MLP_HALF, SUB, LANES), BF16),
        ),
        in_specs=[smem(), vmem(), vmem(), vmem()],
        out_specs=(vmem(), vmem()),
        scratch_shapes=[
            pltpu.VMEM((ATT_BEFORE + att_rows + ATT_AFTER, LANES), F32),
            pltpu.VMEM((MLP_BEFORE + mlp_rows + MLP_AFTER, LANES), F32),
            pltpu.VMEM((2 * SUB, LANES), F32),
        ],
        name="pack",
    )(me, own, tails, heads)


def spread_kernel(
    att_rows, scale, me_ref, att, mlp, mine, to_before, to_after, win_a, win_m, table
):
    me = me_ref[0]
    mlp_rows = mine.shape[0] - att_rows
    att_off, mlp_off = window_offsets(me, att_rows, mlp_rows)
    win_a[...] = jnp.zeros_like(win_a)
    win_m[...] = jnp.zeros_like(win_m)

    def tile(kind, half, index, first, stride):
        window, off = (win_a, att_off) if kind == "att" else (win_m, mlp_off)
        source = att if kind == "att" else mlp
        window[pl.ds(off + first, SUB, stride=stride), :] = source[half, index] * scale

    each_tile(me, tile)
    for h in range(2):
        table[SUB * h : SUB * h + SUB, :] = att[h, ATT_HALF] * scale

    def vector(kind, before, rows, first):
        window, off, size = (win_a, att_off, 576) if kind == "att" else (win_m, mlp_off, 1152)
        start = off - 12 if before else off + size
        place = sent_rows(kind, first)
        window[pl.ds(start, rows), :] = table[place : place + rows, :]

    small_rows(me, vector)
    mine[0:att_rows, :] = win_a[ATT_BEFORE : ATT_BEFORE + att_rows, :]
    mine[att_rows:, :] = win_m[MLP_BEFORE : MLP_BEFORE + mlp_rows, :]
    to_before[0:ATT_BEFORE, :] = win_a[0:ATT_BEFORE, :]
    to_before[ATT_BEFORE:, :] = win_m[0:MLP_BEFORE, :]
    to_after[0:ATT_AFTER, :] = win_a[ATT_BEFORE + att_rows :, :]
    to_after[ATT_AFTER:, :] = win_m[MLP_BEFORE + mlp_rows :, :]


def spread(me, att, mlp, att_rows, mlp_rows, scale):
    return pl.pallas_call(
        partial(spread_kernel, att_rows, scale),
        out_shape=(
            shape((att_rows + mlp_rows, LANES), F32),
            shape((ATT_BEFORE + MLP_BEFORE, LANES), F32),
            shape((ATT_AFTER + MLP_AFTER, LANES), F32),
        ),
        in_specs=[smem(), vmem(), vmem()],
        out_specs=(vmem(), vmem(), vmem()),
        scratch_shapes=[
            pltpu.VMEM((ATT_BEFORE + att_rows + ATT_AFTER, LANES), F32),
            pltpu.VMEM((MLP_BEFORE + mlp_rows + MLP_AFTER, LANES), F32),
            pltpu.VMEM((2 * SUB, LANES), F32),
        ],
        name="spread",
    )(me, att, mlp)


def close_kernel(att_rows, mine, below, above, out):
    rows = mine.shape[0]
    out[...] = mine[...]
    out[0:ATT_AFTER, :] += below[0:ATT_AFTER, :]
    out[att_rows : att_rows + MLP_AFTER, :] += below[ATT_AFTER:, :]
    out[att_rows - ATT_BEFORE : att_rows, :] += above[0:ATT_BEFORE, :]
    out[rows - MLP_BEFORE : rows, :] += above[ATT_BEFORE:, :]


def close(mine, below, above, att_rows):
    return pl.pallas_call(
        partial(close_kernel, att_rows),
        out_shape=shape(mine.shape, F32),
        in_specs=[vmem()] * 3,
        out_specs=vmem(),
        name="close",
    )(mine, below, above)


def slot_of(x, c, z, y):
    return x * 16 + c * 8 + z * 2 + y


GATHERED = [
    [
        [slot_of(i, c, z, s) if h == 0 else slot_of(s, c, z, i) for i in range(2) for z in range(4)]
        for c in range(2)
        for s in range(2)
    ]
    for h in range(2)
]
REDUCED = [
    [
        [slot_of(i, c, z, j) if h == 0 else slot_of(j, c, z, i)
         for i in range(2) for j in range(2) for z in range(4)]
        for c in range(2)
    ]
    for h in range(2)
]


def fetch_blocks(me, buffers, w, sems, first=0):
    for h in range(2):
        for k, slots in enumerate(GATHERED[h]):
            for index, slot in enumerate(slots):
                d = jnp.bitwise_xor(me, slot)

                def start(d=d, h=h, k=k, index=index):
                    source = buffers[4 * h + k].at[index]
                    pltpu.make_async_copy(source, w.at[d - first, h], sems.at[h, d]).start()

                if first:
                    pl.when(d >= first)(start)
                else:
                    start()


def wait_block(buffers, w, sems, d, h, first=0):
    pltpu.make_async_copy(buffers[0].at[0], w.at[d - first, h], sems.at[h, d]).wait()


def leaving_copies(me, buffers, w, sems):
    return [
        pltpu.make_async_copy(
            w.at[jnp.bitwise_xor(me, slot), h],
            buffers[2 * h + c].at[index],
            sems.at[h, jnp.bitwise_xor(me, slot)],
        )
        for h in range(2)
        for c in range(2)
        for index, slot in enumerate(REDUCED[h][c])
    ]


def att_scratch():
    return pltpu.VMEM((BLOCKS, 2, ATT_SENT, SUB, LANES), BF16)


def block_sems():
    return pltpu.SemaphoreType.DMA((2, BLOCKS))


def qkv_column(w, ct):
    h, place = ct // 9, ct % 9 * QKV_RT
    tiles = [w[d, h, place + rt] for d in range(QKV_BLOCKS) for rt in range(QKV_RT)]
    return jnp.concatenate(tiles, axis=0)


def wo_column(w, ct, first=QKV_BLOCKS):
    tiles = [
        w[QKV_BLOCKS - first + i, rt // 3, rt % 3 * WO_CT + ct]
        for i in range(WO_BLOCKS)
        for rt in range(WO_RT)
    ]
    return jnp.concatenate(tiles, axis=0)


def norm_rows(rows, gain, shift, source, target, step=256):
    def one(i, carry):
        at = pl.ds(pl.multiple_of(i * step, step), step)
        unit, _ = normalized(source[at, :].astype(F32))
        target[at, :] = (unit * gain + shift).astype(BF16)
        return carry

    lax.fori_loop(0, rows // step, one, 0)


def qkv_kernel(me_ref, tokens, *refs):
    buffers, (n1, qkv, small, w, sems) = refs[:8], refs[8:]
    fetch_blocks(me_ref[0], buffers, w, sems)
    for owner in OWNERS:
        for h in range(2):
            wait_block(buffers, w, sems, owner, h)
    tables = [
        jnp.concatenate([w[d, h, ATT_HALF] for h in range(2)], axis=0).astype(F32) for d in OWNERS
    ]
    small[G1 : G1 + 12, :] = tables[0][0:12]
    small[G2 : G2 + 12, :] = tables[0][12:24]
    small[B1 : B1 + 24, :] = tables[1][0:24]
    small[BQ : BQ + 12, :] = tables[2][0:12]
    small[BO : BO + 12, :] = tables[3][0:12]
    small[B2 : B2 + 12, :] = tables[3][12:24]
    small[SMALL - 4 :, :] = jnp.zeros((4, LANES), F32)
    rows = tokens.shape[0]
    norm_rows(rows, row_of(small, G1, 6), row_of(small, C1, 6), tokens, n1)
    for d in range(BLOCKS):
        for h in range(2):
            if d not in OWNERS:
                wait_block(buffers, w, sems, d, h)
    bias = jnp.concatenate(
        [row_of(small, BQ, 6), jnp.zeros((1, 768), F32), row_of(small, BV, 6)], axis=1
    )
    for c in range(QKV_CT // 2):
        weight = jnp.concatenate([qkv_column(w, 2 * c), qkv_column(w, 2 * c + 1)], axis=1)
        lanes = slice(256 * c, 256 * c + 256)
        qkv[:, lanes] = (mm(n1[...], weight, NN) + bias[:, lanes]).astype(BF16)


def project_qkv(me, tokens, att):
    rows, width = tokens.shape
    return pl.pallas_call(
        qkv_kernel,
        out_shape=(
            shape((rows, width), BF16),
            shape((rows, 3 * width), BF16),
            shape((SMALL, LANES), F32),
        ),
        in_specs=[smem(), vmem()] + [anywhere()] * 8,
        out_specs=(vmem(), vmem(), vmem()),
        scratch_shapes=[att_scratch(), block_sems()],
        compiler_params=pltpu.CompilerParams(vmem_limit_bytes=40 * MEGA),
        cost_estimate=cost(6 * rows * width * width, 12 * rows * width),
        name="qkv_forward",
    )(me, tokens, *att)


CLASSES = (128, 256, 384, 512, 768)


def head_masked(block):
    lane = lax.broadcasted_iota(jnp.int32, block.shape, 1)
    zero = jnp.zeros_like(block)
    return jnp.concatenate(
        [jnp.where(lane < 64, block, zero), jnp.where(lane >= 64, block, zero)], axis=0
    )


def pick_heads(both):
    return jnp.concatenate([both[0:64, 0:QB], both[64:128, QB : 2 * QB]], axis=0)


def lane_block(p, group):
    return pl.ds(pl.multiple_of((group * 6 + p) * LANES, LANES), LANES)


def mask_bias(start, width, b, key_ids, query_ids, bias):
    for j in range(width // QB):
        at = pl.ds(pl.multiple_of(start + j * QB, SUB), QB)
        same = key_ids[at, :] == query_ids[pl.ds(b, 1), :]
        bias[j * QB : (j + 1) * QB, :] = jnp.where(same, 0.0, NEGATIVE)


def attend_kernel(windows, qkv, key_ids, query_ids, mixed, stats, bias, scores):
    blocks = qkv.shape[0] // QB

    def one_block(b, carry):
        start = pl.multiple_of(windows[0, b], SUB)
        rows = pl.ds(pl.multiple_of(b * QB, QB), QB)
        for index, width in enumerate(CLASSES):

            @pl.when(windows[1, b] == index)
            def _(width=width):
                mask_bias(start, width, b, key_ids, query_ids, bias)
                pieces = [slice(j * QB, (j + 1) * QB) for j in range(width // QB)]

                def one_pair(p, inner):
                    queries = head_masked(qkv[rows, lane_block(p, 0)] * 0.125)
                    highest = jnp.full((8, 2 * QB), NEGATIVE, F32)
                    for piece in pieces:
                        at = pl.ds(pl.multiple_of(start + piece.start, SUB), QB)
                        part = mm(qkv[at, lane_block(p, 1)], queries, NT)
                        part = part + jnp.concatenate([bias[piece, :]] * 2, axis=1)
                        scores[piece, :] = part
                        highest = jnp.maximum(
                            highest, jnp.max(part.reshape(QB // 8, 8, 2 * QB), axis=0)
                        )
                    highest = jnp.max(highest, axis=0, keepdims=True)
                    summed = jnp.zeros((8, 2 * QB), F32)
                    both = jnp.zeros((LANES, 2 * QB), F32)
                    for piece in pieces:
                        at = pl.ds(pl.multiple_of(start + piece.start, SUB), QB)
                        raised = jnp.exp(scores[piece, :] - highest)
                        summed = summed + fold8(raised)
                        both = both + mm(qkv[at, lane_block(p, 2)], raised.astype(BF16), TN)
                    inverse = 1.0 / total(summed)
                    out = pick_heads(both * inverse)
                    mixed[rows, lane_block(p, 0)] = out.T.astype(BF16)
                    stats[b * 6 + p, 0:1, :] = highest
                    stats[b * 6 + p, 1:2, :] = inverse
                    return inner

                lax.fori_loop(0, 6, one_pair, 0, unroll=2)

        return carry

    lax.fori_loop(0, blocks, one_block, 0)


def attend(windows, qkv, key_ids, query_ids):
    rows = qkv.shape[0]
    width = qkv.shape[1] // 3
    return pl.pallas_call(
        attend_kernel,
        out_shape=(shape((rows, width), BF16), shape((rows // QB * 6, 2, 2 * QB), F32)),
        in_specs=[smem(), vmem(), vmem(), vmem()],
        out_specs=(vmem(), vmem()),
        scratch_shapes=[
            pltpu.VMEM((CLASSES[-1], QB), F32),
            pltpu.VMEM((CLASSES[-1], 2 * QB), F32),
        ],
        compiler_params=pltpu.CompilerParams(vmem_limit_bytes=40 * MEGA),
        cost_estimate=cost(2 * rows * rows * width, 8 * rows * width, 4 * rows * rows),
        name="attend_forward",
    )(windows, qkv, key_ids, query_ids)


def wo_scratch():
    return pltpu.VMEM((WO_BLOCKS, 2, ATT_SENT, SUB, LANES), BF16)


def wait_wo(buffers, w, sems):
    for i in range(WO_BLOCKS):
        for h in range(2):
            wait_block(buffers, w, sems, QKV_BLOCKS + i, h, QKV_BLOCKS)


def join_kernel(me_ref, tokens, mixed, small, *refs):
    buffers, (x1, branch, n2, w, sems) = refs[:8], refs[8:]
    fetch_blocks(me_ref[0], buffers, w, sems, QKV_BLOCKS)
    rows = tokens.shape[0]
    bias, scale = row_of(small, BO, 6), row_of(small, S1, 6)
    gain, shift = row_of(small, G2, 6), row_of(small, C2, 6)
    wait_wo(buffers, w, sems)
    for c in range(3):
        weight = jnp.concatenate([wo_column(w, 2 * c), wo_column(w, 2 * c + 1)], axis=1)
        lanes = slice(256 * c, 256 * c + 256)
        branch[:, lanes] = mm(mixed[...], weight, NN) + bias[:, lanes]
    step = 128

    def one(i, carry):
        at = pl.ds(pl.multiple_of(i * step, step), step)
        values = tokens[at, :].astype(F32) + scale * branch[at, :]
        x1[at, :] = values
        unit, _ = normalized(values)
        n2[at, :] = (unit * gain + shift).astype(BF16)
        return carry

    lax.fori_loop(0, rows // step, one, 0)


def join(me, tokens, mixed, small, att):
    rows, width = tokens.shape
    return pl.pallas_call(
        join_kernel,
        out_shape=(
            shape((rows, width), F32),
            shape((rows, width), F32),
            shape((rows, width), BF16),
        ),
        in_specs=[smem(), vmem(), vmem(), vmem()] + [anywhere()] * 8,
        out_specs=(vmem(), vmem(), vmem()),
        scratch_shapes=[
            wo_scratch(),
            block_sems(),
        ],
        compiler_params=pltpu.CompilerParams(vmem_limit_bytes=40 * MEGA),
        cost_estimate=cost(2 * rows * width * width, 14 * rows * width),
        name="project_and_norm",
    )(me, tokens, mixed, small, *att)


def w1_columns(w, f, c):
    columns = []
    for ct in (2 * c, 2 * c + 1):
        place = MLP_HALF // 2 * (f % 2) + ct * W1_RT
        tiles = [w[d, f // 2, place + rt] for d in range(W1_BLOCKS) for rt in range(W1_RT)]
        columns.append(jnp.concatenate(tiles, axis=0))
    return jnp.concatenate(columns, axis=1)


def w2_place(f, row, ct):
    rt = row % W2_RT
    return W1_BLOCKS + 4 * f + row // W2_RT, rt // 6, rt % 6 * W2_CT + ct


def w2_rows(w, f, c):
    columns = []
    for ct in range(W2_CT):
        tiles = [w[w2_place(f, row, ct)] for row in range(SUB * c, SUB * c + SUB)]
        columns.append(jnp.concatenate(tiles, axis=0))
    return jnp.concatenate(columns, axis=1)


TALL = 256
PARTS = CHUNK // 256


def mlp_kernel(me_ref, n2, cot, x1, small, *refs):
    arriving, refs = refs[:8], refs[8:]
    out, dx1, vectors, *leaving = refs[:7]
    w, macc, dnacc, dm, u, dz, zs, dus, bias_sums, b1_lines, sums, sems = refs[7:]
    me = me_ref[0]
    rows, width = n2.shape
    tiles = rows // TALL
    fetch_blocks(me, arriving, w, sems)
    scale = row_of(small, S2, 6)
    step = 128

    def prepare(i, carry):
        at = pl.ds(pl.multiple_of(i * step, step), step)
        rounded = (cot[at, :].astype(F32) * scale).astype(BF16)
        dm[at, :] = rounded
        return carry + fold8(rounded.astype(F32))

    zero = jnp.zeros((8, width), F32)
    gb2 = lax.fori_loop(0, rows // step, prepare, zero)
    bias_sums[...] = jnp.zeros_like(bias_sums)

    units = [(t, c) for c in range(PARTS) for t in range(tiles)]

    def lanes_of(f, c):
        return pl.ds(pl.multiple_of(CHUNK * f + 256 * c, 256), 256)

    def one_chunk(f, carry):
        @pl.when((f & 1) == 0)
        def _():
            for d in range(W1_BLOCKS):
                wait_block(arriving, w, sems, d, f >> 1)

        for k in range(4):
            for h in range(2):
                wait_block(arriving, w, sems, W1_BLOCKS + 4 * f + k, h)

        def multiply(unit, slot):
            t, c = unit
            at = slice(TALL * t, TALL * t + TALL)
            zs[slot] = mm(n2[at, :], w1_columns(w, f, c), NN)
            dus[slot] = mm(dm[at, :], w2_rows(w, f, c), NT)

        def activate(unit, slot):
            t, c = unit
            lanes = lanes_of(f, c)
            bias = b1_lines[pl.ds(f, 1), 256 * c : 256 * c + 256]
            folded = jnp.zeros((8, 256), F32)
            for r in range(TALL // 32):
                part = slice(32 * r, 32 * r + 32)
                place = slice(TALL * t + 32 * r, TALL * t + 32 * r + 32)
                value, slope = gelu_pair(zs[slot, part, :] + bias)
                u[place, lanes] = value.astype(BF16)
                rounded = (dus[slot, part, :] * slope).astype(BF16)
                dz[place, lanes] = rounded
                folded = folded + fold8(rounded.astype(F32))
            bias_sums[:, lanes] += folded

        multiply(units[0], 0)
        for i, unit in enumerate(units):
            if i + 1 < len(units):
                multiply(units[i + 1], (i + 1) % 2)
            activate(unit, i % 2)
        return carry

    for f in range(CHUNKS):
        b1_lines[f : f + 1, :] = row_of(small, B1 + 6 * f, 6)
    lax.fori_loop(0, CHUNKS, one_chunk, 0)

    bias, gain = row_of(small, B2, 6), row_of(small, G2, 6)
    sums[...] = jnp.zeros_like(sums)

    def finish(t):
        for half in range(TALL // step):
            at = pl.ds(pl.multiple_of(TALL * t + step * half, step), step)
            upstream = cot[at, :].astype(F32)
            values = x1[at, :]
            contracted = macc[at, :] + bias
            out[at, :] = (values + scale * contracted).astype(BF16)
            unit, inverse = normalized(values)
            grad = dnacc[at, :]
            dx1[at, :] = upstream + norm_pullback(unit, inverse, grad, gain)
            sums[0:8, :] += fold8(grad * unit)
            sums[8:16, :] += fold8(grad)
            sums[16:24, :] += fold8(upstream * contracted)

    every = [(f, c) for f in range(CHUNKS) for c in range(PARTS)]

    def contract(t):
        at = pl.ds(pl.multiple_of(TALL * t, TALL), TALL)
        second = jnp.concatenate([w2_rows(w, f, c) for f, c in every], axis=0)
        first = jnp.concatenate([w1_columns(w, f, c) for f, c in every], axis=1)
        macc[at, :] = mm(u[at, :], second, NN)
        dnacc[at, :] = mm(dz[at, :], first, NT)

    def one_tile(t, carry):
        contract(t)
        finish(t - 1)
        return carry

    contract(0)
    lax.fori_loop(1, tiles, one_tile, 0)
    finish(tiles - 1)

    def one_grad(f, carry):
        for c in range(PARTS):
            grad = mm(u[:, lanes_of(f, c)], dm[...], TN)
            for r in range(SUB):
                for ct in range(W2_CT):
                    tile = grad[SUB * r : SUB * r + SUB, LANES * ct : LANES * ct + LANES]
                    w[w2_place(f, SUB * c + r, ct)] = tile.astype(BF16)
        chunk = pl.ds(pl.multiple_of(CHUNK * f, CHUNK), CHUNK)
        base = MLP_HALF // 2 * (f & 1)
        for c in range(PARTS):
            lanes = slice(256 * c, 256 * c + 256)
            grad = mm(n2[:, lanes], dz[:, chunk], TN)
            for r in range(SUB):
                d, rt = (SUB * c + r) // W1_RT, (SUB * c + r) % W1_RT
                for ct in range(6):
                    tile = grad[SUB * r : SUB * r + SUB, LANES * ct : LANES * ct + LANES]
                    w[d, f >> 1, base + ct * W1_RT + rt] = tile.astype(BF16)
        return carry

    lax.fori_loop(0, CHUNKS, one_grad, 0)
    copies = leaving_copies(me, leaving, w, sems)
    fetch(copies)
    put_row(vectors, G2 - G2, total(sums[0:8, :]))
    put_row(vectors, C2 - G2, total(sums[8:16, :]))
    put_row(vectors, B1 - G2, total(bias_sums[...]))
    put_row(vectors, B2 - G2, total(gb2))
    put_row(vectors, S2 - G2, total(sums[16:24, :]))
    settle(copies)


def feed_forward(me, n2, cot, x1, small, mlp):
    rows, width = n2.shape
    half = shape((HALF_BLOCKS, MLP_HALF, SUB, LANES), BF16)
    return pl.pallas_call(
        mlp_kernel,
        out_shape=(
            shape((rows, width), BF16),
            shape((rows, width), F32),
            shape((48, LANES), F32),
            half,
            half,
            half,
            half,
        ),
        in_specs=[smem(), vmem(), vmem(), vmem(), vmem()] + [anywhere()] * 8,
        out_specs=(vmem(), vmem(), vmem()) + (anywhere(),) * 4,
        scratch_shapes=[
            pltpu.VMEM((BLOCKS, 2, MLP_HALF, SUB, LANES), BF16),
            pltpu.VMEM((rows, width), F32),
            pltpu.VMEM((rows, width), F32),
            pltpu.VMEM((rows, width), BF16),
            pltpu.VMEM((rows, FF), BF16),
            pltpu.VMEM((rows, FF), BF16),
            pltpu.VMEM((2, TALL, 256), F32),
            pltpu.VMEM((2, TALL, 256), F32),
            pltpu.VMEM((8, FF), F32),
            pltpu.VMEM((CHUNKS, CHUNK), F32),
            pltpu.VMEM((24, width), F32),
            block_sems(),
        ],
        compiler_params=pltpu.CompilerParams(vmem_limit_bytes=58 * MEGA),
        cost_estimate=cost(12 * rows * width * FF, 40 * MEGA),
        name="feed_forward",
    )(me, n2, cot, x1, small, *mlp)


def split_kernel(me_ref, dx1, branch, mixed, small, *refs):
    buffers, (da, vectors, gwo, w, db, sems) = refs[:8], refs[8:]
    fetch_blocks(me_ref[0], buffers, w, sems, QKV_BLOCKS)
    rows = dx1.shape[0]
    scale = row_of(small, S1, 6)
    step = 128

    def one(i, carry):
        gs1, gbo = carry
        at = pl.ds(pl.multiple_of(i * step, step), step)
        grad = dx1[at, :]
        rounded = (grad * scale).astype(BF16)
        db[at, :] = rounded
        return gs1 + fold8(grad * branch[at, :]), gbo + fold8(rounded.astype(F32))

    zero = jnp.zeros((8, 768), F32)
    gs1, gbo = lax.fori_loop(0, rows // step, one, (zero, zero))
    put_row(vectors, 0, total(gbo))
    put_row(vectors, 6, total(gs1))
    wait_wo(buffers, w, sems)
    weight = jnp.concatenate([wo_column(w, ct) for ct in range(WO_CT)], axis=1)
    for c in range(3):
        lanes = slice(256 * c, 256 * c + 256)
        da[:, lanes] = mm(db[...], weight[lanes, :], NT).astype(BF16)
    for c in range(3):
        grad = mm(mixed[:, 256 * c : 256 * c + 256], db[...], TN)
        for r in range(SUB):
            tile_row = SUB * c + r
            i, rt = tile_row // WO_RT, tile_row % WO_RT
            for ct in range(WO_CT):
                tile = grad[SUB * r : SUB * r + SUB, LANES * ct : LANES * ct + LANES]
                gwo[i, rt // 3, rt % 3 * WO_CT + ct] = tile.astype(BF16)


def split(me, dx1, branch, mixed, small, att):
    rows, width = dx1.shape
    return pl.pallas_call(
        split_kernel,
        out_shape=(
            shape((rows, width), BF16),
            shape((12, LANES), F32),
            shape((WO_BLOCKS, 2, ATT_HALF, SUB, LANES), BF16),
        ),
        in_specs=[smem(), vmem(), vmem(), vmem(), vmem()] + [anywhere()] * 8,
        out_specs=(vmem(), vmem(), vmem()),
        scratch_shapes=[wo_scratch(), pltpu.VMEM((rows, width), BF16), block_sems()],
        compiler_params=pltpu.CompilerParams(vmem_limit_bytes=40 * MEGA),
        cost_estimate=cost(4 * rows * width * width, 14 * rows * width),
        name="project_backward",
    )(me, dx1, branch, mixed, small, *att)


def attend_back_kernel(
    windows, qkv, da, stats, key_ids, query_ids, dqkv, bias, probs, dprobs, dkeys, dvalues
):
    blocks = qkv.shape[0] // QB

    def clear(b, carry):
        rows = pl.ds(pl.multiple_of(b * QB, QB), QB)
        dkeys[rows, :] = jnp.zeros((QB, dkeys.shape[1]), F32)
        dvalues[rows, :] = jnp.zeros((QB, dkeys.shape[1]), F32)
        return carry

    lax.fori_loop(0, blocks, clear, 0)

    def one_block(b, carry):
        start = pl.multiple_of(windows[0, b], SUB)
        rows = pl.ds(pl.multiple_of(b * QB, QB), QB)
        for index, width in enumerate(CLASSES):

            @pl.when(windows[1, b] == index)
            def _(width=width):
                mask_bias(start, width, b, key_ids, query_ids, bias)
                pieces = [slice(j * QB, (j + 1) * QB) for j in range(width // QB)]

                def one_pair(p, inner):
                    queries = head_masked(qkv[rows, lane_block(p, 0)] * 0.125)
                    grads = head_masked(da[rows, lane_block(p, 0)])
                    highest = stats[b * 6 + p, 0:1, :]
                    inverse = stats[b * 6 + p, 1:2, :]
                    inner_sum = jnp.zeros((8, 2 * QB), F32)
                    for piece in pieces:
                        at = pl.ds(pl.multiple_of(start + piece.start, SUB), QB)
                        part = mm(qkv[at, lane_block(p, 1)], queries, NT)
                        part = part + jnp.concatenate([bias[piece, :]] * 2, axis=1)
                        weight = jnp.exp(part - highest) * inverse
                        dweight = mm(qkv[at, lane_block(p, 2)], grads, NT)
                        inner_sum = inner_sum + fold8(weight * dweight)
                        probs[piece, :] = weight
                        dprobs[piece, :] = dweight
                        dvalues[at, lane_block(p, 0)] += mm(weight.astype(BF16), grads, NN)
                    inner_sum = total(inner_sum)
                    both = jnp.zeros((LANES, 2 * QB), F32)
                    for piece in pieces:
                        at = pl.ds(pl.multiple_of(start + piece.start, SUB), QB)
                        dscore = probs[piece, :] * (dprobs[piece, :] - inner_sum)
                        dscore = dscore.astype(BF16)
                        dkeys[at, lane_block(p, 0)] += mm(dscore, queries, NN)
                        both = both + mm(qkv[at, lane_block(p, 1)], dscore, TN)
                    out = pick_heads(both) * 0.125
                    dqkv[rows, lane_block(p, 0)] = out.T.astype(BF16)
                    return inner

                lax.fori_loop(0, 6, one_pair, 0, unroll=2)

        return carry

    lax.fori_loop(0, blocks, one_block, 0)
    width = dkeys.shape[1]

    def store(b, carry):
        rows = pl.ds(pl.multiple_of(b * 32, 32), 32)
        dqkv[rows, width : 2 * width] = dkeys[rows, :].astype(BF16)
        dqkv[rows, 2 * width :] = dvalues[rows, :].astype(BF16)
        return carry

    lax.fori_loop(0, qkv.shape[0] // 32, store, 0)


def attend_back(windows, qkv, da, stats, key_ids, query_ids):
    rows, triple = qkv.shape
    width = triple // 3
    return pl.pallas_call(
        attend_back_kernel,
        out_shape=shape((rows, triple), BF16),
        in_specs=[smem()] + [vmem()] * 5,
        out_specs=vmem(),
        scratch_shapes=[
            pltpu.VMEM((CLASSES[-1], QB), F32),
            pltpu.VMEM((CLASSES[-1], 2 * QB), F32),
            pltpu.VMEM((CLASSES[-1], 2 * QB), F32),
            pltpu.VMEM((rows, width), F32),
            pltpu.VMEM((rows, width), F32),
        ],
        compiler_params=pltpu.CompilerParams(vmem_limit_bytes=48 * MEGA),
        cost_estimate=cost(6 * rows * rows * width, 14 * rows * width, 4 * rows * rows),
        name="attend_backward",
    )(windows, qkv, da, stats, key_ids, query_ids)


def qkv_back_kernel(me_ref, tokens, n1, dx1, dqkv, small, proj, mlp, gwo, *refs):
    arriving, refs = refs[:8], refs[8:]
    dx, *leaving = refs[:5]
    w, dn, sums, table, sems = refs[5:]
    me = me_ref[0]
    fetch_blocks(me, arriving, w, sems)
    rows = tokens.shape[0]
    zero = jnp.zeros((8, 768), F32)

    def column_sums(i, carry):
        at = pl.ds(pl.multiple_of(i * 128, 128), 128)
        return (
            carry[0] + fold8(dqkv[at, 0:768].astype(F32)),
            carry[1] + fold8(dqkv[at, 1536:2304].astype(F32)),
        )

    gbq, gbv = lax.fori_loop(0, rows // 128, column_sums, (zero, zero))
    sums[...] = jnp.zeros_like(sums)
    gain = row_of(small, G1, 6)
    for d in range(BLOCKS):
        for h in range(2):
            wait_block(arriving, w, sems, d, h)

    def contract(t):
        at = pl.ds(pl.multiple_of(TALL * t, TALL), TALL)
        weight = jnp.concatenate([qkv_column(w, ct) for ct in range(QKV_CT)], axis=1)
        dn[at, :] = mm(dqkv[at, :], weight, NT)

    def finish(t):
        for half in range(TALL // 128):
            at = pl.ds(pl.multiple_of(TALL * t + 128 * half, 128), 128)
            unit, inverse = normalized(tokens[at, :].astype(F32))
            grad = dn[at, :]
            dx[at, :] = dx1[at, :] + norm_pullback(unit, inverse, grad, gain)
            sums[0:8, :] += fold8(grad * unit)
            sums[8:16, :] += fold8(grad)

    def one_tile(t, carry):
        contract(t)
        finish(t - 1)
        return carry

    contract(0)
    lax.fori_loop(1, rows // TALL, one_tile, 0)
    finish(rows // TALL - 1)

    def put_table(owner, *places):
        table[...] = jnp.zeros_like(table)
        for place, values in places:
            if values.shape[1] == LANES:
                table[place : place + values.shape[0], :] = values
            else:
                put_row(table, place, values)
        for h in range(2):
            w[owner, h, ATT_HALF] = table[SUB * h : SUB * h + SUB, :].astype(BF16)

    put_table(
        OWNERS[0], (0, total(sums[0:8, :])), (6, total(sums[8:16, :])), (12, mlp[0:12, :])
    )
    put_table(OWNERS[1], (0, mlp[B1 - G2 : B1 - G2 + 24, :]))
    put_table(OWNERS[2], (0, total(gbq)), (6, total(gbv)))
    put_table(OWNERS[3], (0, proj[...]), (12, mlp[B2 - G2 : B2 - G2 + 12, :]))
    for i in range(WO_BLOCKS):
        for h in range(2):
            w[QKV_BLOCKS + i, h, 0:ATT_HALF] = gwo[i, h]
    for c in range(3):
        for half in range(2):
            columns = slice(1152 * half, 1152 * half + 1152)
            grad = mm(n1[:, 256 * c : 256 * c + 256], dqkv[:, columns], TN)
            for r in range(SUB):
                d, rt = (SUB * c + r) // QKV_RT, (SUB * c + r) % QKV_RT
                for ct in range(9):
                    tile = grad[SUB * r : SUB * r + SUB, LANES * ct : LANES * ct + LANES]
                    w[d, half, ct * QKV_RT + rt] = tile.astype(BF16)
    copies = leaving_copies(me, leaving, w, sems)
    fetch(copies)
    settle(copies)


def qkv_back(me, tokens, n1, dx1, dqkv, small, proj, mlp, gwo, att):
    rows, width = tokens.shape
    half = shape((HALF_BLOCKS, ATT_SENT, SUB, LANES), BF16)
    return pl.pallas_call(
        qkv_back_kernel,
        out_shape=(shape((rows, width), F32), half, half, half, half),
        in_specs=[smem()] + [vmem()] * 8 + [anywhere()] * 8,
        out_specs=(vmem(),) + (anywhere(),) * 4,
        scratch_shapes=[
            att_scratch(),
            pltpu.VMEM((rows, width), F32),
            pltpu.VMEM((16, width), F32),
            pltpu.VMEM((2 * SUB, LANES), F32),
            block_sems(),
        ],
        compiler_params=pltpu.CompilerParams(vmem_limit_bytes=48 * MEGA),
        cost_estimate=cost(12 * rows * width * width, 30 * rows * width),
        name="qkv_backward",
    )(me, tokens, n1, dx1, dqkv, small, proj, mlp, gwo, *att)


X, C, Z1, Z0, Y = 16, 8, 4, 2, 1


def exchange(values, bit):
    return lax.ppermute(values, AXES, [(d, d ^ bit) for d in range(BLOCKS)])


def shifted(values, by):
    pairs = [(d, d + by) for d in range(BLOCKS) if 0 <= d + by < BLOCKS]
    return lax.ppermute(values, AXES, pairs)


def together(*values):
    return lax.optimization_barrier(values)


def along_z(first, second, received):
    return (
        jnp.stack([first] + [r[0] for r in received]),
        jnp.stack([second] + [r[1] for r in received]),
    )


def joined(own, received):
    return jnp.concatenate([own, received])


def sum_terms(terms):
    summed = terms[0].astype(F32)
    for term in terms[1:]:
        summed = summed + term.astype(F32)
    return summed


def kept(terms):
    return [t[: t.shape[0] // 2] for t in terms]


def sent(terms):
    return sum_terms([t[t.shape[0] // 2 :] for t in terms]).astype(BF16)


def attention_amounts(width):
    return [width, width, 3 * width * width, width, width, width * width, width, width]


def feedforward_amounts(width):
    return [width, width, width * FF, FF, FF * width, width, width]


def pieces_of(vector, amounts):
    out, offset = [], 0
    for amount in amounts:
        out.append(vector[offset : offset + amount])
        offset += amount
    return out


def tiles_by_column(matrix, blocks, rt):
    ct = matrix.shape[1] // LANES
    return matrix.reshape(blocks, rt, SUB, ct, LANES).transpose(0, 3, 1, 2, 4)


def tiles_by_row(matrix, blocks, rt):
    ct = matrix.shape[1] // LANES
    return matrix.reshape(blocks, rt, SUB, ct, LANES).transpose(0, 1, 3, 2, 4)


def gather_plainly(params, att_rows, width):
    rounded = params.astype(BF16)
    att = lax.all_gather(rounded[:att_rows], AXES, axis=0, tiled=True).reshape(-1)
    mlp = lax.all_gather(rounded[att_rows:], AXES, axis=0, tiled=True).reshape(-1)
    g1, c1, wqkv, bq, bv, wo, bo, s1 = pieces_of(att, attention_amounts(width))
    g2, c2, w1, b1, w2, b2, s2 = pieces_of(mlp, feedforward_amounts(width))
    tile = (SUB, LANES)
    att = jnp.concatenate(
        [
            tiles_by_column(wqkv.reshape(width, -1), QKV_BLOCKS, QKV_RT).reshape((-1, 36) + tile),
            tiles_by_row(wo.reshape(width, -1), WO_BLOCKS, WO_RT).reshape((-1, 36) + tile),
        ]
    )
    mlp = jnp.concatenate(
        [
            tiles_by_column(w1.reshape(width, -1), W1_BLOCKS, W1_RT).reshape((-1, 72) + tile),
            tiles_by_row(w2.reshape(FF, -1), W2_BLOCKS, W2_RT).reshape((-1, 72) + tile),
        ]
    )
    vectors = jnp.concatenate([g1, c1, bq, bv, bo, s1, g2, c2, b1, b2, s2]).astype(F32)
    lines = vectors.reshape(-1, LANES)
    sent = jnp.zeros((BLOCKS, 2 * SUB, LANES), F32)
    for owner, place, first, count in (
        (OWNERS[0], 0, G1, 12),
        (OWNERS[0], 12, G2, 12),
        (OWNERS[1], 0, B1, 24),
        (OWNERS[2], 0, BQ, 12),
        (OWNERS[3], 0, BO, 12),
        (OWNERS[3], 12, B2, 12),
    ):
        sent = sent.at[owner, place : place + count].set(lines[first : first + count])
    sent = sent.astype(BF16).reshape((BLOCKS, 2, 1) + tile)
    att = [jnp.concatenate([att[:, 18 * h : 18 * h + 18], sent[:, h]], axis=1) for h in range(2)]
    return by_slot(*att), by_slot(mlp[:, :36], mlp[:, 36:])


def by_slot(first, second):
    halves = (first, second)
    return [
        jnp.stack([halves[h][slot] for slot in slots]) for h in range(2) for slots in GATHERED[h]
    ]


def from_slots(buffers):
    halves = []
    for h in range(2):
        blocks = [None] * BLOCKS
        for c in range(2):
            for index, slot in enumerate(REDUCED[h][c]):
                blocks[slot] = buffers[2 * h + c][index]
        halves.append(jnp.stack(blocks))
    return halves


def reduce_plainly(gatt, gmlp, att_rows, mlp_rows, width, devices):
    first, second = from_slots(gatt)
    vectors = jnp.concatenate([first[:, ATT_HALF:], second[:, ATT_HALF:]], axis=1).astype(F32)
    vectors = vectors.reshape(BLOCKS, 2 * SUB, LANES)
    att = jnp.concatenate([first[:, :ATT_HALF], second[:, :ATT_HALF]], axis=1).astype(F32)
    mlp = jnp.concatenate(from_slots(gmlp), axis=1).astype(F32)
    five = lambda v, dims: v.reshape((v.shape[0],) + dims + (SUB, LANES))
    wqkv = five(att[:QKV_BLOCKS], (QKV_CT, QKV_RT)).transpose(0, 2, 3, 1, 4).reshape(-1)
    wo = five(att[QKV_BLOCKS:], (WO_RT, WO_CT)).transpose(0, 1, 3, 2, 4).reshape(-1)
    w1 = five(mlp[:W1_BLOCKS], (W1_CT, W1_RT)).transpose(0, 2, 3, 1, 4).reshape(-1)
    w2 = five(mlp[W1_BLOCKS:], (W2_RT, W2_CT)).transpose(0, 1, 3, 2, 4).reshape(-1)
    line = lambda owner, first, count: vectors[owner, first : first + count].reshape(-1)
    att = [line(OWNERS[0], 0, 12), wqkv, line(OWNERS[2], 0, 12), wo, line(OWNERS[3], 0, 12)]
    mlp = [line(OWNERS[0], 12, 12), w1, line(OWNERS[1], 0, 24), w2, line(OWNERS[3], 12, 12)]

    def lay(parts, rows):
        vector = jnp.concatenate(parts)
        vector = jnp.pad(vector, (0, devices * rows * LANES - vector.shape[0]))
        return vector.reshape(devices, rows, LANES)

    whole = jnp.concatenate([lay(att, att_rows), lay(mlp, mlp_rows)], axis=1)
    return lax.psum_scatter(whole.reshape(-1, LANES), AXES, scatter_dimension=0, tiled=True)


def key_windows(segments, real):
    length = segments.shape[0]
    position = jnp.arange(length, dtype=jnp.int32)
    ids = jnp.where(real, segments, length + position)
    first = segments[0::QB]
    final = segments[QB - 1 :: QB]
    begin = jnp.sum((segments[None, :] < first[:, None]).astype(jnp.int32), axis=1)
    begin = jnp.where(real[0::QB], begin, position[0::QB])
    end = jnp.sum(((segments[None, :] <= final[:, None]) & real[None, :]).astype(jnp.int32), axis=1)
    end = jnp.where(real[QB - 1 :: QB], end, position[QB - 1 :: QB] + 1)
    begin = begin // SUB * SUB
    need = end - begin
    kind = sum((need > width).astype(jnp.int32) for width in CLASSES[:-1])
    widths = sum(
        jnp.where(kind == i, width, 0) for i, width in enumerate(CLASSES)
    )
    begin = jnp.minimum(begin, length - widths)
    return ids, jnp.stack([begin, kind]).astype(jnp.int32)


def local(tokens, cotangent, segment_ids, pad_mask, lengths, params):
    rows, width = tokens.shape
    wide, narrow = lax.axis_size("wide"), lax.axis_size("narrow")
    devices = wide * narrow
    att_count = 4 * width * width + 6 * width
    att_rows = (att_count // LANES + devices - 1) // devices
    mlp_rows = params.shape[0] - att_rows
    paired = (wide, narrow) == (4, 8)
    scale = 1.0 / math.sqrt(rows * devices)

    position = jnp.arange(rows, dtype=jnp.int32)
    real = (pad_mask > 0) & (position < lengths[0])
    ids, windows = key_windows(segment_ids, real)
    key_ids = ids.reshape(rows, 1)
    query_ids = ids.reshape(rows // QB, QB)

    if not paired:
        me = jnp.zeros((1,), jnp.int32)
        att, mlp = gather_plainly(params, att_rows, width)
        n1, qkv, small = project_qkv(me, tokens, att)
        mixed, stats = attend(windows, qkv, key_ids, query_ids)
        x1, branch, n2 = join(me, tokens, mixed, small, att)
        output, dx1, small_mlp, *gmlp = feed_forward(me, n2, cotangent, x1, small, mlp)
        da, small_proj, gwo = split(me, dx1, branch, mixed, small, att)
        dqkv = attend_back(windows, qkv, da, stats, key_ids, query_ids)
        grad_input, *gatt = qkv_back(
            me, tokens, n1, dx1, dqkv, small, small_proj, small_mlp, gwo, att
        )
        owned = reduce_plainly(gatt, gmlp, att_rows, mlp_rows, width, devices)
        return output, grad_input, owned * scale

    me = lax.axis_index(AXES).astype(jnp.int32).reshape(1)
    tails = jnp.concatenate([params[att_rows - ATT_BEFORE : att_rows], params[-MLP_BEFORE:]])
    heads = jnp.concatenate([params[:ATT_AFTER], params[att_rows : att_rows + MLP_AFTER]])
    tails, heads = shifted(tails, 1), shifted(heads, -1)
    att_own, mlp_own = pack(me, params, tails, heads, att_rows)

    got = [exchange(att_own, k * Z0) for k in range(1, 4)]
    a, b = along_z(att_own[0], att_own[1], got)
    a, b, mlp_own = together(a, b, mlp_own)
    ax, by = exchange(a, X), exchange(b, Y)
    z1, z3 = exchange(mlp_own, Z0), exchange(mlp_own, 3 * Z0)
    a, b = joined(a, ax), joined(b, by)
    a, b, z1, z3, mlp_own = together(a, b, z1, z3, mlp_own)
    ay, bx = exchange(a, Y), exchange(b, X)
    ac, bc = exchange(a, C), exchange(b, C)
    z2 = exchange(mlp_own, 2 * Z0)
    m, n = along_z(mlp_own[0], mlp_own[1], [z1, z2, z3])
    ay, bx, ac, bc, m, n = together(ay, bx, ac, bc, m, n)
    ayc, bxc = exchange(ay, C), exchange(bx, C)
    att = together(a, ay, ac, ayc, b, bx, bc, bxc, m, n, tokens)
    *att, m, n, tokens_now = att
    mx, ny = exchange(m, X), exchange(n, Y)
    n1, qkv, small = project_qkv(me, tokens_now, att)
    m, n = joined(m, mx), joined(n, ny)
    m, n, qkv = together(m, n, qkv)
    my, nx = exchange(m, Y), exchange(n, X)
    mc, nc = exchange(m, C), exchange(n, C)
    mixed, stats = attend(windows, qkv, key_ids, query_ids)
    x1, branch, n2 = join(me, tokens, mixed, small, att)
    m, n, my, nx, mc, nc, n2 = together(m, n, my, nx, mc, nc, n2)
    myc, nxc = exchange(my, C), exchange(nx, C)
    mlp = (m, my, mc, myc, n, nx, nc, nxc)

    output, dx1, small_mlp, *gmlp = feed_forward(me, n2, cotangent, x1, small, mlp)

    mc, nc = exchange(gmlp[1], C), exchange(gmlp[3], C)
    da, small_proj, gwo = split(me, dx1, branch, mixed, small, att)
    mc, nc, da = together(mc, nc, da)
    m, n = [gmlp[0], mc], [gmlp[2], nc]
    mx, ny, da = together(sent(m), sent(n), da)
    mx, ny = exchange(mx, X), exchange(ny, Y)
    dqkv = attend_back(windows, qkv, da, stats, key_ids, query_ids)
    mx, ny, dqkv = together(mx, ny, dqkv)
    m, n = kept(m) + [mx], kept(n) + [ny]
    my, nx, dqkv = together(sent(m), sent(n), dqkv)
    my, nx = exchange(my, Y), exchange(nx, X)
    grad_input, *gatt = qkv_back(
        me, tokens, n1, dx1, dqkv, small, small_proj, small_mlp, gwo, att
    )
    my, nx, *gatt = together(my, nx, *gatt)
    m, n = sum_terms(kept(m) + [my]), sum_terms(kept(n) + [nx])
    m_sums = jnp.stack([m, n], axis=1)
    z1, z2, z3 = [m_sums[k].astype(BF16) for k in range(1, 4)]
    z1, z2, z3, *gatt = together(z1, z2, z3, *gatt)
    ac, bc = exchange(gatt[1], C), exchange(gatt[3], C)
    z1 = exchange(z1, Z0)
    a, b = [gatt[0], ac], [gatt[2], bc]
    ax, by, z1, z2, z3 = together(sent(a), sent(b), z1, z2, z3)
    ax, by = exchange(ax, X), exchange(by, Y)
    z2 = exchange(z2, 2 * Z0)
    a, b = kept(a) + [ax], kept(b) + [by]
    ay, bx, z2, z3 = together(sent(a), sent(b), z2, z3)
    ay, bx = exchange(ay, Y), exchange(bx, X)
    z3 = exchange(z3, 3 * Z0)
    a, b = sum_terms(kept(a) + [ay]), sum_terms(kept(b) + [bx])
    a_sums = jnp.stack([a, b], axis=1)
    m_own = sum_terms([m_sums[0], z1, z2, z3])
    s1, s2, s3 = [a_sums[k].astype(BF16) for k in range(1, 4)]
    s1, s2, s3, m_own = together(s1, s2, s3, m_own)
    got = [exchange(s1, Z0), exchange(s2, 2 * Z0), exchange(s3, 3 * Z0)]
    a_own = sum_terms([a_sums[0]] + got)
    mine, to_before, to_after = spread(me, a_own, m_own, att_rows, mlp_rows, scale)
    grad_params = close(mine, shifted(to_after, 1), shifted(to_before, -1), att_rows)
    return output, grad_input, grad_params


def solution(mesh):
    return jax.shard_map(
        local,
        mesh=mesh,
        in_specs=(
            P(AXES, None),
            P(AXES, None),
            P(AXES),
            P(AXES),
            P(AXES),
            P(AXES, None),
        ),
        out_specs=(P(AXES, None), P(AXES, None), P(AXES, None)),
        check_vma=False,
    )
```

time: 567 us -> 372 us (0.66)
  blocking collectives: 91.7 us -> 0 us
  waiting for transfers between devices: 134 us -> 91.3 us
  local copies, waits for them, and re-layouts: 49 us -> 23.2 us
  Pallas kernels: 199 us -> 178 us
  other arithmetic: 36.1 us -> 15.9 us
  starting transfers between devices: 45.9 us -> 55.6 us
    psum x2 -> x0, blocking collectives: 91.7 us -> none  [the longest x1 49 us: local(): small_sums = lax.psum(small_grads, AXES)]
    ppermute x36 -> x40, waiting for transfers between devices: 128 us -> 83.4 us  [exchange(): return lax.ppermute(values, AXES, [(d, d ^ bit) for d in range(BLOCKS)])]
    slice x13 -> x8, local copies, waits for them, and re-layouts: 18.2 us -> 1.08 us  [the longest x1 0.97 us: local(): a, b = along_z(att_own[0], att_own[1], got)]
    another operation x16 -> x9, other arithmetic: 18.7 us -> 3.46 us  [the longest x2 2.69 us: local(): m_sums = jnp.stack([m, n], axis=1)]
    pallas_call x4, Pallas kernels: 44.5 us -> 33.8 us  [the longest x1 27.2 us: qkv_back(): pl.pallas_call(qkv_back_kernel, out_shape=(shape((rows, width), F32), hal...]
    ppermute x36 -> x40, starting transfers between devices: 30.9 us -> 40.7 us  [exchange(): return lax.ppermute(values, AXES, [(d, d ^ bit) for d in range(BLOCKS)])]
    another operation x4 -> x0, local copies, waits for them, and re-layouts: 7.06 us -> none  [widen(): return jnp.stack([values, exchange(values, bit)], axis=axis)]
    unnamed x72 -> x82, local copies, waits for them, and re-layouts: 18.8 us -> 18.1 us
  transfers between devices with their start and end apart: 40 -> 44, of which waited for: 19 -> 23; matrix products, arithmetic and copies ran while one was open for 8% -> 2% of each run, Pallas kernels for 13% -> 30%
where the time goes in v2:
time: 372 us; the launch traced here: 366 us
  Pallas kernels  178 us (48%)
  waiting for transfers between devices  91.3 us (25%)
  starting transfers between devices  55.6 us (15%)
  local copies, waits for them, and re-layouts  23.2 us (6%)
  other arithmetic  15.9 us (4%)
    ppermute x40, waiting for transfers between devices, exchange(): return lax.ppermute(values, AXES, [(d, d ^ bit) for d in range(BLOCKS)])  83.4 us
    pallas_call x1, Pallas kernels, feed_forward(): pl.pallas_call(mlp_kernel, out_shape=(shape((rows, width), BF16), shape((...  63 us
    ppermute x40, starting transfers between devices, exchange(): return lax.ppermute(values, AXES, [(d, d ^ bit) for d in range(BLOCKS)])  40.7 us
    pallas_call x1, Pallas kernels, attend_back(): pl.pallas_call(attend_back_kernel, out_shape=shape((rows, triple), BF16),...  34.8 us
    pallas_call x1, Pallas kernels, qkv_back(): pl.pallas_call(qkv_back_kernel, out_shape=(shape((rows, width), F32), hal...  27.2 us
    unnamed x82, local copies, waits for them, and re-layouts  18.1 us
    pallas_call x1, Pallas kernels, attend(): pl.pallas_call(attend_kernel, out_shape=(shape((rows, width), BF16), shap...  17.6 us
    ppermute x4, starting transfers between devices, shifted(): return lax.ppermute(values, AXES, pairs)  15 us
  transfers between devices with their start and end apart: 44, of which 23 were waited for; matrix products, arithmetic and copies ran while one was open for 2% of the time, Pallas kernels for 30%

profile of v2, /device:TPU:2, one launch (start us, length us, event | category | flops | bytes accessed | tf_op | source)
XLA Modules:
  0.0 366.0 jit_solution(14479513321223118310)
XLA Ops:
  1.4 3.4 collective-permute-start
  6.3 5.7 %collective-permute-start.1 = (f32[72,128]{1,0:T(8,128)S(1)}, f32[72,128]{1,0:T(8,128)S(1)}, u32[]{:S(2)}, u32[]{:S(2)}) collective-permute-start(f32[72,128]{1,0:T(8,128)S(1)} %pad_maximum_fusion.11), channel_id=1, source_target_pairs={{1,0},{2,1},{3,2},{4,3},{5,4},{6,5},{7,6},{8,7},{9,8},{10,9},{11,1... | collective-permute-start | bytes 110600 | tf_op jit(solution)/shard_map/ppermute | solution.py:1030
  12.1 1.6 collective-permute-done.1.heads
  14.3 2.1 pack.1
  16.4 2.1 collective-permute-start.4
  18.5 2.3 collective-permute-start.2
  21.8 3.6 collective-permute-done.4
  25.4 6.0 %collective-permute-done.3 = bf16[2,19,16,128]{3,2,1,0:T(8,128)(2,1)S(1)} collective-permute-done((bf16[2,19,16,128]{3,2,1,0:T(8,128)(2,1)}, bf16[2,19,16,128]{3,2,1,0:T(8,128)(2,1)S(1)}, u32[]{:S(2)}, u32[]{:S(2)}) %collective-permute-start.3) | collective-permute-done | bytes 155680 | tf_op jit(solution)/shard_map/ppermute | solution.py:1025
  32.2 2.4 collective-permute-start.6
  34.6 2.4 collective-permute-start.8
  37.0 2.5 collective-permute-done.5
  39.6 1.7 collective-permute-done.6
  41.3 5.1 %collective-permute-done.8 = bf16[2,36,16,128]{3,2,1,0:T(8,128)(2,1)S(1)} collective-permute-done((bf16[2,36,16,128]{3,2,1,0:T(8,128)(2,1)S(1)}, bf16[2,36,16,128]{3,2,1,0:T(8,128)(2,1)S(1)}, u32[]{:S(2)}, u32[]{:S(2)}) %collective-permute-start.8) | collective-permute-done | bytes 294944 | tf_op jit(solution)/shard_map/ppermute | solution.py:1025
  46.4 4.2 %collective-permute-done.7 = bf16[2,36,16,128]{3,2,1,0:T(8,128)(2,1)S(1)} collective-permute-done((bf16[2,36,16,128]{3,2,1,0:T(8,128)(2,1)S(1)}, bf16[2,36,16,128]{3,2,1,0:T(8,128)(2,1)S(1)}, u32[]{:S(2)}, u32[]{:S(2)}) %collective-permute-start.7) | collective-permute-done | bytes 294944 | tf_op jit(solution)/shard_map/ppermute | solution.py:1025
  52.2 13.9 %collective-permute-done.13 = bf16[2,36,16,128]{3,2,1,0:T(8,128)(2,1)S(1)} collective-permute-done((bf16[2,36,16,128]{3,2,1,0:T(8,128)(2,1)S(1)}, bf16[2,36,16,128]{3,2,1,0:T(8,128)(2,1)S(1)}, u32[]{:S(2)}, u32[]{:S(2)}) %collective-permute-start.13) | collective-permute-done | bytes 294944 | tf_op jit(solution)/shard_map/ppermute | solution.py:1025
  66.4 1.3 collective-permute-done.9.refs_1_
  68.5 1.5 collective-permute-done.14.refs_3_
  71.4 1.7 collective-permute-start.17
  73.0 12.8 %qkv_forward.1 = (bf16[1024,768]{1,0:T(8,128)(2,1)S(1)}, bf16[1024,2304]{1,0:T(8,128)(2,1)S(1)}, f32[88,128]{1,0:T(8,128)S(1)}) custom-call(s32[1]{0:T(128)} %bitcast.me_ref, bf16[1024,768]{1,0:T(8,128)(2,1)S(1)} %copy-done.11, bf16[8,19,16,128]{3,2,1,0:T(8,128)(2,1)S(1)} %pad_maximum_fusion.4.refs_0_, ...), custom_call_target="tpu_custom_call" | custom-call | flops 3623878656 | bytes 9437184 | tf_op jit(solution)/shard_map/qkv_forward/pallas_call | solution.py:425
  85.9 2.2 copy-done.20
  88.1 1.3 pad_maximum_fusion.2.refs_0_
  89.4 1.2 pad_maximum_fusion.3.refs_4_
  91.2 1.6 collective-permute-start.19
  96.3 2.3 copy-done.21
  98.7 17.6 %attend_forward.1 = (bf16[1024,768]{1,0:T(8,128)(2,1)S(1)}, f32[48,2,256]{2,1,0:T(2,128)S(1)}) custom-call(s32[2,8]{1,0:T(2,128)S(1)} %pad_add_fusion.windows, bf16[1024,2304]{1,0:T(8,128)(2,1)S(1)} %copy-done.21, s32[1024,1]{1,0:T(8,128)S(1)} %copy-done.13, s32[8,128]{1,0:T(8,128)S(1)} %bitcast.45), custom_call_target="tpu_custom_call" | custom-call | flops 1610612736 | bytes 6291456 | tf_op jit(solution)/shard_map/attend_forward/pallas_call | solution.py:516
  116.4 7.8 %project_and_norm.1 = (f32[1024,768]{1,0:T(8,128)S(1)}, f32[1024,768]{1,0:T(8,128)}, bf16[1024,768]{1,0:T(8,128)(2,1)S(1)}) custom-call(s32[1]{0:T(128)} %bitcast.me_ref, bf16[1024,768]{1,0:T(8,128)(2,1)S(1)} %copy-done.12, bf16[1024,768]{1,0:T(8,128)(2,1)S(1)} %get-tuple-element.135.mixed, f32[88,128]{1,0:T(8,128)S(1)} %get-tuple-element.136.small, ...), custom_call_target="tpu_custom_call" | custom-call | flops 1207959552 | bytes 11010048 | tf_op jit(solution)/shard_map/project_and_norm/pallas_call | solution.py:567
  124.2 1.7 copy-done.17
  125.8 1.2 copy-done.18
  127.9 2.6 collective-permute-done.22.refs_3_
  130.5 1.7 collective-permute-done.23.refs_7_
  133.2 63.0 %feed_forward.1 = (bf16[1024,768]{1,0:T(8,128)(2,1)}, f32[1024,768]{1,0:T(8,128)}, f32[48,128]{1,0:T(8,128)}, bf16[16,36,16,128]{3,2,1,0:T(8,128)(2,1)}, bf16[16...) custom-call(s32[1]{0:T(128)} %bitcast.me_ref, ...), custom_call_target="tpu_custom_call" | custom-call | flops 28991029248 | bytes 41943040 | tf_op jit(solution)/shard_map/feed_forward/pallas_call | solution.py:748
  196.1 1.1 collective-permute-start.24
  197.3 1.9 copy-done
  199.2 1.1 copy-done.5
  200.3 1.1 copy-done.9
  201.4 8.0 %project_backward.1 = (bf16[1024,768]{1,0:T(8,128)(2,1)S(1)}, f32[12,128]{1,0:T(8,128)S(1)}, bf16[8,2,18,16,128]{4,3,2,1,0:T(8,128)(2,1)S(1)}) custom-call(s32[1]{0:T(128)} %bitcast.me_ref, f32[1024,768]{1,0:T(8,128)S(1)} %copy-done, f32[1024,768]{1,0:T(8,128)} %get-tuple-element.152.branch, bf16[1024,768]{1,0:T(8,128)(2,1)S(1)} %get-tuple-element.135.mixed, ...), custom_call_target="tpu_custom_call" | custom-call | flops 2415919104 | bytes 11010048 | tf_op jit(solution)/shard_map/project_backward/pallas_call | solution.py:817
  209.5 1.4 add_convert_fusion.1
  212.8 1.3 add_convert_fusion
  214.2 2.1 collective-permute-start.27
  216.3 34.8 %attend_backward.1.dqkv = bf16[1024,2304]{1,0:T(8,128)(2,1)} custom-call(s32[2,8]{1,0:T(2,128)S(1)} %pad_add_fusion.windows, bf16[1024,2304]{1,0:T(8,128)(2,1)} %copy-done.20, bf16[1024,768]{1,0:T(8,128)(2,1)S(1)} %get-tuple-element.160.da, f32[48,2,256]{2,1,0:T(2,128)S(1)} %get-tuple-element.161.stats, s32[1024,1]{1,0:T(8,128)S(1)} %copy-done.14, ...), custom_call_target="tpu_custom_call" | custom-call | flops 4831838208 | bytes 11010048 | tf_op jit(solution)/shard_map/attend_backward/pallas_call | solution.py:903
  251.2 2.3 add_convert_fusion.5
  253.5 2.2 add_convert_fusion.4
  255.7 3.2 collective-permute-start.29
  258.9 27.2 %qkv_backward.1 = (f32[1024,768]{1,0:T(8,128)}, bf16[16,19,16,128]{3,2,1,0:T(8,128)(2,1)}, bf16[16,19,16,128]{3,2,1,0:T(8,128)(2,1)}, bf16[16,19,16,128]{3,2,1,0:T(8,128)(2,1)}, bf16[16,19,16,128]{3,2,1,0:T(8,128)(2,1)}) custom-call(s32[1]{0:T(128)} %bitcast.me_ref, bf16[1024,768]{1,0:T(8,128)(2,1)} %tokens.4, bf16[1024,768]{1,0:T(8,128)(2,1)} %copy-done.22, ...), custom_call_target="tpu_custom_call" | custom-call | flops 7247757312 | bytes 23592960 | tf_op jit(solution)/shard_map/qkv_backward/pallas_call | solution.py:1003
  286.2 1.4 add_bitcast_fusion
  287.5 1.3 add_bitcast_fusion.1
  291.2 1.9 collective-permute-done.30
  293.3 1.6 collective-permute-done.31
  295.1 4.9 %collective-permute-done.32 = bf16[2,36,16,128]{3,2,1,0:T(8,128)(2,1)S(1)} collective-permute-done((bf16[2,36,16,128]{3,2,1,0:T(8,128)(2,1)S(1)}, bf16[2,36,16,128]{3,2,1,0:T(8,128)(2,1)S(1)}, u32[]{:S(2)}, u32[]{:S(2)}) %collective-permute-start.32) | collective-permute-done | bytes 294944 | tf_op jit(solution)/shard_map/ppermute | solution.py:1025
  300.8 6.1 %collective-permute-start.35 = (bf16[2,36,16,128]{3,2,1,0:T(8,128)(2,1)S(1)}, bf16[2,36,16,128]{3,2,1,0:T(8,128)(2,1)S(1)}, u32[]{:S(2)}, u32[]{:S(2)}) collective-permute-start(bf16[2,36,16,128]{3,2,1,0:T(8,128)(2,1)S(1)} %get-tuple-element.191), channel_id=1, source_target_pairs={{0,4},{1,5},{2,6},{3,7},{4,0},{5,1},{6,2},{7,3},{8,12},{9,13},{10,... | collective-permute-start | bytes 884744 | tf_op jit(solution)/shard_map/ppermute | solution.py:1025
  306.9 8.5 %collective-permute-done.33 = bf16[8,19,16,128]{3,2,1,0:T(8,128)(2,1)S(1)} collective-permute-done((bf16[8,19,16,128]{3,2,1,0:T(8,128)(2,1)S(1)}, bf16[8,19,16,128]{3,2,1,0:T(8,128)(2,1)S(1)}, u32[]{:S(2)}, u32[]{:S(2)}) %collective-permute-start.33) | collective-permute-done | bytes 622624 | tf_op jit(solution)/shard_map/ppermute | solution.py:1025
  315.7 3.7 collective-permute-done.35
  319.4 2.6 collective-permute-start.38
  323.0 7.2 %collective-permute-done.38 = bf16[2,36,16,128]{3,2,1,0:T(8,128)(2,1)S(1)} collective-permute-done((bf16[2,36,16,128]{3,2,1,0:T(8,128)(2,1)S(1)}, bf16[2,36,16,128]{3,2,1,0:T(8,128)(2,1)S(1)}, u32[]{:S(2)}, u32[]{:S(2)}) %collective-permute-start.38) | collective-permute-done | bytes 294944 | tf_op jit(solution)/shard_map/ppermute | solution.py:1025
  331.6 3.3 collective-permute-start.39
  334.9 1.1 collective-permute-start.40
  336.0 1.4 collective-permute-start.41
  337.4 2.0 collective-permute-done.39
  339.4 8.3 %collective-permute-done.40 = bf16[2,19,16,128]{3,2,1,0:T(8,128)(2,1)S(1)} collective-permute-done((bf16[2,19,16,128]{3,2,1,0:T(8,128)(2,1)S(1)}, bf16[2,19,16,128]{3,2,1,0:T(8,128)(2,1)S(1)}, u32[]{:S(2)}, u32[]{:S(2)}) %collective-permute-start.40) | collective-permute-done | bytes 155680 | tf_op jit(solution)/shard_map/ppermute | solution.py:1025
  348.5 2.3 spread.1
  350.8 3.1 collective-permute-start.43
  353.9 2.8 collective-permute-start.42
  356.7 6.3 %collective-permute-done.42.below = f32[72,128]{1,0:T(8,128)S(1)} collective-permute-done((f32[72,128]{1,0:T(8,128)}, f32[72,128]{1,0:T(8,128)S(1)}, u32[]{:S(2)}, u32[]{:S(2)}) %collective-permute-start.42) | collective-permute-done | bytes 36896 | tf_op jit(solution)/shard_map/ppermute | solution.py:1030
  363.6 2.2 close.1
  (167 shorter events, 23.9 us)
Async XLA Ops:
  1.4 12.3 %collective-permute-start = (f32[128,128]{1,0:T(8,128)S(1)}, f32[128,128]{1,0:T(8,128)S(1)}, u32[]{:S(2)}, u32[]{:S(2)}) collective-permute-start(f32[128,128]{1,0:T(8,128)S(1)} %pad_maximum_fusion.10), channel_id=1, source_target_pairs={{0,1},{1,2},{2,3},{3,4},{4,5},{5,6},{6,7},{7,8},{8,9},{9,10},{10,1... | collective-permute-start | bytes 196616 | tf_op jit(solution)/shard_map/ppermute | solution.py:1030
  6.3 7.3 %collective-permute-start.1 = (f32[72,128]{1,0:T(8,128)S(1)}, f32[72,128]{1,0:T(8,128)S(1)}, u32[]{:S(2)}, u32[]{:S(2)}) collective-permute-start(f32[72,128]{1,0:T(8,128)S(1)} %pad_maximum_fusion.11), channel_id=1, source_target_pairs={{1,0},{2,1},{3,2},{4,3},{5,4},{6,5},{7,6},{8,7},{9,8},{10,9},{11,1... | collective-permute-start | bytes 110600 | tf_op jit(solution)/shard_map/ppermute | solution.py:1030
  16.4 18.2 %copy-start.30 = (bf16[2,36,16,128]{3,2,1,0:T(8,128)(2,1)S(1)}, bf16[2,36,16,128]{3,2,1,0:T(8,128)(2,1)}, u32[]{:S(2)}) copy-start(bf16[2,36,16,128]{3,2,1,0:T(8,128)(2,1)} %get-tuple-element.111) | copy-start | bytes 884740
  16.4 9.0 %collective-permute-start.4 = (bf16[2,19,16,128]{3,2,1,0:T(8,128)(2,1)}, bf16[2,19,16,128]{3,2,1,0:T(8,128)(2,1)S(1)}, u32[]{:S(2)}, u32[]{:S(2)}) collective-permute-start(bf16[2,19,16,128]{3,2,1,0:T(8,128)(2,1)} %get-tuple-element.104), channel_id=1, source_target_pairs={{0,6},{1,7},{2,4},{3,5},{4,2},{5,3},{6,0},{7,1},{8,14},{9,15},{10,... | collective-permute-start | bytes 466952 | tf_op jit(solution)/shard_map/ppermute | solution.py:1025
  18.5 12.9 %collective-permute-start.3 = (bf16[2,19,16,128]{3,2,1,0:T(8,128)(2,1)}, bf16[2,19,16,128]{3,2,1,0:T(8,128)(2,1)S(1)}, u32[]{:S(2)}, u32[]{:S(2)}) collective-permute-start(bf16[2,19,16,128]{3,2,1,0:T(8,128)(2,1)} %get-tuple-element.104), channel_id=1, source_target_pairs={{0,4},{1,5},{2,6},{3,7},{4,0},{5,1},{6,2},{7,3},{8,12},{9,13},{10,... | collective-permute-start | bytes 466952 | tf_op jit(solution)/shard_map/ppermute | solution.py:1025
  18.5 12.9 %collective-permute-start.2 = (bf16[2,19,16,128]{3,2,1,0:T(8,128)(2,1)}, bf16[2,19,16,128]{3,2,1,0:T(8,128)(2,1)S(1)}, u32[]{:S(2)}, u32[]{:S(2)}) collective-permute-start(bf16[2,19,16,128]{3,2,1,0:T(8,128)(2,1)} %get-tuple-element.104), channel_id=1, source_target_pairs={{0,2},{1,3},{2,0},{3,1},{4,6},{5,7},{6,4},{7,5},{8,10},{9,11},{10,... | collective-permute-start | bytes 466952 | tf_op jit(solution)/shard_map/ppermute | solution.py:1025
  31.5 8.0 %collective-permute-start.5 = (bf16[4,19,16,128]{3,2,1,0:T(8,128)(2,1)S(1)}, bf16[4,19,16,128]{3,2,1,0:T(8,128)(2,1)S(1)}, u32[]{:S(2)}, u32[]{:S(2)}) collective-permute-start(bf16[4,19,16,128]{3,2,1,0:T(8,128)(2,1)S(1)} %get-tuple-element.106), channel_id=1, source_target_pairs={{0,16},{1,17},{2,18},{3,19},{4,20},{5,21},{6,22},{7,23},{8,24},{9,... | collective-permute-start | bytes 933896 | tf_op jit(solution)/shard_map/ppermute | solution.py:1025
  32.2 9.0 %collective-permute-start.6 = (bf16[4,19,16,128]{3,2,1,0:T(8,128)(2,1)S(1)}, bf16[4,19,16,128]{3,2,1,0:T(8,128)(2,1)S(1)}, u32[]{:S(2)}, u32[]{:S(2)}) collective-permute-start(bf16[4,19,16,128]{3,2,1,0:T(8,128)(2,1)S(1)} %get-tuple-element.107), channel_id=1, source_target_pairs={{0,1},{1,0},{2,3},{3,2},{4,5},{5,4},{6,7},{7,6},{8,9},{9,8},{10,11... | collective-permute-start | bytes 933896 | tf_op jit(solution)/shard_map/ppermute | solution.py:1025
  34.6 11.8 %collective-permute-start.8 = (bf16[2,36,16,128]{3,2,1,0:T(8,128)(2,1)S(1)}, bf16[2,36,16,128]{3,2,1,0:T(8,128)(2,1)S(1)}, u32[]{:S(2)}, u32[]{:S(2)}) collective-permute-start(bf16[2,36,16,128]{3,2,1,0:T(8,128)(2,1)S(1)} %copy-done.30), channel_id=1, source_target_pairs={{0,6},{1,7},{2,4},{3,5},{4,2},{5,3},{6,0},{7,1},{8,14},{9,15},{10,... | collective-permute-start | bytes 884744 | tf_op jit(solution)/shard_map/ppermute | solution.py:1025
  37.0 13.6 %collective-permute-start.7 = (bf16[2,36,16,128]{3,2,1,0:T(8,128)(2,1)S(1)}, bf16[2,36,16,128]{3,2,1,0:T(8,128)(2,1)S(1)}, u32[]{:S(2)}, u32[]{:S(2)}) collective-permute-start(bf16[2,36,16,128]{3,2,1,0:T(8,128)(2,1)S(1)} %copy-done.30), channel_id=1, source_target_pairs={{0,2},{1,3},{2,0},{3,1},{4,6},{5,7},{6,4},{7,5},{8,10},{9,11},{10,... | collective-permute-start | bytes 884744 | tf_op jit(solution)/shard_map/ppermute | solution.py:1025
  50.6 15.6 %collective-permute-start.13 = (bf16[2,36,16,128]{3,2,1,0:T(8,128)(2,1)S(1)}, bf16[2,36,16,128]{3,2,1,0:T(8,128)(2,1)S(1)}, u32[]{:S(2)}, u32[]{:S(2)}) collective-permute-start(bf16[2,36,16,128]{3,2,1,0:T(8,128)(2,1)S(1)} %copy-done.30), channel_id=1, source_target_pairs={{0,4},{1,5},{2,6},{3,7},{4,0},{5,1},{6,2},{7,3},{8,12},{9,13},{10,... | collective-permute-start | bytes 884744 | tf_op jit(solution)/shard_map/ppermute | solution.py:1025
  51.2 15.2 %collective-permute-start.11 = (bf16[8,19,16,128]{3,2,1,0:T(8,128)(2,1)S(1)}, bf16[8,19,16,128]{3,2,1,0:T(8,128)(2,1)S(1)}, u32[]{:S(2)}, u32[]{:S(2)}) collective-permute-start(bf16[8,19,16,128]{3,2,1,0:T(8,128)(2,1)S(1)} %pad_maximum_fusion.4.refs_0_), channel_id=1, source_target_pairs={{0,8},{1,9},{2,10},{3,11},{4,12},{5,13},{6,14},{7,15},{8,0},{9,1},... | collective-permute-start | bytes 1867784 | tf_op jit(solution)/shard_map/ppermute | solution.py:1025
  51.2 16.4 %collective-permute-start.9 = (bf16[8,19,16,128]{3,2,1,0:T(8,128)(2,1)S(1)}, bf16[8,19,16,128]{3,2,1,0:T(8,128)(2,1)S(1)}, u32[]{:S(2)}, u32[]{:S(2)}) collective-permute-start(bf16[8,19,16,128]{3,2,1,0:T(8,128)(2,1)S(1)} %pad_maximum_fusion.4.refs_0_), channel_id=1, source_target_pairs={{0,1},{1,0},{2,3},{3,2},{4,5},{5,4},{6,7},{7,6},{8,9},{9,8},{10,11... | collective-permute-start | bytes 1867784 | tf_op jit(solution)/shard_map/ppermute | solution.py:1025
  51.5 16.2 %collective-permute-start.12 = (bf16[8,19,16,128]{3,2,1,0:T(8,128)(2,1)S(1)}, bf16[8,19,16,128]{3,2,1,0:T(8,128)(2,1)S(1)}, u32[]{:S(2)}, u32[]{:S(2)}) collective-permute-start(bf16[8,19,16,128]{3,2,1,0:T(8,128)(2,1)S(1)} %pad_maximum_fusion.5.refs_4_), channel_id=1, source_target_pairs={{0,8},{1,9},{2,10},{3,11},{4,12},{5,13},{6,14},{7,15},{8,0},{9,1},... | collective-permute-start | bytes 1867784 | tf_op jit(solution)/shard_map/ppermute | solution.py:1025
  51.7 16.2 %collective-permute-start.10 = (bf16[8,19,16,128]{3,2,1,0:T(8,128)(2,1)S(1)}, bf16[8,19,16,128]{3,2,1,0:T(8,128)(2,1)S(1)}, u32[]{:S(2)}, u32[]{:S(2)}) collective-permute-start(bf16[8,19,16,128]{3,2,1,0:T(8,128)(2,1)S(1)} %pad_maximum_fusion.5.refs_4_), channel_id=1, source_target_pairs={{0,16},{1,17},{2,18},{3,19},{4,20},{5,21},{6,22},{7,23},{8,24},{9,... | collective-permute-start | bytes 1867784 | tf_op jit(solution)/shard_map/ppermute | solution.py:1025
  66.2 6.8 %copy-start.11 = (bf16[1024,768]{1,0:T(8,128)(2,1)S(1)}, bf16[1024,768]{1,0:T(8,128)(2,1)}, u32[]{:S(2)}) copy-start(bf16[1024,768]{1,0:T(8,128)(2,1)} %tokens.4) | copy-start | bytes 4718596
  68.0 17.9 %copy-start.1 = (bf16[8,19,16,128]{3,2,1,0:T(8,128)(2,1)}, bf16[8,19,16,128]{3,2,1,0:T(8,128)(2,1)S(1)}, u32[]{:S(2)}) copy-start(bf16[8,19,16,128]{3,2,1,0:T(8,128)(2,1)S(1)} %collective-permute-done.10.refs_5_) | copy-start | bytes 1867780
  68.0 2.1 collective-permute-start.14
  68.0 2.9 collective-permute-start.15
  70.0 15.8 %copy-start.3 = (bf16[8,19,16,128]{3,2,1,0:T(8,128)(2,1)}, bf16[8,19,16,128]{3,2,1,0:T(8,128)(2,1)S(1)}, u32[]{:S(2)}) copy-start(bf16[8,19,16,128]{3,2,1,0:T(8,128)(2,1)S(1)} %collective-permute-done.14.refs_3_) | copy-start | bytes 1867780
  70.9 15.0 %copy-start.7 = (bf16[8,19,16,128]{3,2,1,0:T(8,128)(2,1)}, bf16[8,19,16,128]{3,2,1,0:T(8,128)(2,1)S(1)}, u32[]{:S(2)}) copy-start(bf16[8,19,16,128]{3,2,1,0:T(8,128)(2,1)S(1)} %collective-permute-done.15.refs_7_) | copy-start | bytes 1867780
  70.9 17.2 %collective-permute-start.16 = (bf16[4,36,16,128]{3,2,1,0:T(8,128)(2,1)S(1)}, bf16[4,36,16,128]{3,2,1,0:T(8,128)(2,1)S(1)}, u32[]{:S(2)}, u32[]{:S(2)}) collective-permute-start(bf16[4,36,16,128]{3,2,1,0:T(8,128)(2,1)S(1)} %pad_maximum_fusion.6), channel_id=1, source_target_pairs={{0,16},{1,17},{2,18},{3,19},{4,20},{5,21},{6,22},{7,23},{8,24},{9,... | collective-permute-start | bytes 1769480 | tf_op jit(solution)/shard_map/ppermute | solution.py:1025
  71.4 18.0 %collective-permute-start.17 = (bf16[4,36,16,128]{3,2,1,0:T(8,128)(2,1)S(1)}, bf16[4,36,16,128]{3,2,1,0:T(8,128)(2,1)S(1)}, u32[]{:S(2)}, u32[]{:S(2)}) collective-permute-start(bf16[4,36,16,128]{3,2,1,0:T(8,128)(2,1)S(1)} %pad_maximum_fusion.7), channel_id=1, source_target_pairs={{0,1},{1,0},{2,3},{3,2},{4,5},{5,4},{6,7},{7,6},{8,9},{9,8},{10,11... | collective-permute-start | bytes 1769480 | tf_op jit(solution)/shard_map/ppermute | solution.py:1025
  88.1 28.2 %copy-start.15 = (f32[88,128]{1,0:T(8,128)}, f32[88,128]{1,0:T(8,128)S(1)}, u32[]{:S(2)}) copy-start(f32[88,128]{1,0:T(8,128)S(1)} %get-tuple-element.136.small) | copy-start | bytes 135172
  89.4 3.4 copy-start.35
  89.4 4.2 %copy-start.36 = (s32[1024]{0:T(1024)S(1)}, s32[1024]{0:T(1024)}, u32[]{:S(2)}) copy-start(s32[1024]{0:T(1024)} %param.9) | copy-start | bytes 12292
  90.6 36.5 %collective-permute-start.20 = (bf16[8,36,16,128]{3,2,1,0:T(8,128)(2,1)}, bf16[8,36,16,128]{3,2,1,0:T(8,128)(2,1)}, u32[]{:S(2)}, u32[]{:S(2)}) collective-permute-start(bf16[8,36,16,128]{3,2,1,0:T(8,128)(2,1)} %pad_maximum_fusion.2.refs_0_), channel_id=1, source_target_pairs={{0,8},{1,9},{2,10},{3,11},{4,12},{5,13},{6,14},{7,15},{8,0},{9,1},... | collective-permute-start | bytes 3538952 | tf_op jit(solution)/shard_map/ppermute | solution.py:1025
  90.6 36.5 %collective-permute-start.18 = (bf16[8,36,16,128]{3,2,1,0:T(8,128)(2,1)}, bf16[8,36,16,128]{3,2,1,0:T(8,128)(2,1)}, u32[]{:S(2)}, u32[]{:S(2)}) collective-permute-start(bf16[8,36,16,128]{3,2,1,0:T(8,128)(2,1)} %pad_maximum_fusion.2.refs_0_), channel_id=1, source_target_pairs={{0,1},{1,0},{2,3},{3,2},{4,5},{5,4},{6,7},{7,6},{8,9},{9,8},{10,11... | collective-permute-start | bytes 3538952 | tf_op jit(solution)/shard_map/ppermute | solution.py:1025
  90.9 36.1 %collective-permute-start.21 = (bf16[8,36,16,128]{3,2,1,0:T(8,128)(2,1)}, bf16[8,36,16,128]{3,2,1,0:T(8,128)(2,1)}, u32[]{:S(2)}, u32[]{:S(2)}) collective-permute-start(bf16[8,36,16,128]{3,2,1,0:T(8,128)(2,1)} %pad_maximum_fusion.3.refs_4_), channel_id=1, source_target_pairs={{0,8},{1,9},{2,10},{3,11},{4,12},{5,13},{6,14},{7,15},{8,0},{9,1},... | collective-permute-start | bytes 3538952 | tf_op jit(solution)/shard_map/ppermute | solution.py:1025
  91.2 35.9 %collective-permute-start.19 = (bf16[8,36,16,128]{3,2,1,0:T(8,128)(2,1)}, bf16[8,36,16,128]{3,2,1,0:T(8,128)(2,1)}, u32[]{:S(2)}, u32[]{:S(2)}) collective-permute-start(bf16[8,36,16,128]{3,2,1,0:T(8,128)(2,1)} %pad_maximum_fusion.3.refs_4_), channel_id=1, source_target_pairs={{0,16},{1,17},{2,18},{3,19},{4,20},{5,21},{6,22},{7,23},{8,24},{9,... | collective-permute-start | bytes 3538952 | tf_op jit(solution)/shard_map/ppermute | solution.py:1025
  98.7 17.6 %copy-start.2 = (bf16[8,19,16,128]{3,2,1,0:T(8,128)(2,1)S(1)}, bf16[8,19,16,128]{3,2,1,0:T(8,128)(2,1)}, u32[]{:S(2)}) copy-start(bf16[8,19,16,128]{3,2,1,0:T(8,128)(2,1)} %copy-done.1) | copy-start | bytes 1867780
  98.7 17.6 %copy-start.4 = (bf16[8,19,16,128]{3,2,1,0:T(8,128)(2,1)S(1)}, bf16[8,19,16,128]{3,2,1,0:T(8,128)(2,1)}, u32[]{:S(2)}) copy-start(bf16[8,19,16,128]{3,2,1,0:T(8,128)(2,1)} %copy-done.3) | copy-start | bytes 1867780
  98.7 17.7 %copy-start.8 = (bf16[8,19,16,128]{3,2,1,0:T(8,128)(2,1)S(1)}, bf16[8,19,16,128]{3,2,1,0:T(8,128)(2,1)}, u32[]{:S(2)}) copy-start(bf16[8,19,16,128]{3,2,1,0:T(8,128)(2,1)} %copy-done.7) | copy-start | bytes 1867780
  98.7 17.7 %copy-start.12 = (bf16[1024,768]{1,0:T(8,128)(2,1)S(1)}, bf16[1024,768]{1,0:T(8,128)(2,1)}, u32[]{:S(2)}) copy-start(bf16[1024,768]{1,0:T(8,128)(2,1)} %tokens.4) | copy-start | bytes 4718596
  127.0 3.4 collective-permute-start.22
  127.8 4.4 %collective-permute-start.23 = (bf16[8,36,16,128]{3,2,1,0:T(8,128)(2,1)}, bf16[8,36,16,128]{3,2,1,0:T(8,128)(2,1)S(1)}, u32[]{:S(2)}, u32[]{:S(2)}) collective-permute-start(bf16[8,36,16,128]{3,2,1,0:T(8,128)(2,1)} %collective-permute-done.19.refs_5_), channel_id=1, source_target_pairs={{0,8},{1,9},{2,10},{3,11},{4,12},{5,13},{6,14},{7,15},{8,0},{9,1},... | collective-permute-start | bytes 3538952 | tf_op jit(solution)/shard_map/ppermute | solution.py:1025
  133.2 64.2 %copy-start.16 = (f32[88,128]{1,0:T(8,128)S(1)}, f32[88,128]{1,0:T(8,128)}, u32[]{:S(2)}) copy-start(f32[88,128]{1,0:T(8,128)} %copy-done.15) | copy-start | bytes 135172
  196.1 13.3 %collective-permute-start.24 = (bf16[16,36,16,128]{3,2,1,0:T(8,128)(2,1)}, bf16[16,36,16,128]{3,2,1,0:T(8,128)(2,1)S(1)}, u32[]{:S(2)}, u32[]{:S(2)}) collective-permute-start(bf16[16,36,16,128]{3,2,1,0:T(8,128)(2,1)} %get-tuple-element.150), channel_id=1, source_target_pairs={{0,8},{1,9},{2,10},{3,11},{4,12},{5,13},{6,14},{7,15},{8,0},{9,1},... | collective-permute-start | bytes 7077896 | tf_op jit(solution)/shard_map/ppermute | solution.py:1025
  197.3 12.2 %collective-permute-start.25 = (bf16[16,36,16,128]{3,2,1,0:T(8,128)(2,1)}, bf16[16,36,16,128]{3,2,1,0:T(8,128)(2,1)S(1)}, u32[]{:S(2)}, u32[]{:S(2)}) collective-permute-start(bf16[16,36,16,128]{3,2,1,0:T(8,128)(2,1)} %get-tuple-element.151), channel_id=1, source_target_pairs={{0,8},{1,9},{2,10},{3,11},{4,12},{5,13},{6,14},{7,15},{8,0},{9,1},... | collective-permute-start | bytes 7077896 | tf_op jit(solution)/shard_map/ppermute | solution.py:1025
  201.4 8.1 %copy-start.24 = (bf16[16,36,16,128]{3,2,1,0:T(8,128)(2,1)S(1)}, bf16[16,36,16,128]{3,2,1,0:T(8,128)(2,1)}, u32[]{:S(2)}) copy-start(bf16[16,36,16,128]{3,2,1,0:T(8,128)(2,1)} %get-tuple-element.149) | copy-start | bytes 7077892
  212.8 3.5 copy-start.14
  214.1 37.1 %collective-permute-start.26 = (bf16[8,36,16,128]{3,2,1,0:T(8,128)(2,1)}, bf16[8,36,16,128]{3,2,1,0:T(8,128)(2,1)}, u32[]{:S(2)}, u32[]{:S(2)}) collective-permute-start(bf16[8,36,16,128]{3,2,1,0:T(8,128)(2,1)} %add_convert_fusion.1), channel_id=1, source_target_pairs={{0,16},{1,17},{2,18},{3,19},{4,20},{5,21},{6,22},{7,23},{8,24},{9,... | collective-permute-start | bytes 3538952 | tf_op jit(solution)/shard_map/ppermute | solution.py:1025
  214.2 36.9 %collective-permute-start.27 = (bf16[8,36,16,128]{3,2,1,0:T(8,128)(2,1)}, bf16[8,36,16,128]{3,2,1,0:T(8,128)(2,1)}, u32[]{:S(2)}, u32[]{:S(2)}) collective-permute-start(bf16[8,36,16,128]{3,2,1,0:T(8,128)(2,1)} %add_convert_fusion), channel_id=1, source_target_pairs={{0,1},{1,0},{2,3},{3,2},{4,5},{5,4},{6,7},{7,6},{8,9},{9,8},{10,11... | collective-permute-start | bytes 3538952 | tf_op jit(solution)/shard_map/ppermute | solution.py:1025
  253.5 5.5 %copy-start.6 = (bf16[8,19,16,128]{3,2,1,0:T(8,128)(2,1)S(1)}, bf16[8,19,16,128]{3,2,1,0:T(8,128)(2,1)}, u32[]{:S(2)}) copy-start(bf16[8,19,16,128]{3,2,1,0:T(8,128)(2,1)} %copy-done.3) | copy-start | bytes 1867780
  253.5 5.5 %copy-start.10 = (bf16[8,19,16,128]{3,2,1,0:T(8,128)(2,1)S(1)}, bf16[8,19,16,128]{3,2,1,0:T(8,128)(2,1)}, u32[]{:S(2)}) copy-start(bf16[8,19,16,128]{3,2,1,0:T(8,128)(2,1)} %copy-done.7) | copy-start | bytes 1867780
  253.5 5.5 %copy-start.23 = (f32[48,128]{1,0:T(8,128)S(1)}, f32[48,128]{1,0:T(8,128)}, u32[]{:S(2)}) copy-start(f32[48,128]{1,0:T(8,128)} %get-tuple-element.167.mlp) | copy-start | bytes 73732
  255.7 30.4 %collective-permute-start.28 = (bf16[4,36,16,128]{3,2,1,0:T(8,128)(2,1)}, bf16[4,36,16,128]{3,2,1,0:T(8,128)(2,1)S(1)}, u32[]{:S(2)}, u32[]{:S(2)}) collective-permute-start(bf16[4,36,16,128]{3,2,1,0:T(8,128)(2,1)} %add_convert_fusion.5), channel_id=1, source_target_pairs={{0,1},{1,0},{2,3},{3,2},{4,5},{5,4},{6,7},{7,6},{8,9},{9,8},{10,11... | collective-permute-start | bytes 1769480 | tf_op jit(solution)/shard_map/ppermute | solution.py:1025
  255.7 30.4 %collective-permute-start.29 = (bf16[4,36,16,128]{3,2,1,0:T(8,128)(2,1)}, bf16[4,36,16,128]{3,2,1,0:T(8,128)(2,1)S(1)}, u32[]{:S(2)}, u32[]{:S(2)}) collective-permute-start(bf16[4,36,16,128]{3,2,1,0:T(8,128)(2,1)} %add_convert_fusion.4), channel_id=1, source_target_pairs={{0,16},{1,17},{2,18},{3,19},{4,20},{5,21},{6,22},{7,23},{8,24},{9,... | collective-permute-start | bytes 1769480 | tf_op jit(solution)/shard_map/ppermute | solution.py:1025
  289.0 4.1 %copy-start.29 = (bf16[16,19,16,128]{3,2,1,0:T(8,128)(2,1)S(1)}, bf16[16,19,16,128]{3,2,1,0:T(8,128)(2,1)}, u32[]{:S(2)}) copy-start(bf16[16,19,16,128]{3,2,1,0:T(8,128)(2,1)} %get-tuple-element.182) | copy-start | bytes 3735556
  289.2 5.7 %copy-start.28 = (bf16[16,19,16,128]{3,2,1,0:T(8,128)(2,1)S(1)}, bf16[16,19,16,128]{3,2,1,0:T(8,128)(2,1)}, u32[]{:S(2)}) copy-start(bf16[16,19,16,128]{3,2,1,0:T(8,128)(2,1)} %get-tuple-element.184) | copy-start | bytes 3735556
  290.2 2.9 collective-permute-start.30
  290.5 4.3 %collective-permute-start.31 = (bf16[16,19,16,128]{3,2,1,0:T(8,128)(2,1)S(1)}, bf16[16,19,16,128]{3,2,1,0:T(8,128)(2,1)S(1)}, u32[]{:S(2)}, u32[]{:S(2)}) collective-permute-start(bf16[16,19,16,128]{3,2,1,0:T(8,128)(2,1)S(1)} %copy-done.37), channel_id=1, source_target_pairs={{0,8},{1,9},{2,10},{3,11},{4,12},{5,13},{6,14},{7,15},{8,0},{9,1},... | collective-permute-start | bytes 3735560 | tf_op jit(solution)/shard_map/ppermute | solution.py:1025
  290.7 9.3 %collective-permute-start.32 = (bf16[2,36,16,128]{3,2,1,0:T(8,128)(2,1)S(1)}, bf16[2,36,16,128]{3,2,1,0:T(8,128)(2,1)S(1)}, u32[]{:S(2)}, u32[]{:S(2)}) collective-permute-start(bf16[2,36,16,128]{3,2,1,0:T(8,128)(2,1)S(1)} %get-tuple-element.186), channel_id=1, source_target_pairs={{0,2},{1,3},{2,0},{3,1},{4,6},{5,7},{6,4},{7,5},{8,10},{9,11},{10,... | collective-permute-start | bytes 884744 | tf_op jit(solution)/shard_map/ppermute | solution.py:1025
  300.0 15.5 %collective-permute-start.33 = (bf16[8,19,16,128]{3,2,1,0:T(8,128)(2,1)S(1)}, bf16[8,19,16,128]{3,2,1,0:T(8,128)(2,1)S(1)}, u32[]{:S(2)}, u32[]{:S(2)}) collective-permute-start(bf16[8,19,16,128]{3,2,1,0:T(8,128)(2,1)S(1)} %add_convert_fusion.3), channel_id=1, source_target_pairs={{0,16},{1,17},{2,18},{3,19},{4,20},{5,21},{6,22},{7,23},{8,24},{9,... | collective-permute-start | bytes 1867784 | tf_op jit(solution)/shard_map/ppermute | solution.py:1025
  300.0 15.6 %collective-permute-start.34 = (bf16[8,19,16,128]{3,2,1,0:T(8,128)(2,1)S(1)}, bf16[8,19,16,128]{3,2,1,0:T(8,128)(2,1)S(1)}, u32[]{:S(2)}, u32[]{:S(2)}) collective-permute-start(bf16[8,19,16,128]{3,2,1,0:T(8,128)(2,1)S(1)} %add_convert_fusion.2), channel_id=1, source_target_pairs={{0,1},{1,0},{2,3},{3,2},{4,5},{5,4},{6,7},{7,6},{8,9},{9,8},{10,11... | collective-permute-start | bytes 1867784 | tf_op jit(solution)/shard_map/ppermute | solution.py:1025
  300.8 18.6 %collective-permute-start.35 = (bf16[2,36,16,128]{3,2,1,0:T(8,128)(2,1)S(1)}, bf16[2,36,16,128]{3,2,1,0:T(8,128)(2,1)S(1)}, u32[]{:S(2)}, u32[]{:S(2)}) collective-permute-start(bf16[2,36,16,128]{3,2,1,0:T(8,128)(2,1)S(1)} %get-tuple-element.191), channel_id=1, source_target_pairs={{0,4},{1,5},{2,6},{3,7},{4,0},{5,1},{6,2},{7,3},{8,12},{9,13},{10,... | collective-permute-start | bytes 884744 | tf_op jit(solution)/shard_map/ppermute | solution.py:1025
  319.4 10.8 %collective-permute-start.38 = (bf16[2,36,16,128]{3,2,1,0:T(8,128)(2,1)S(1)}, bf16[2,36,16,128]{3,2,1,0:T(8,128)(2,1)S(1)}, u32[]{:S(2)}, u32[]{:S(2)}) collective-permute-start(bf16[2,36,16,128]{3,2,1,0:T(8,128)(2,1)S(1)} %get-tuple-element.197), channel_id=1, source_target_pairs={{0,6},{1,7},{2,4},{3,5},{4,2},{5,3},{6,0},{7,1},{8,14},{9,15},{10,... | collective-permute-start | bytes 884744 | tf_op jit(solution)/shard_map/ppermute | solution.py:1025
  322.0 9.2 %collective-permute-start.36 = (bf16[4,19,16,128]{3,2,1,0:T(8,128)(2,1)S(1)}, bf16[4,19,16,128]{3,2,1,0:T(8,128)(2,1)S(1)}, u32[]{:S(2)}, u32[]{:S(2)}) collective-permute-start(bf16[4,19,16,128]{3,2,1,0:T(8,128)(2,1)S(1)} %add_convert_fusion.7), channel_id=1, source_target_pairs={{0,1},{1,0},{2,3},{3,2},{4,5},{5,4},{6,7},{7,6},{8,9},{9,8},{10,11... | collective-permute-start | bytes 933896 | tf_op jit(solution)/shard_map/ppermute | solution.py:1025
  322.3 9.0 %collective-permute-start.37 = (bf16[4,19,16,128]{3,2,1,0:T(8,128)(2,1)S(1)}, bf16[4,19,16,128]{3,2,1,0:T(8,128)(2,1)S(1)}, u32[]{:S(2)}, u32[]{:S(2)}) collective-permute-start(bf16[4,19,16,128]{3,2,1,0:T(8,128)(2,1)S(1)} %add_convert_fusion.6), channel_id=1, source_target_pairs={{0,16},{1,17},{2,18},{3,19},{4,20},{5,21},{6,22},{7,23},{8,24},{9,... | collective-permute-start | bytes 933896 | tf_op jit(solution)/shard_map/ppermute | solution.py:1025
  331.6 7.8 %collective-permute-start.39 = (bf16[2,19,16,128]{3,2,1,0:T(8,128)(2,1)S(1)}, bf16[2,19,16,128]{3,2,1,0:T(8,128)(2,1)S(1)}, u32[]{:S(2)}, u32[]{:S(2)}) collective-permute-start(bf16[2,19,16,128]{3,2,1,0:T(8,128)(2,1)S(1)} %get-tuple-element.198), channel_id=1, source_target_pairs={{0,2},{1,3},{2,0},{3,1},{4,6},{5,7},{6,4},{7,5},{8,10},{9,11},{10,... | collective-permute-start | bytes 466952 | tf_op jit(solution)/shard_map/ppermute | solution.py:1025
  334.9 12.7 %collective-permute-start.40 = (bf16[2,19,16,128]{3,2,1,0:T(8,128)(2,1)S(1)}, bf16[2,19,16,128]{3,2,1,0:T(8,128)(2,1)S(1)}, u32[]{:S(2)}, u32[]{:S(2)}) collective-permute-start(bf16[2,19,16,128]{3,2,1,0:T(8,128)(2,1)S(1)} %get-tuple-element.199), channel_id=1, source_target_pairs={{0,4},{1,5},{2,6},{3,7},{4,0},{5,1},{6,2},{7,3},{8,12},{9,13},{10,... | collective-permute-start | bytes 466952 | tf_op jit(solution)/shard_map/ppermute | solution.py:1025
  336.0 11.6 %collective-permute-start.41 = (bf16[2,19,16,128]{3,2,1,0:T(8,128)(2,1)S(1)}, bf16[2,19,16,128]{3,2,1,0:T(8,128)(2,1)S(1)}, u32[]{:S(2)}, u32[]{:S(2)}) collective-permute-start(bf16[2,19,16,128]{3,2,1,0:T(8,128)(2,1)S(1)} %get-tuple-element.200), channel_id=1, source_target_pairs={{0,6},{1,7},{2,4},{3,5},{4,2},{5,3},{6,0},{7,1},{8,14},{9,15},{10,... | collective-permute-start | bytes 466952 | tf_op jit(solution)/shard_map/ppermute | solution.py:1025
  350.8 12.2 %collective-permute-start.43 = (f32[128,128]{1,0:T(8,128)}, f32[128,128]{1,0:T(8,128)S(1)}, u32[]{:S(2)}, u32[]{:S(2)}) collective-permute-start(f32[128,128]{1,0:T(8,128)} %get-tuple-element.204), channel_id=1, source_target_pairs={{1,0},{2,1},{3,2},{4,3},{5,4},{6,5},{7,6},{8,7},{9,8},{10,9},{11,1... | collective-permute-start | bytes 196616 | tf_op jit(solution)/shard_map/ppermute | solution.py:1030
  353.9 9.1 %collective-permute-start.42 = (f32[72,128]{1,0:T(8,128)}, f32[72,128]{1,0:T(8,128)S(1)}, u32[]{:S(2)}, u32[]{:S(2)}) collective-permute-start(f32[72,128]{1,0:T(8,128)} %get-tuple-element.203), channel_id=1, source_target_pairs={{0,1},{1,2},{2,3},{3,4},{4,5},{5,6},{6,7},{7,8},{8,9},{9,10},{10,1... | collective-permute-start | bytes 110600 | tf_op jit(solution)/shard_map/ppermute | solution.py:1030
  (21 other events, 32.6 us)
